TPU v7x, 768 devices: a whole 4x8x12 slice. The times are simulated.
768 devices in a mesh: blk: 384 (over z, x, y_hi, core), nrm: 2 (over y_lo).
Axes of the slice: x: 4, y: 8 (y_hi: 4, y_lo: 2; y = y_hi * 2 + y_lo), z: 12, core: 2. Of those that a mesh axis runs over, the one named last changes fastest.
Arguments:
- right_side: float32 [10, 3072, 512], P(None, 'blk', 'nrm'), may hold values from -6 to 6
- mean_flow: float32 [5, 3072, 512], P(None, 'blk', 'nrm'), may hold values from -4 to 4
- jac_basis: float32 [4, 5, 10, 10], replicated, may hold values from -0.23 to 0.23
- pattern: int32 [4, 3072, 512], P(None, 'blk', 'nrm'), may hold values 0 or 1
- shift_diag: float32 [3072, 512], P('blk', 'nrm'), may hold values from 1.2 to 2.4
- dissipation: float32 [3072, 512], P('blk', 'nrm'), may hold values from 0.04 to 0.15
- donors: int32 [384, 2, 512], P('blk', None, 'nrm'), may hold values from 0 to 511, as said below
Outputs:
- solution: float32 [10, 3072, 512], P(None, 'blk', 'nrm')
- residual: float32 [10, 3072, 512], P(None, 'blk', 'nrm')
Inputs may be any that keep to these rules, and one draw needn't show every extreme that they name: donors[b, s, j] lies in the same slab of 256 wall-normal cells as j (the same value of j // 256) and differs from j by at most 3.
All inputs are finite; a program needn't handle non-finite values. No bound on the sum of `pattern` on one device may be relied on, other than what follows from the above.
Results may differ from a plain program's by a relative error of at most 0.00015.
Values sent between devices are 32-bit elements; how exact they have to be, the bound alone decides.
No kernel may reach another device: no remote copies, remote signals or barrier semaphores. Data moves between devices by JAX's collectives and lax.ppermute only.
A program may use at most 32 MiB of HBM per device.

v0:
```python
import jax
import jax.numpy as jnp
from jax import lax
from jax.sharding import PartitionSpec as P

ITERS = 6


OMEGA = 0.3
DELTA = 0.9


def padded(cells, sides, width):
    for axis, dim in sides:
        count = lax.axis_size(axis)
        ends = count - 1
        head = lax.slice_in_dim(cells, 0, width, axis=dim)
        tail = lax.slice_in_dim(cells, cells.shape[dim] - width, cells.shape[dim], axis=dim)
        cells = jnp.concatenate(
            [
                lax.ppermute(tail, axis, [(i, (i + 1) % count) for i in range(ends)]),
                cells,
                lax.ppermute(head, axis, [((i + 1) % count, i) for i in range(ends)]),
            ],
            axis=dim,
        )
    return cells


def rotate(v):
    half = v.shape[0] // 2
    return jnp.concatenate([-v[half:], v[:half]], 0)


def on_device(right_side, mean_flow, jac_basis, pattern, shift_diag, dissipation, donors):
    highest = lax.Precision.HIGHEST
    nvar = right_side.shape[0]
    nmean = mean_flow.shape[0]
    width = right_side.shape[2]
    rhs, flow, shifts, damping, masks = (right_side, mean_flow, shift_diag, dissipation, pattern)
    donor_local = donors[0] - lax.axis_index("nrm") * width
    rows = rhs.shape[1]
    cols = rhs.shape[2]
    weights = masks.astype(jnp.float32)
    basis_flat = jac_basis.reshape(4, nmean * nvar, nvar)

    def precond(vec):
        return (shifts * vec - OMEGA * rotate(vec)) / (shifts * shifts + OMEGA * OMEGA)

    sigma = 1.0 / DELTA
    rho = DELTA
    solution = jnp.zeros_like(rhs)
    residual = rhs
    direction = precond(residual)
    for step in range(ITERS):
        solution = solution + direction
        extended = padded(direction, (("blk", 1),), 2)
        left = jnp.take(extended[:, :2, :], donor_local[0], axis=2)
        right = jnp.take(extended[:, -2:, :], donor_local[1], axis=2)
        wide = jnp.concatenate([left, direction, right], 1)
        tall = padded(direction, (("nrm", 2),), 1)
        neighbours = [wide[:, 1 : rows + 1], wide[:, 3 : rows + 3], tall[:, :, :-2], tall[:, :, 2:]]
        result = (
            shifts * direction
            + OMEGA * rotate(direction)
            + damping * (wide[:, 0:rows] + wide[:, 4 : rows + 4])
        )
        for face in range(4):
            product = jnp.dot(
                basis_flat[face],
                neighbours[face].reshape(nvar, rows * cols),
                precision=highest,
                preferred_element_type=jnp.float32,
            )
            product = product.reshape(nmean, nvar, rows, cols)
            term = jnp.sum(flow[:, None] * product, 0)
            result = result + weights[face] * term
        residual = residual - result
        if step + 1 < ITERS:
            rho_new = 1.0 / (2.0 * sigma - rho)
            direction = rho_new * rho * direction + 2.0 * rho_new / DELTA * precond(residual)
            rho = rho_new
    return (solution, residual)


def solution(mesh):
    return jax.shard_map(
        on_device,
        mesh=mesh,
        in_specs=(
            P(None, "blk", "nrm"),
            P(None, "blk", "nrm"),
            P(),
            P(None, "blk", "nrm"),
            P("blk", "nrm"),
            P("blk", "nrm"),
            P("blk", None, "nrm"),
        ),
        out_specs=(P(None, "blk", "nrm"), P(None, "blk", "nrm")),
        check_vma=False,
    )
```

profile of v0, /device:TPU:512, one launch (start us, length us, event | category | flops | bytes accessed | tf_op | source)
XLA Modules:
  0.0 154.9 jit_solution(14836854252910737839)
XLA Ops:
  0.6 0.7 multiply_add_fusion
  1.4 0.8 slice_negate_fusion.11
  2.2 0.9 fusion.61
  3.1 1.9 %collective-permute-start = (f32[10,2,256]{2,1,0:T(2,128)S(1)}, f32[10,2,256]{2,1,0:T(2,128)S(1)}, u32[]{:S(2)}, u32[]{:S(2)}) collective-permute-start(f32[10,2,256]{2,1,0:T(2,128)S(1)} %get-tuple-element.107), channel_id=1, source_target_pairs={{0,2},{2,4},{4,6},{6,8},{8,10},{10,12},{12,14},{14,16},{16,18},{18... | collective-permute-start | bytes 61448 | tf_op jit(solution)/shard_map/ppermute | solution.py:21
  5.1 10.0 %collective-permute-start.1 = (f32[10,2,256]{2,1,0:T(2,128)S(1)}, f32[10,2,256]{2,1,0:T(2,128)S(1)}, u32[]{:S(2)}, u32[]{:S(2)}) collective-permute-start(f32[10,2,256]{2,1,0:T(2,128)S(1)} %get-tuple-element.108), channel_id=1, source_target_pairs={{2,0},{4,2},{6,4},{8,6},{10,8},{12,10},{14,12},{16,14},{18,16},{20... | collective-permute-start | bytes 61448 | tf_op jit(solution)/shard_map/ppermute | solution.py:23
  15.1 3.5 %collective-permute-start.2 = (f32[10,8,1]{2,1,0:T(8,128)S(1)}, f32[10,8,1]{2,1,0:T(8,128)S(1)}, u32[]{:S(2)}, u32[]{:S(2)}) collective-permute-start(f32[10,8,1]{2,1,0:T(8,128)S(1)} %get-tuple-element.104), channel_id=1, source_target_pairs={{0,1},{2,3},{4,5},{6,7},{8,9},{10,11},{12,13},{14,15},{16,17},{18,... | collective-permute-start | bytes 968 | tf_op jit(solution)/shard_map/ppermute | solution.py:21
  18.6 1.3 collective-permute-start.3
  20.6 1.0 gather_fusion
  22.1 1.0 gather_fusion.1
  23.7 0.8 collective-permute-done.3
  24.7 0.5 fusion.102
  25.5 0.5 fusion.103
  26.2 0.5 fusion.104
  27.0 0.5 fusion.105
  27.7 0.7 copy-done
  28.6 0.5 copy-done.1
  29.6 1.9 %collective-permute-start.4 = (f32[10,2,256]{2,1,0:T(2,128)S(1)}, f32[10,2,256]{2,1,0:T(2,128)S(1)}, u32[]{:S(2)}, u32[]{:S(2)}) collective-permute-start(f32[10,2,256]{2,1,0:T(2,128)S(1)} %get-tuple-element.95), channel_id=1, source_target_pairs={{0,2},{2,4},{4,6},{6,8},{8,10},{10,12},{12,14},{14,16},{16,18},{18... | collective-permute-start | bytes 61448 | tf_op jit(solution)/shard_map/ppermute | solution.py:21
  31.5 10.0 %collective-permute-start.5 = (f32[10,2,256]{2,1,0:T(2,128)S(1)}, f32[10,2,256]{2,1,0:T(2,128)S(1)}, u32[]{:S(2)}, u32[]{:S(2)}) collective-permute-start(f32[10,2,256]{2,1,0:T(2,128)S(1)} %get-tuple-element.96), channel_id=1, source_target_pairs={{2,0},{4,2},{6,4},{8,6},{10,8},{12,10},{14,12},{16,14},{18,16},{20... | collective-permute-start | bytes 61448 | tf_op jit(solution)/shard_map/ppermute | solution.py:23
  41.5 3.8 %collective-permute-start.6 = (f32[10,8,1]{2,1,0:T(8,128)S(1)}, f32[10,8,1]{2,1,0:T(8,128)S(1)}, u32[]{:S(2)}, u32[]{:S(2)}) collective-permute-start(f32[10,8,1]{2,1,0:T(8,128)S(1)} %get-tuple-element.92), channel_id=1, source_target_pairs={{0,1},{2,3},{4,5},{6,7},{8,9},{10,11},{12,13},{14,15},{16,17},{18,... | collective-permute-start | bytes 968 | tf_op jit(solution)/shard_map/ppermute | solution.py:21
  45.3 1.3 collective-permute-start.7
  46.8 1.0 gather_fusion.2
  48.3 1.0 gather_fusion.3
  49.9 1.3 collective-permute-done.7
  52.1 0.5 fusion.108
  53.7 0.5 fusion.106
  54.8 1.9 %collective-permute-start.8 = (f32[10,2,256]{2,1,0:T(2,128)S(1)}, f32[10,2,256]{2,1,0:T(2,128)S(1)}, u32[]{:S(2)}, u32[]{:S(2)}) collective-permute-start(f32[10,2,256]{2,1,0:T(2,128)S(1)} %get-tuple-element.83), channel_id=1, source_target_pairs={{0,2},{2,4},{4,6},{6,8},{8,10},{10,12},{12,14},{14,16},{16,18},{18... | collective-permute-start | bytes 61448 | tf_op jit(solution)/shard_map/ppermute | solution.py:21
  56.7 10.0 %collective-permute-start.9 = (f32[10,2,256]{2,1,0:T(2,128)S(1)}, f32[10,2,256]{2,1,0:T(2,128)S(1)}, u32[]{:S(2)}, u32[]{:S(2)}) collective-permute-start(f32[10,2,256]{2,1,0:T(2,128)S(1)} %get-tuple-element.84), channel_id=1, source_target_pairs={{2,0},{4,2},{6,4},{8,6},{10,8},{12,10},{14,12},{16,14},{18,16},{20... | collective-permute-start | bytes 61448 | tf_op jit(solution)/shard_map/ppermute | solution.py:23
  66.7 3.2 %collective-permute-start.10 = (f32[10,8,1]{2,1,0:T(8,128)S(1)}, f32[10,8,1]{2,1,0:T(8,128)S(1)}, u32[]{:S(2)}, u32[]{:S(2)}) collective-permute-start(f32[10,8,1]{2,1,0:T(8,128)S(1)} %get-tuple-element.80), channel_id=1, source_target_pairs={{0,1},{2,3},{4,5},{6,7},{8,9},{10,11},{12,13},{14,15},{16,17},{18,... | collective-permute-start | bytes 968 | tf_op jit(solution)/shard_map/ppermute | solution.py:21
  69.9 1.5 collective-permute-start.11
  71.6 1.0 gather_fusion.4
  73.1 1.0 gather_fusion.5
  74.7 1.1 collective-permute-done.11
  78.3 0.5 fusion.110
  79.4 1.9 %collective-permute-start.12 = (f32[10,2,256]{2,1,0:T(2,128)S(1)}, f32[10,2,256]{2,1,0:T(2,128)S(1)}, u32[]{:S(2)}, u32[]{:S(2)}) collective-permute-start(f32[10,2,256]{2,1,0:T(2,128)S(1)} %get-tuple-element.71), channel_id=1, source_target_pairs={{0,2},{2,4},{4,6},{6,8},{8,10},{10,12},{12,14},{14,16},{16,18},{18... | collective-permute-start | bytes 61448 | tf_op jit(solution)/shard_map/ppermute | solution.py:21
  81.3 10.0 %collective-permute-start.13 = (f32[10,2,256]{2,1,0:T(2,128)S(1)}, f32[10,2,256]{2,1,0:T(2,128)S(1)}, u32[]{:S(2)}, u32[]{:S(2)}) collective-permute-start(f32[10,2,256]{2,1,0:T(2,128)S(1)} %get-tuple-element.72), channel_id=1, source_target_pairs={{2,0},{4,2},{6,4},{8,6},{10,8},{12,10},{14,12},{16,14},{18,16},{20... | collective-permute-start | bytes 61448 | tf_op jit(solution)/shard_map/ppermute | solution.py:23
  91.3 3.4 %collective-permute-start.14 = (f32[10,8,1]{2,1,0:T(8,128)S(1)}, f32[10,8,1]{2,1,0:T(8,128)S(1)}, u32[]{:S(2)}, u32[]{:S(2)}) collective-permute-start(f32[10,8,1]{2,1,0:T(8,128)S(1)} %get-tuple-element.68), channel_id=1, source_target_pairs={{0,1},{2,3},{4,5},{6,7},{8,9},{10,11},{12,13},{14,15},{16,17},{18,... | collective-permute-start | bytes 968 | tf_op jit(solution)/shard_map/ppermute | solution.py:21
  94.7 1.3 collective-permute-start.15
  96.2 1.0 gather_fusion.6
  97.7 1.0 gather_fusion.7
  99.3 1.3 collective-permute-done.15
  100.8 0.5 fusion.115
  103.1 0.5 fusion.114
  104.2 1.9 %collective-permute-start.16 = (f32[10,2,256]{2,1,0:T(2,128)S(1)}, f32[10,2,256]{2,1,0:T(2,128)S(1)}, u32[]{:S(2)}, u32[]{:S(2)}) collective-permute-start(f32[10,2,256]{2,1,0:T(2,128)S(1)} %get-tuple-element.59), channel_id=1, source_target_pairs={{0,2},{2,4},{4,6},{6,8},{8,10},{10,12},{12,14},{14,16},{16,18},{18... | collective-permute-start | bytes 61448 | tf_op jit(solution)/shard_map/ppermute | solution.py:21
  106.2 10.0 %collective-permute-start.17 = (f32[10,2,256]{2,1,0:T(2,128)S(1)}, f32[10,2,256]{2,1,0:T(2,128)S(1)}, u32[]{:S(2)}, u32[]{:S(2)}) collective-permute-start(f32[10,2,256]{2,1,0:T(2,128)S(1)} %get-tuple-element.60), channel_id=1, source_target_pairs={{2,0},{4,2},{6,4},{8,6},{10,8},{12,10},{14,12},{16,14},{18,16},{20... | collective-permute-start | bytes 61448 | tf_op jit(solution)/shard_map/ppermute | solution.py:23
  116.1 3.2 %collective-permute-start.18 = (f32[10,8,1]{2,1,0:T(8,128)S(1)}, f32[10,8,1]{2,1,0:T(8,128)S(1)}, u32[]{:S(2)}, u32[]{:S(2)}) collective-permute-start(f32[10,8,1]{2,1,0:T(8,128)S(1)} %get-tuple-element.56), channel_id=1, source_target_pairs={{0,1},{2,3},{4,5},{6,7},{8,9},{10,11},{12,13},{14,15},{16,17},{18,... | collective-permute-start | bytes 968 | tf_op jit(solution)/shard_map/ppermute | solution.py:21
  119.4 1.5 collective-permute-start.19
  121.1 1.0 gather_fusion.8
  122.6 1.0 gather_fusion.9
  124.2 1.1 collective-permute-done.19
  125.5 0.5 fusion.119
  126.2 0.5 fusion.120
  127.8 0.5 fusion.118
  128.7 0.7 add_add_fusion
  129.5 1.9 %collective-permute-start.20 = (f32[10,2,256]{2,1,0:T(2,128)S(1)}, f32[10,2,256]{2,1,0:T(2,128)S(1)}, u32[]{:S(2)}, u32[]{:S(2)}) collective-permute-start(f32[10,2,256]{2,1,0:T(2,128)S(1)} %get-tuple-element.47), channel_id=1, source_target_pairs={{0,2},{2,4},{4,6},{6,8},{8,10},{10,12},{12,14},{14,16},{16,18},{18... | collective-permute-start | bytes 61448 | tf_op jit(solution)/shard_map/ppermute | solution.py:21
  131.5 10.0 %collective-permute-start.21 = (f32[10,2,256]{2,1,0:T(2,128)S(1)}, f32[10,2,256]{2,1,0:T(2,128)S(1)}, u32[]{:S(2)}, u32[]{:S(2)}) collective-permute-start(f32[10,2,256]{2,1,0:T(2,128)S(1)} %get-tuple-element.48), channel_id=1, source_target_pairs={{2,0},{4,2},{6,4},{8,6},{10,8},{12,10},{14,12},{16,14},{18,16},{20... | collective-permute-start | bytes 61448 | tf_op jit(solution)/shard_map/ppermute | solution.py:23
  141.4 3.5 %collective-permute-start.22 = (f32[10,8,1]{2,1,0:T(8,128)S(1)}, f32[10,8,1]{2,1,0:T(8,128)S(1)}, u32[]{:S(2)}, u32[]{:S(2)}) collective-permute-start(f32[10,8,1]{2,1,0:T(8,128)S(1)} %get-tuple-element.44), channel_id=1, source_target_pairs={{0,1},{2,3},{4,5},{6,7},{8,9},{10,11},{12,13},{14,15},{16,17},{18,... | collective-permute-start | bytes 968 | tf_op jit(solution)/shard_map/ppermute | solution.py:21
  144.9 1.3 collective-permute-start.23
  146.4 1.0 gather_fusion.10
  147.9 1.0 gather_fusion.11
  149.5 1.3 collective-permute-done.23
  151.0 0.5 fusion.123
  151.8 0.5 fusion.124
  153.3 0.5 fusion.122
  154.1 0.7 fusion.8
  (230 shorter events, 20.9 us)
Async XLA Ops:
  0.6 19.3 %copy-start.6 = (s32[1,2,256]{2,1,0:T(2,128)S(1)}, s32[1,2,256]{2,1,0:T(2,128)}, u32[]{:S(2)}) copy-start(s32[1,2,256]{2,1,0:T(2,128)} %param.15) | copy-start | bytes 6148
  0.6 19.4 %copy-start.4 = (f32[4,5,10,10]{3,0,2,1:T(4,128)S(1)}, f32[4,5,10,10]{3,0,2,1:T(4,128)}, u32[]{:S(2)}) copy-start(f32[4,5,10,10]{3,0,2,1:T(4,128)} %param.11) | copy-start | bytes 24004
  2.2 18.1 %copy-start.5 = (s32[4,8,256]{2,1,0:T(8,128)S(1)}, s32[4,8,256]{2,1,0:T(8,128)}, u32[]{:S(2)}) copy-start(s32[4,8,256]{2,1,0:T(8,128)} %param.12) | copy-start | bytes 98308
  3.1 17.3 %collective-permute-start = (f32[10,2,256]{2,1,0:T(2,128)S(1)}, f32[10,2,256]{2,1,0:T(2,128)S(1)}, u32[]{:S(2)}, u32[]{:S(2)}) collective-permute-start(f32[10,2,256]{2,1,0:T(2,128)S(1)} %get-tuple-element.107), channel_id=1, source_target_pairs={{0,2},{2,4},{4,6},{6,8},{8,10},{10,12},{12,14},{14,16},{16,18},{18... | collective-permute-start | bytes 61448 | tf_op jit(solution)/shard_map/ppermute | solution.py:21
  5.1 16.9 %collective-permute-start.1 = (f32[10,2,256]{2,1,0:T(2,128)S(1)}, f32[10,2,256]{2,1,0:T(2,128)S(1)}, u32[]{:S(2)}, u32[]{:S(2)}) collective-permute-start(f32[10,2,256]{2,1,0:T(2,128)S(1)} %get-tuple-element.108), channel_id=1, source_target_pairs={{2,0},{4,2},{6,4},{8,6},{10,8},{12,10},{14,12},{16,14},{18,16},{20... | collective-permute-start | bytes 61448 | tf_op jit(solution)/shard_map/ppermute | solution.py:23
  15.1 8.6 %collective-permute-start.2 = (f32[10,8,1]{2,1,0:T(8,128)S(1)}, f32[10,8,1]{2,1,0:T(8,128)S(1)}, u32[]{:S(2)}, u32[]{:S(2)}) collective-permute-start(f32[10,8,1]{2,1,0:T(8,128)S(1)} %get-tuple-element.104), channel_id=1, source_target_pairs={{0,1},{2,3},{4,5},{6,7},{8,9},{10,11},{12,13},{14,15},{16,17},{18,... | collective-permute-start | bytes 968 | tf_op jit(solution)/shard_map/ppermute | solution.py:21
  18.6 5.9 %collective-permute-start.3 = (f32[10,8,1]{2,1,0:T(8,128)S(1)}, f32[10,8,1]{2,1,0:T(8,128)S(1)}, u32[]{:S(2)}, u32[]{:S(2)}) collective-permute-start(f32[10,8,1]{2,1,0:T(8,128)S(1)} %get-tuple-element.103), channel_id=1, source_target_pairs={{1,0},{3,2},{5,4},{7,6},{9,8},{11,10},{13,12},{15,14},{17,16},{19,... | collective-permute-start | bytes 968 | tf_op jit(solution)/shard_map/ppermute | solution.py:23
  27.7 0.8 copy-start
  28.4 0.7 copy-start.1
  28.4 0.9 copy-start.2
  28.5 0.9 copy-start.3
  29.6 17.0 %collective-permute-start.4 = (f32[10,2,256]{2,1,0:T(2,128)S(1)}, f32[10,2,256]{2,1,0:T(2,128)S(1)}, u32[]{:S(2)}, u32[]{:S(2)}) collective-permute-start(f32[10,2,256]{2,1,0:T(2,128)S(1)} %get-tuple-element.95), channel_id=1, source_target_pairs={{0,2},{2,4},{4,6},{6,8},{8,10},{10,12},{12,14},{14,16},{16,18},{18... | collective-permute-start | bytes 61448 | tf_op jit(solution)/shard_map/ppermute | solution.py:21
  31.5 16.6 %collective-permute-start.5 = (f32[10,2,256]{2,1,0:T(2,128)S(1)}, f32[10,2,256]{2,1,0:T(2,128)S(1)}, u32[]{:S(2)}, u32[]{:S(2)}) collective-permute-start(f32[10,2,256]{2,1,0:T(2,128)S(1)} %get-tuple-element.96), channel_id=1, source_target_pairs={{2,0},{4,2},{6,4},{8,6},{10,8},{12,10},{14,12},{16,14},{18,16},{20... | collective-permute-start | bytes 61448 | tf_op jit(solution)/shard_map/ppermute | solution.py:23
  41.5 8.3 %collective-permute-start.6 = (f32[10,8,1]{2,1,0:T(8,128)S(1)}, f32[10,8,1]{2,1,0:T(8,128)S(1)}, u32[]{:S(2)}, u32[]{:S(2)}) collective-permute-start(f32[10,8,1]{2,1,0:T(8,128)S(1)} %get-tuple-element.92), channel_id=1, source_target_pairs={{0,1},{2,3},{4,5},{6,7},{8,9},{10,11},{12,13},{14,15},{16,17},{18,... | collective-permute-start | bytes 968 | tf_op jit(solution)/shard_map/ppermute | solution.py:21
  45.3 5.9 %collective-permute-start.7 = (f32[10,8,1]{2,1,0:T(8,128)S(1)}, f32[10,8,1]{2,1,0:T(8,128)S(1)}, u32[]{:S(2)}, u32[]{:S(2)}) collective-permute-start(f32[10,8,1]{2,1,0:T(8,128)S(1)} %get-tuple-element.91), channel_id=1, source_target_pairs={{1,0},{3,2},{5,4},{7,6},{9,8},{11,10},{13,12},{15,14},{17,16},{19,... | collective-permute-start | bytes 968 | tf_op jit(solution)/shard_map/ppermute | solution.py:23
  54.8 16.6 %collective-permute-start.8 = (f32[10,2,256]{2,1,0:T(2,128)S(1)}, f32[10,2,256]{2,1,0:T(2,128)S(1)}, u32[]{:S(2)}, u32[]{:S(2)}) collective-permute-start(f32[10,2,256]{2,1,0:T(2,128)S(1)} %get-tuple-element.83), channel_id=1, source_target_pairs={{0,2},{2,4},{4,6},{6,8},{8,10},{10,12},{12,14},{14,16},{16,18},{18... | collective-permute-start | bytes 61448 | tf_op jit(solution)/shard_map/ppermute | solution.py:21
  56.7 16.2 %collective-permute-start.9 = (f32[10,2,256]{2,1,0:T(2,128)S(1)}, f32[10,2,256]{2,1,0:T(2,128)S(1)}, u32[]{:S(2)}, u32[]{:S(2)}) collective-permute-start(f32[10,2,256]{2,1,0:T(2,128)S(1)} %get-tuple-element.84), channel_id=1, source_target_pairs={{2,0},{4,2},{6,4},{8,6},{10,8},{12,10},{14,12},{16,14},{18,16},{20... | collective-permute-start | bytes 61448 | tf_op jit(solution)/shard_map/ppermute | solution.py:23
  66.7 8.0 %collective-permute-start.10 = (f32[10,8,1]{2,1,0:T(8,128)S(1)}, f32[10,8,1]{2,1,0:T(8,128)S(1)}, u32[]{:S(2)}, u32[]{:S(2)}) collective-permute-start(f32[10,8,1]{2,1,0:T(8,128)S(1)} %get-tuple-element.80), channel_id=1, source_target_pairs={{0,1},{2,3},{4,5},{6,7},{8,9},{10,11},{12,13},{14,15},{16,17},{18,... | collective-permute-start | bytes 968 | tf_op jit(solution)/shard_map/ppermute | solution.py:21
  69.9 5.9 %collective-permute-start.11 = (f32[10,8,1]{2,1,0:T(8,128)S(1)}, f32[10,8,1]{2,1,0:T(8,128)S(1)}, u32[]{:S(2)}, u32[]{:S(2)}) collective-permute-start(f32[10,8,1]{2,1,0:T(8,128)S(1)} %get-tuple-element.79), channel_id=1, source_target_pairs={{1,0},{3,2},{5,4},{7,6},{9,8},{11,10},{13,12},{15,14},{17,16},{19,... | collective-permute-start | bytes 968 | tf_op jit(solution)/shard_map/ppermute | solution.py:23
  79.4 16.6 %collective-permute-start.12 = (f32[10,2,256]{2,1,0:T(2,128)S(1)}, f32[10,2,256]{2,1,0:T(2,128)S(1)}, u32[]{:S(2)}, u32[]{:S(2)}) collective-permute-start(f32[10,2,256]{2,1,0:T(2,128)S(1)} %get-tuple-element.71), channel_id=1, source_target_pairs={{0,2},{2,4},{4,6},{6,8},{8,10},{10,12},{12,14},{14,16},{16,18},{18... | collective-permute-start | bytes 61448 | tf_op jit(solution)/shard_map/ppermute | solution.py:21
  81.3 16.2 %collective-permute-start.13 = (f32[10,2,256]{2,1,0:T(2,128)S(1)}, f32[10,2,256]{2,1,0:T(2,128)S(1)}, u32[]{:S(2)}, u32[]{:S(2)}) collective-permute-start(f32[10,2,256]{2,1,0:T(2,128)S(1)} %get-tuple-element.72), channel_id=1, source_target_pairs={{2,0},{4,2},{6,4},{8,6},{10,8},{12,10},{14,12},{16,14},{18,16},{20... | collective-permute-start | bytes 61448 | tf_op jit(solution)/shard_map/ppermute | solution.py:23
  91.3 8.0 %collective-permute-start.14 = (f32[10,8,1]{2,1,0:T(8,128)S(1)}, f32[10,8,1]{2,1,0:T(8,128)S(1)}, u32[]{:S(2)}, u32[]{:S(2)}) collective-permute-start(f32[10,8,1]{2,1,0:T(8,128)S(1)} %get-tuple-element.68), channel_id=1, source_target_pairs={{0,1},{2,3},{4,5},{6,7},{8,9},{10,11},{12,13},{14,15},{16,17},{18,... | collective-permute-start | bytes 968 | tf_op jit(solution)/shard_map/ppermute | solution.py:21
  94.7 5.9 %collective-permute-start.15 = (f32[10,8,1]{2,1,0:T(8,128)S(1)}, f32[10,8,1]{2,1,0:T(8,128)S(1)}, u32[]{:S(2)}, u32[]{:S(2)}) collective-permute-start(f32[10,8,1]{2,1,0:T(8,128)S(1)} %get-tuple-element.67), channel_id=1, source_target_pairs={{1,0},{3,2},{5,4},{7,6},{9,8},{11,10},{13,12},{15,14},{17,16},{19,... | collective-permute-start | bytes 968 | tf_op jit(solution)/shard_map/ppermute | solution.py:23
  104.2 16.7 %collective-permute-start.16 = (f32[10,2,256]{2,1,0:T(2,128)S(1)}, f32[10,2,256]{2,1,0:T(2,128)S(1)}, u32[]{:S(2)}, u32[]{:S(2)}) collective-permute-start(f32[10,2,256]{2,1,0:T(2,128)S(1)} %get-tuple-element.59), channel_id=1, source_target_pairs={{0,2},{2,4},{4,6},{6,8},{8,10},{10,12},{12,14},{14,16},{16,18},{18... | collective-permute-start | bytes 61448 | tf_op jit(solution)/shard_map/ppermute | solution.py:21
  106.2 16.3 %collective-permute-start.17 = (f32[10,2,256]{2,1,0:T(2,128)S(1)}, f32[10,2,256]{2,1,0:T(2,128)S(1)}, u32[]{:S(2)}, u32[]{:S(2)}) collective-permute-start(f32[10,2,256]{2,1,0:T(2,128)S(1)} %get-tuple-element.60), channel_id=1, source_target_pairs={{2,0},{4,2},{6,4},{8,6},{10,8},{12,10},{14,12},{16,14},{18,16},{20... | collective-permute-start | bytes 61448 | tf_op jit(solution)/shard_map/ppermute | solution.py:23
  116.1 8.0 %collective-permute-start.18 = (f32[10,8,1]{2,1,0:T(8,128)S(1)}, f32[10,8,1]{2,1,0:T(8,128)S(1)}, u32[]{:S(2)}, u32[]{:S(2)}) collective-permute-start(f32[10,8,1]{2,1,0:T(8,128)S(1)} %get-tuple-element.56), channel_id=1, source_target_pairs={{0,1},{2,3},{4,5},{6,7},{8,9},{10,11},{12,13},{14,15},{16,17},{18,... | collective-permute-start | bytes 968 | tf_op jit(solution)/shard_map/ppermute | solution.py:21
  119.4 5.9 %collective-permute-start.19 = (f32[10,8,1]{2,1,0:T(8,128)S(1)}, f32[10,8,1]{2,1,0:T(8,128)S(1)}, u32[]{:S(2)}, u32[]{:S(2)}) collective-permute-start(f32[10,8,1]{2,1,0:T(8,128)S(1)} %get-tuple-element.55), channel_id=1, source_target_pairs={{1,0},{3,2},{5,4},{7,6},{9,8},{11,10},{13,12},{15,14},{17,16},{19,... | collective-permute-start | bytes 968 | tf_op jit(solution)/shard_map/ppermute | solution.py:23
  129.5 16.7 %collective-permute-start.20 = (f32[10,2,256]{2,1,0:T(2,128)S(1)}, f32[10,2,256]{2,1,0:T(2,128)S(1)}, u32[]{:S(2)}, u32[]{:S(2)}) collective-permute-start(f32[10,2,256]{2,1,0:T(2,128)S(1)} %get-tuple-element.47), channel_id=1, source_target_pairs={{0,2},{2,4},{4,6},{6,8},{8,10},{10,12},{12,14},{14,16},{16,18},{18... | collective-permute-start | bytes 61448 | tf_op jit(solution)/shard_map/ppermute | solution.py:21
  131.5 16.2 %collective-permute-start.21 = (f32[10,2,256]{2,1,0:T(2,128)S(1)}, f32[10,2,256]{2,1,0:T(2,128)S(1)}, u32[]{:S(2)}, u32[]{:S(2)}) collective-permute-start(f32[10,2,256]{2,1,0:T(2,128)S(1)} %get-tuple-element.48), channel_id=1, source_target_pairs={{2,0},{4,2},{6,4},{8,6},{10,8},{12,10},{14,12},{16,14},{18,16},{20... | collective-permute-start | bytes 61448 | tf_op jit(solution)/shard_map/ppermute | solution.py:23
  141.4 8.0 %collective-permute-start.22 = (f32[10,8,1]{2,1,0:T(8,128)S(1)}, f32[10,8,1]{2,1,0:T(8,128)S(1)}, u32[]{:S(2)}, u32[]{:S(2)}) collective-permute-start(f32[10,8,1]{2,1,0:T(8,128)S(1)} %get-tuple-element.44), channel_id=1, source_target_pairs={{0,1},{2,3},{4,5},{6,7},{8,9},{10,11},{12,13},{14,15},{16,17},{18,... | collective-permute-start | bytes 968 | tf_op jit(solution)/shard_map/ppermute | solution.py:21
  144.9 5.9 %collective-permute-start.23 = (f32[10,8,1]{2,1,0:T(8,128)S(1)}, f32[10,8,1]{2,1,0:T(8,128)S(1)}, u32[]{:S(2)}, u32[]{:S(2)}) collective-permute-start(f32[10,8,1]{2,1,0:T(8,128)S(1)} %get-tuple-element.43), channel_id=1, source_target_pairs={{1,0},{3,2},{5,4},{7,6},{9,8},{11,10},{13,12},{15,14},{17,16},{19,... | collective-permute-start | bytes 968 | tf_op jit(solution)/shard_map/ppermute | solution.py:23
where the time goes:
time: 156 us; the launch traced here: 155 us
  starting transfers between devices  100 us (64%)
  local copies, waits for them, and re-layouts  23 us (15%)
  matrix products  12.1 us (8%)
  other arithmetic  10.2 us (7%)
  waiting for transfers between devices  7.09 us (5%)
  between operations  2.42 us (2%)
    ppermute x12, starting transfers between devices, padded(): lax.ppermute(head, axis, [((i + 1) % count, i) for i in range(ends)])  68 us
    ppermute x12, starting transfers between devices, padded(): lax.ppermute(tail, axis, [(i, (i + 1) % count) for i in range(ends)])  32.1 us
    dot_general x24, matrix products, on_device(): jnp.dot(basis_flat[face], neighbours[face].reshape(nvar, rows * cols), pr...  12.1 us
    ppermute x12, waiting for transfers between devices, padded(): lax.ppermute(head, axis, [((i + 1) % count, i) for i in range(ends)])  7.05 us
    unnamed x110, local copies, waits for them, and re-layouts  6.95 us
    gather x6, local copies, waits for them, and re-layouts, on_device(): left = jnp.take(extended[:, :2, :], donor_local[0], axis=2)  5.87 us
    gather x6, local copies, waits for them, and re-layouts, on_device(): right = jnp.take(extended[:, -2:, :], donor_local[1], axis=2)  5.86 us
  transfers between devices with their start and end apart: 24, of which 6 were waited for; matrix products, arithmetic and copies ran while one was open for 13% of the time, Pallas kernels for 0%

commit v1 on v0

v1 whole, which is shorter than its diff:
```python
import functools

import jax
import jax.numpy as jnp
from jax import lax
from jax.experimental import pallas as pl
from jax.experimental.pallas import tpu as pltpu
from jax.sharding import PartitionSpec as P

ITERS = 6
OMEGA = 0.3
DELTA = 0.9

SHIFT, DAMP, DON0, DON1 = 5, 6, 7, 13
MASK = (14, 15, 21, 22)
FLOW = 16
PA, PB = 23, 24
FEATS = 24
HALO = 16
LANES = 128
RING = 384

L2, L1, OWN, R1, R2 = 0, 8, 20, 32, 44
SLOTS = 48
RANGES = (
    ((2, 1), (8, 4), (20, 4), (32, 4), (44, 1)),
    ((8, 4), (20, 4), (32, 4)),
    ((10, 3), (20, 4), (32, 3)),
    ((12, 2), (20, 4), (32, 2)),
    ((14, 1), (20, 4), (32, 1)),
    ((20, 4),),
)
LISTS = ((L2 + 3, DON1), (L1, DON0), (L1, DON1), (OWN, DON0), (OWN, DON1), (R1, DON0), (R1, DON1), (R2, DON0))
FILLS = (
    (4, 8, 0), (6, 2, 1), (16, 20, 2), (18, 14, 3),
    (28, 32, 4), (30, 26, 5), (40, 44, 6), (42, 38, 7),
)
FILLS_AT = (range(8), (1, 2, 3, 4, 5, 6), (2, 3, 4, 5), (2, 3, 4, 5), (2, 3, 4, 5), (3, 4))


def chebyshev():
    sigma = 1.0 / DELTA
    rho = DELTA
    steps = []
    for _ in range(ITERS - 1):
        rho_new = 1.0 / (2.0 * sigma - rho)
        steps.append((rho_new * rho, 2.0 * rho_new / DELTA))
        rho = rho_new
    return steps


def pack_kernel(rhs, flow, mask, shift, damp, donors, main, strip):
    nrm = lax.axis_index("nrm")
    width = rhs.shape[2]
    here = lax.broadcasted_iota(jnp.int32, (1, width), 1) + nrm * width
    offsets = (donors[0] - here).astype(jnp.float32)
    lane = lax.broadcasted_iota(jnp.int32, (FEATS, LANES), 1)
    sent = jnp.zeros((FEATS, LANES), jnp.float32)
    for i in range(rhs.shape[1]):
        at = slice(i * width, (i + 1) * width)
        main[0:5, at] = rhs[0:5, i, :]
        main[SHIFT : SHIFT + 1, at] = shift[i : i + 1, :]
        main[DAMP : DAMP + 1, at] = damp[i : i + 1, :]
        main[DON0 : DON0 + 1, at] = offsets[0:1]
        main[8:13, at] = rhs[5:10, i, :]
        main[DON1 : DON1 + 1, at] = offsets[1:2]
        main[14:16, at] = mask[0:2, i, :].astype(jnp.float32)
        main[16:21, at] = flow[:, i, :]
        main[21:23, at] = mask[2:4, i, :].astype(jnp.float32)
        main[23:24, at] = jnp.zeros((1, width), jnp.float32)
        first = main[:, i * width : i * width + LANES]
        last = main[:, (i + 1) * width - LANES : (i + 1) * width]
        low = first if i == 0 else pltpu.roll(first, HALO * i, 1)
        turn = (HALO * (i + 1)) % LANES
        high = pltpu.roll(last, turn, 1) if turn else last
        edge = jnp.where(nrm == 0, high, low)
        sent = jnp.where((lane >= HALO * i) & (lane < HALO * (i + 1)), edge, sent)
    strip[...] = sent


def solve_kernel(left2, left1, own, right1, right2, jac, sol_out, res_out, feat, dirs, res, sol, index, basis):
    nrm = lax.axis_index("nrm")
    lane8 = lax.broadcasted_iota(jnp.int32, (8, LANES), 1)
    row8 = lax.broadcasted_iota(jnp.int32, (8, RING), 0)
    lane = lax.broadcasted_iota(jnp.int32, (FEATS, LANES), 1)
    in_halo = jnp.where(nrm == 0, lane, LANES - 1 - lane) < HALO

    j = jac[...]
    high = j.astype(jnp.bfloat16)
    low = (j - high.astype(jnp.float32)).astype(jnp.bfloat16)
    basis[:, 0:64] = high
    basis[:, 64:128] = high
    basis[:, 128:192] = low

    def precond(pa, pb, a, b):
        return pa * a + pb * b, pa * b - pb * a

    def unpack(ref, columns, first_column, slot):
        for c in range(columns):
            s = slot + c
            halo = ref[:, columns * 256 : columns * 256 + LANES]
            halo = pltpu.roll(halo, lax.rem(112 * nrm + 2 * LANES - HALO * (first_column + c), LANES), 1)
            feat[s, 0:FEATS, 0:256] = ref[:, c * 256 : (c + 1) * 256]
            feat[s, 0:FEATS, 256:RING] = jnp.where(in_halo, halo, 0.0)
            shift = feat[s, SHIFT : SHIFT + 1, :]
            scale = 1.0 / (shift * shift + OMEGA * OMEGA)
            feat[s, PA : PA + 1, :] = shift * scale
            feat[s, PB : PB + 1, :] = OMEGA * scale
            a = jnp.where(row8 < 5, feat[s, 0:8, :], 0.0)
            b = jnp.where(row8 < 5, feat[s, 8:16, :], 0.0)
            res[s, 0] = a
            res[s, 1] = b
            da, db = precond(shift * scale, OMEGA * scale, a, b)
            dirs[0, s, 0] = da
            dirs[0, s, 1] = db

    unpack(left2, 4, 4, L2)
    unpack(left1, 8, 0, L1)
    unpack(own, 8, 0, OWN)
    unpack(right1, 8, 0, R1)
    unpack(right2, 4, 0, R2)

    for n, (slot, row) in enumerate(LISTS):
        for t in range(3):
            offset = feat[slot, row : row + 1, t * LANES : (t + 1) * LANES].astype(jnp.int32)
            index[n, t] = jnp.bitwise_and(lane8 + offset, LANES - 1)

    def ghosts(par, n):
        dst, src, which = FILLS[n]
        for t in range(3):
            at = index[which, t]
            across = jnp.abs(at - lane8) > LANES // 2
            for c in range(2):
                for h in range(2):
                    tiles = [dirs[par, src + c, h, :, u * LANES : (u + 1) * LANES] for u in ((t + 2) % 3, t, (t + 1) % 3)]
                    beside = jnp.where(lane8 < LANES // 2, tiles[2], tiles[0])
                    picked = jnp.where(
                        across,
                        jnp.take_along_axis(beside, at, axis=1),
                        jnp.take_along_axis(tiles[1], at, axis=1),
                    )
                    dirs[par, dst + c, h, :, t * LANES : (t + 1) * LANES] = picked

    steps = chebyshev()

    def column(s, par, step, mine):
        d = [dirs[par, s, h] for h in range(2)]
        near = []
        for h in range(2):
            near.append(
                [
                    dirs[par, s - 1, h],
                    dirs[par, s + 1, h],
                    pltpu.roll(d[h], 1, 1),
                    pltpu.roll(d[h], RING - 1, 1),
                ]
            )
        rows = []
        for face in range(4):
            m = feat[s, MASK[face] : MASK[face] + 1, :]
            for h in range(2):
                rows.append(m * near[h][face])
        full = jnp.concatenate(rows, 0)
        high = full.astype(jnp.bfloat16)
        low = (full - high.astype(jnp.float32)).astype(jnp.bfloat16)
        return d, jnp.concatenate([high, low, high], 0)

    def finish(s, par, step, mine, d, y):
        shift = feat[s, SHIFT : SHIFT + 1, :]
        damp = feat[s, DAMP : DAMP + 1, :]
        out = [shift * d[0] - OMEGA * d[1], shift * d[1] + OMEGA * d[0]]
        for h in range(2):
            out[h] = out[h] + damp * (dirs[par, s - 2, h] + dirs[par, s + 2, h])
        for m in range(5):
            f = feat[s, FLOW + m : FLOW + m + 1, :]
            for h in range(2):
                out[h] = out[h] + f * y[16 * m + 8 * h : 16 * m + 8 * h + 8]
        new = [res[s, h] - out[h] for h in range(2)]
        for h in range(2):
            res[s, h] = new[h]
            if mine:
                sol[s - OWN, h] = d[h] if step == 0 else sol[s - OWN, h] + d[h]
        if step + 1 < ITERS:
            keep, gain = steps[step]
            pa = feat[s, PA : PA + 1, :]
            pb = feat[s, PB : PB + 1, :]
            turned = precond(pa, pb, new[0], new[1])
            for h in range(2):
                dirs[1 - par, s, h] = keep * d[h] + gain * turned[h]

    for step in range(ITERS):
        par = step % 2
        for n in FILLS_AT[step]:
            ghosts(par, n)
        for start, pairs in RANGES[step]:
            mine = start == OWN

            def body(p, carry, start=start, mine=mine, step=step, par=par):
                s = start + 2 * p
                d0, w0 = column(s, par, step, mine)
                d1, w1 = column(s + 1, par, step, mine)
                y = jnp.dot(basis[...], jnp.concatenate([w0, w1], 1), preferred_element_type=jnp.float32)
                finish(s, par, step, mine, d0, y[:, :RING])
                finish(s + 1, par, step, mine, d1, y[:, RING:])
                return carry

            lax.fori_loop(0, pairs, body, 0, unroll=True)

    for i in range(8):
        for h in range(2):
            sol_out[5 * h : 5 * h + 5, i, :] = sol[i, h, 0:5, 0:256]
            res_out[5 * h : 5 * h + 5, i, :] = res[OWN + i, h, 0:5, 0:256]


def shifted(cells, by):
    count = lax.axis_size("blk")
    return lax.ppermute(cells, "blk", [(i, i + by) for i in range(count) if 0 <= i + by < count])


def on_device(right_side, mean_flow, jac_basis, pattern, shift_diag, dissipation, donors):
    rows, width = right_side.shape[1:]
    f32 = jnp.float32
    vmem = pl.BlockSpec(memory_space=pltpu.VMEM)

    main, strip = pl.pallas_call(
        pack_kernel,
        out_shape=(
            jax.ShapeDtypeStruct((FEATS, rows * width), f32),
            jax.ShapeDtypeStruct((FEATS, LANES), f32),
        ),
        in_specs=[vmem] * 6,
        out_specs=(vmem, vmem),
    )(right_side, mean_flow, pattern, shift_diag, dissipation, donors)

    halo = lax.ppermute(strip, "nrm", [(0, 1), (1, 0)])
    half = rows * width // 2
    whole = jnp.concatenate([main, halo], 1)
    left1 = shifted(whole, 1)
    left2 = shifted(jnp.concatenate([main[:, half:], halo], 1), 2)
    right1 = shifted(whole, -1)
    right2 = shifted(jnp.concatenate([main[:, :half], halo], 1), -2)

    jac = jac_basis.reshape(4, 5, 2, 5, 2, 5).transpose(1, 2, 3, 0, 4, 5)
    jac = jnp.pad(jac, ((0, 0), (0, 0), (0, 3), (0, 0), (0, 0), (0, 3))).reshape(80, 64)

    out = jax.ShapeDtypeStruct(right_side.shape, f32)
    return pl.pallas_call(
        solve_kernel,
        out_shape=(out, out),
        in_specs=[vmem] * 6,
        out_specs=(vmem, vmem),
        scratch_shapes=[
            pltpu.VMEM((SLOTS, 32, RING), f32),
            pltpu.VMEM((2, SLOTS, 2, 8, RING), f32),
            pltpu.VMEM((SLOTS, 2, 8, RING), f32),
            pltpu.VMEM((8, 2, 8, RING), f32),
            pltpu.VMEM((8, 3, 8, LANES), jnp.int32),
            pltpu.VMEM((80, 192), jnp.bfloat16),
        ],
    )(left2, left1, whole, right1, right2, jac)


def solution(mesh):
    return jax.shard_map(
        on_device,
        mesh=mesh,
        in_specs=(
            P(None, "blk", "nrm"),
            P(None, "blk", "nrm"),
            P(),
            P(None, "blk", "nrm"),
            P("blk", "nrm"),
            P("blk", "nrm"),
            P("blk", None, "nrm"),
        ),
        out_specs=(P(None, "blk", "nrm"), P(None, "blk", "nrm")),
        check_vma=False,
    )
```

time: 156 us -> 49.3 us (0.32)
  the two profiles are of different devices: /device:TPU:512 before, /device:TPU:513 now
where the time goes in v1:
time: 49.3 us; the launch traced here: 49 us
  starting transfers between devices  26.3 us (53%)
  Pallas kernels  8.86 us (18%)
  waiting for transfers between devices  8.81 us (18%)
  local copies, waits for them, and re-layouts  4.28 us (9%)
  between operations  0.75 us (2%)
    ppermute x4, starting transfers between devices, shifted(): lax.ppermute(cells, 'blk', [(i, i + by) for i in range(count) if 0 <= i +...  23.1 us
    ppermute x4, waiting for transfers between devices, shifted(): lax.ppermute(cells, 'blk', [(i, i + by) for i in range(count) if 0 <= i +...  8.41 us
    pallas_call x1, Pallas kernels, on_device(): pl.pallas_call(solve_kernel, out_shape=(out, out), in_specs=[vmem] * 6, o...  7.13 us
    ppermute x1, starting transfers between devices, on_device(): halo = lax.ppermute(strip, 'nrm', [(0, 1), (1, 0)])  3.19 us
    pallas_call x1, Pallas kernels, on_device(): pl.pallas_call(pack_kernel, out_shape=(jax.ShapeDtypeStruct((FEATS, rows...  1.73 us
    unnamed x15, local copies, waits for them, and re-layouts  1.42 us
    slice x1, local copies, waits for them, and re-layouts, on_device(): right2 = shifted(jnp.concatenate([main[:, :half], halo], 1), -2)  0.99 us
  transfers between devices with their start and end apart: 5, of which 2 were waited for; matrix products, arithmetic and copies ran while one was open for 6% of the time, Pallas kernels for 0%

profile of v1, /device:TPU:513, one launch (start us, length us, event | category | flops | bytes accessed | tf_op | source)
XLA Modules:
  0.0 49.0 jit_solution(13719881825430789327)
XLA Ops:
  0.6 1.7 %shard_map.86 = (f32[24,2048]{1,0:T(8,128)}, f32[24,128]{1,0:T(8,128)}) custom-call(f32[10,8,256]{2,1,0:T(8,128)} %rhs.1, f32[5,8,256]{2,1,0:T(8,128)} %flow.1, s32[4,8,256]{2,1,0:T(8,128)} %mask.1, f32[8,256]{1,0:T(8,128)} %shift.1, f32[8,256]{1,0:T(8,128)} %damp.1, s32[1,2,256]{2,1,0:T(2,128)} %donors.1), custom_call_target="tpu_custom_call" | custom-call | tf_op jit(solution)/shard_map/pallas_call | solution.py:225
  2.4 3.2 %collective-permute-start = (f32[24,128]{1,0:T(8,128)}, f32[24,128]{1,0:T(8,128)S(1)}, u32[]{:S(2)}, u32[]{:S(2)}) collective-permute-start(f32[24,128]{1,0:T(8,128)} %get-tuple-element.5), channel_id=1, source_target_pairs={{0,1},{1,0},{2,3},{3,2},{4,5},{5,4},{6,7},{7,6},{8,9},{9,8},{10,11... | collective-permute-start | bytes 36872 | tf_op jit(solution)/shard_map/ppermute | solution.py:235
  5.6 0.0 copy-start.1
  5.6 1.0 %fusion = (f32[24,1024]{1,0:T(8,128)S(1)}, f32[24,1024]{1,0:T(8,128)S(1)}) fusion(f32[24,2048]{1,0:T(8,128)} %get-tuple-element.4), kind=kLoop, calls=%fused_computation.4 | loop fusion | bytes 393216 | tf_op jit(solution)/shard_map/slice | solution.py:241
  6.6 0.0 copy-done.1
  6.6 0.4 collective-permute-done
  7.0 0.0 copy-start
  7.0 3.7 %collective-permute-start.3 = (f32[24,2176]{1,0:T(8,128)S(1)}, f32[24,2176]{1,0:T(8,128)S(1)}, u32[]{:S(2)}, u32[]{:S(2)}) collective-permute-start(f32[24,2176]{1,0:T(8,128)S(1)} %constant_dynamic-update-slice_fusion.own), channel_id=1, source_target_pairs={{2,0},{4,2},{6,4},{8,6},{10,8},{12,10},{14,12},{16,14},{18,16},{20... | collective-permute-start | bytes 626696 | tf_op jit(solution)/shard_map/ppermute | solution.py:217
  10.7 4.1 %collective-permute-start.2 = (f32[24,2176]{1,0:T(8,128)S(1)}, f32[24,2176]{1,0:T(8,128)S(1)}, u32[]{:S(2)}, u32[]{:S(2)}) collective-permute-start(f32[24,2176]{1,0:T(8,128)S(1)} %constant_dynamic-update-slice_fusion.own), channel_id=1, source_target_pairs={{0,2},{2,4},{4,6},{6,8},{8,10},{10,12},{12,14},{14,16},{16,18},{18... | collective-permute-start | bytes 626696 | tf_op jit(solution)/shard_map/ppermute | solution.py:217
  14.9 0.0 copy-start.6
  14.9 0.0 copy-done
  14.9 13.3 %collective-permute-start.4 = (f32[24,1152]{1,0:T(8,128)S(1)}, f32[24,1152]{1,0:T(8,128)S(1)}, u32[]{:S(2)}, u32[]{:S(2)}) collective-permute-start(f32[24,1152]{1,0:T(8,128)S(1)} %get-tuple-element.8), channel_id=1, source_target_pairs={{4,0},{6,2},{8,4},{10,6},{12,8},{14,10},{16,12},{18,14},{20,16},{2... | collective-permute-start | bytes 331784 | tf_op jit(solution)/shard_map/ppermute | solution.py:217
  28.2 1.9 %collective-permute-start.1 = (f32[24,1152]{1,0:T(8,128)S(1)}, f32[24,1152]{1,0:T(8,128)S(1)}, u32[]{:S(2)}, u32[]{:S(2)}) collective-permute-start(f32[24,1152]{1,0:T(8,128)S(1)} %get-tuple-element.9), channel_id=1, source_target_pairs={{0,4},{2,6},{4,8},{6,10},{8,12},{10,14},{12,16},{14,18},{16,20},{1... | collective-permute-start | bytes 331784 | tf_op jit(solution)/shard_map/ppermute | solution.py:217
  30.2 0.0 copy-done.6
  30.2 0.2 reshape.10
  30.3 0.6 %copy.9 = f32[4,5,2,5,2,5]{3,2,1,5,4,0:T(2,128)S(1)} copy(f32[4,5,2,5,2,5]{5,4,0,3,2,1:T(2,128)S(1)} %reshape.10) | data formatting | bytes 16000 | tf_op jit(solution)/shard_map/reshape | solution.py:243
  31.0 0.1 pad.4
  31.1 0.2 reshape.11
  31.3 0.7 %copy.10.jac = f32[80,64]{1,0:T(8,128)} copy(f32[80,64]{0,1:T(8,128)S(1)} %reshape.11) | data formatting | bytes 40960 | tf_op jit(solution)/shard_map/reshape | solution.py:244
  32.0 0.0 collective-permute-done.4.right2
  32.0 0.0 copy-start.4
  32.1 8.4 %collective-permute-done.1.left2 = f32[24,1152]{1,0:T(8,128)S(1)} collective-permute-done((f32[24,1152]{1,0:T(8,128)S(1)}, f32[24,1152]{1,0:T(8,128)S(1)}, u32[]{:S(2)}, u32[]{:S(2)}) %collective-permute-start.1) | collective-permute-done | bytes 110624 | tf_op jit(solution)/shard_map/ppermute | solution.py:217
  40.5 0.0 copy-start.5
  40.5 0.0 collective-permute-done.3.right1
  40.5 0.0 copy-start.2
  40.5 0.0 collective-permute-done.2.left1
  40.5 0.0 copy-done.4
  40.5 0.6 %copy-done.5 = f32[24,1152]{1,0:T(8,128)} copy-done((f32[24,1152]{1,0:T(8,128)}, f32[24,1152]{1,0:T(8,128)S(1)}, u32[]{:S(2)}) %copy-start.5) | copy-done | bytes 110616
  41.1 0.1 copy-done.2
  41.2 0.0 copy-start.3
  41.2 0.7 %copy-done.3 = f32[24,2176]{1,0:T(8,128)} copy-done((f32[24,2176]{1,0:T(8,128)}, f32[24,2176]{1,0:T(8,128)S(1)}, u32[]{:S(2)}) %copy-start.3) | copy-done | bytes 208920
  41.9 7.1 %shard_map.87 = (f32[10,8,256]{2,1,0:T(8,128)}, f32[10,8,256]{2,1,0:T(8,128)}) custom-call(f32[24,1152]{1,0:T(8,128)} %copy-done.5, f32[24,2176]{1,0:T(8,128)} %copy-done.3, f32[24,2176]{1,0:T(8,128)} %copy-done, f32[24,2176]{1,0:T(8,128)} %copy-done.2, f32[24,1152]{1,0:T(8,128)} %copy-done.4, f32[80,64]{1,0:T(8,128)} %copy.10.jac), custom_call_target="tpu_custom_call" | custom-call | tf_op jit(solution)/shard_map/pallas_call | solution.py:247
  (3 shorter events, 0.0 us)
Async XLA Ops:
  2.4 4.6 %collective-permute-start = (f32[24,128]{1,0:T(8,128)}, f32[24,128]{1,0:T(8,128)S(1)}, u32[]{:S(2)}, u32[]{:S(2)}) collective-permute-start(f32[24,128]{1,0:T(8,128)} %get-tuple-element.5), channel_id=1, source_target_pairs={{0,1},{1,0},{2,3},{3,2},{4,5},{5,4},{6,7},{7,6},{8,9},{9,8},{10,11... | collective-permute-start | bytes 36872 | tf_op jit(solution)/shard_map/ppermute | solution.py:235
  5.6 1.0 %copy-start.1 = (f32[24,2048]{1,0:T(8,128)S(1)}, f32[24,2048]{1,0:T(8,128)}, u32[]{:S(2)}) copy-start(f32[24,2048]{1,0:T(8,128)} %get-tuple-element.4) | copy-start | bytes 589828
  7.0 7.9 %copy-start = (f32[24,2176]{1,0:T(8,128)}, f32[24,2176]{1,0:T(8,128)S(1)}, u32[]{:S(2)}) copy-start(f32[24,2176]{1,0:T(8,128)S(1)} %constant_dynamic-update-slice_fusion.own) | copy-start | bytes 626692
  7.0 33.5 %collective-permute-start.3 = (f32[24,2176]{1,0:T(8,128)S(1)}, f32[24,2176]{1,0:T(8,128)S(1)}, u32[]{:S(2)}, u32[]{:S(2)}) collective-permute-start(f32[24,2176]{1,0:T(8,128)S(1)} %constant_dynamic-update-slice_fusion.own), channel_id=1, source_target_pairs={{2,0},{4,2},{6,4},{8,6},{10,8},{12,10},{14,12},{16,14},{18,16},{20... | collective-permute-start | bytes 626696 | tf_op jit(solution)/shard_map/ppermute | solution.py:217
  10.7 29.7 %collective-permute-start.2 = (f32[24,2176]{1,0:T(8,128)S(1)}, f32[24,2176]{1,0:T(8,128)S(1)}, u32[]{:S(2)}, u32[]{:S(2)}) collective-permute-start(f32[24,2176]{1,0:T(8,128)S(1)} %constant_dynamic-update-slice_fusion.own), channel_id=1, source_target_pairs={{0,2},{2,4},{4,6},{6,8},{8,10},{10,12},{12,14},{14,16},{16,18},{18... | collective-permute-start | bytes 626696 | tf_op jit(solution)/shard_map/ppermute | solution.py:217
  14.9 15.3 %copy-start.6 = (f32[4,5,10,10]{3,0,2,1:T(4,128)S(1)}, f32[4,5,10,10]{3,0,2,1:T(4,128)}, u32[]{:S(2)}) copy-start(f32[4,5,10,10]{3,0,2,1:T(4,128)} %param.9) | copy-start | bytes 24004
  14.9 17.1 %collective-permute-start.4 = (f32[24,1152]{1,0:T(8,128)S(1)}, f32[24,1152]{1,0:T(8,128)S(1)}, u32[]{:S(2)}, u32[]{:S(2)}) collective-permute-start(f32[24,1152]{1,0:T(8,128)S(1)} %get-tuple-element.8), channel_id=1, source_target_pairs={{4,0},{6,2},{8,4},{10,6},{12,8},{14,10},{16,12},{18,14},{20,16},{2... | collective-permute-start | bytes 331784 | tf_op jit(solution)/shard_map/ppermute | solution.py:217
  28.2 12.2 %collective-permute-start.1 = (f32[24,1152]{1,0:T(8,128)S(1)}, f32[24,1152]{1,0:T(8,128)S(1)}, u32[]{:S(2)}, u32[]{:S(2)}) collective-permute-start(f32[24,1152]{1,0:T(8,128)S(1)} %get-tuple-element.9), channel_id=1, source_target_pairs={{0,4},{2,6},{4,8},{6,10},{8,12},{10,14},{12,16},{14,18},{16,20},{1... | collective-permute-start | bytes 331784 | tf_op jit(solution)/shard_map/ppermute | solution.py:217
  32.0 8.4 %copy-start.4 = (f32[24,1152]{1,0:T(8,128)}, f32[24,1152]{1,0:T(8,128)S(1)}, u32[]{:S(2)}) copy-start(f32[24,1152]{1,0:T(8,128)S(1)} %collective-permute-done.4.right2) | copy-start | bytes 331780
  40.5 0.6 %copy-start.5 = (f32[24,1152]{1,0:T(8,128)}, f32[24,1152]{1,0:T(8,128)S(1)}, u32[]{:S(2)}) copy-start(f32[24,1152]{1,0:T(8,128)S(1)} %collective-permute-done.1.left2) | copy-start | bytes 331780
  40.5 0.7 %copy-start.2 = (f32[24,2176]{1,0:T(8,128)}, f32[24,2176]{1,0:T(8,128)S(1)}, u32[]{:S(2)}) copy-start(f32[24,2176]{1,0:T(8,128)S(1)} %collective-permute-done.3.right1) | copy-start | bytes 626692
  41.2 0.7 %copy-start.3 = (f32[24,2176]{1,0:T(8,128)}, f32[24,2176]{1,0:T(8,128)S(1)}, u32[]{:S(2)}) copy-start(f32[24,2176]{1,0:T(8,128)S(1)} %collective-permute-done.2.left1) | copy-start | bytes 626692

commit v2 on v0

v2 whole, which is shorter than its diff:
```python
import jax
import jax.numpy as jnp
from jax import lax
from jax.experimental import pallas as pl
from jax.experimental.pallas import tpu as pltpu
from jax.sharding import PartitionSpec as P


ITERS = 6
OMEGA = 0.3
DELTA = 0.9

SHIFT, DAMP, DON0, DON1 = 5, 6, 7, 13
MASK = (14, 15, 21, 22)
FLOW = 16
FEATS = 24
HALO = 16
LANES = 128
WIDTH = 256

BLOCKS = ((0, 4, 4), (8, 8, 0), (20, 8, 0), (32, 8, 0), (44, 4, 0))
FIRST = (0, 4, 12, 20, 28)
SLOTS = 48
OWN = 2
RANGES = (
    ((0, 2, 1), (1, 0, 4), (2, 0, 4), (3, 0, 4), (4, 0, 1)),
    ((1, 0, 4), (2, 0, 4), (3, 0, 4)),
    ((1, 2, 3), (2, 0, 4), (3, 0, 3)),
    ((1, 4, 2), (2, 0, 4), (3, 0, 2)),
    ((1, 6, 1), (2, 0, 4), (3, 0, 1)),
    ((2, 0, 4),),
)
STRIPS = ((0, 1, 2, 3, 4), (1, 2, 3), (1, 2, 3), (1, 2, 3), (1, 2, 3), ())
LISTS = ((0, 3, DON1), (1, 0, DON0), (1, 0, DON1), (2, 0, DON0), (2, 0, DON1), (3, 0, DON0), (3, 0, DON1), (4, 0, DON0))
FILLS = (
    (4, 8, 0), (6, 2, 1), (16, 20, 2), (18, 14, 3),
    (28, 32, 4), (30, 26, 5), (40, 44, 6), (42, 38, 7),
)
FILLS_AT = (range(8), (1, 2, 3, 4, 5, 6), (2, 3, 4, 5), (2, 3, 4, 5), (2, 3, 4, 5), (3, 4))


def chebyshev():
    sigma = 1.0 / DELTA
    rho = DELTA
    steps = []
    for _ in range(ITERS - 1):
        rho_new = 1.0 / (2.0 * sigma - rho)
        steps.append((rho_new * rho, 2.0 * rho_new / DELTA))
        rho = rho_new
    return steps


def split(full):
    high = full.astype(jnp.bfloat16)
    return high, (full - high.astype(jnp.float32)).astype(jnp.bfloat16)


def precond(pa, pb, a, b):
    return pa * a + pb * b, pa * b - pb * a


def lanes(rows):
    return lax.broadcasted_iota(jnp.int32, (rows, LANES), 1)


def pack_kernel(rhs, flow, mask, shift, damp, donors, whole, lower, upper):
    nrm = lax.axis_index("nrm")
    count, width = rhs.shape[1:]
    here = lax.broadcasted_iota(jnp.int32, (1, width), 1) + nrm * width
    offsets = (donors[0] - here).astype(jnp.float32)
    half = count * width // 2
    for i in range(count):
        side = lower if i < count // 2 else upper
        start = i * width % half
        for out, at in ((whole, slice(i * width, (i + 1) * width)), (side, slice(start, start + width))):
            out[0:5, at] = rhs[0:5, i, :]
            out[SHIFT : SHIFT + 1, at] = shift[i : i + 1, :]
            out[DAMP : DAMP + 1, at] = damp[i : i + 1, :]
            out[DON0 : DON0 + 1, at] = offsets[0:1]
            out[8:13, at] = rhs[5:10, i, :]
            out[DON1 : DON1 + 1, at] = offsets[1:2]
            out[14:16, at] = mask[0:2, i, :].astype(jnp.float32)
            out[16:21, at] = flow[:, i, :]
            out[21:23, at] = mask[2:4, i, :].astype(jnp.float32)
            out[23:24, at] = jnp.zeros((1, width), jnp.float32)


def basis_kernel(jac, basis, full):
    full[...] = jnp.zeros(full.shape, jnp.float32)
    for f in range(4):
        for m in range(5):
            for h in range(2):
                for g in range(2):
                    block = jac[m, 5 * h : 5 * h + 5, f, 5 * g : 5 * g + 5]
                    full[16 * m + 8 * h : 16 * m + 8 * h + 5, 16 * f + 8 * g : 16 * f + 8 * g + 5] = block
    high, low = split(full[...])
    basis[:, 0:64] = high
    basis[:, 64:128] = high
    basis[:, 128:192] = low


def strip_kernel(*refs):
    nrm = lax.axis_index("nrm")
    strip = refs[-1]
    lane = lanes(FEATS)
    for b, (ref, (_, held, first)) in enumerate(zip(refs[:-1], BLOCKS, strict=True)):
        sent = jnp.zeros((FEATS, LANES), jnp.float32)
        for c in range(held):
            at = pl.ds(pl.multiple_of(c * WIDTH + (1 - nrm) * LANES, LANES), LANES)
            col = first + c
            edge = pltpu.roll(ref[:, at], lax.rem(HALO * (col + 1 - nrm), LANES), 1)
            sent = jnp.where((lane >= HALO * col) & (lane < HALO * (col + 1)), edge, sent)
        strip[:, b * LANES : (b + 1) * LANES] = sent


def ghosts(src_d, dst_d, dst_h, index, n):
    dst, src, which = FILLS[n]
    lane = lanes(8)
    for c in range(2):
        for t in range(2):
            at = index[which, t]
            across = jnp.abs(at - lane) > LANES // 2
            picked = []
            for h in range(2):
                tiles = [src_d[src + c, h, :, u * LANES : (u + 1) * LANES] for u in (t, 1 - t)]
                here, there = (jnp.take_along_axis(x, at, axis=1) for x in tiles)
                picked.append(jnp.where(across, there, here))
                dst_d[dst + c, h, :, t * LANES : (t + 1) * LANES] = picked[h]
            high, low = split(jnp.concatenate(picked, 0))
            dst_h[dst + c, 0, :, t * LANES : (t + 1) * LANES] = high
            dst_h[dst + c, 1, :, t * LANES : (t + 1) * LANES] = low


def prep_kernel(left2, left1, own, right1, right2, coef, masks, res, dirs, parts, index):
    nrm = lax.axis_index("nrm")
    refs = (left2, left1, own, right1, right2)
    row = lax.broadcasted_iota(jnp.int32, (8, WIDTH), 0)
    lane = lax.broadcasted_iota(jnp.int32, (16, WIDTH), 1)
    wall = ((lane == 0) & (nrm == 0), (lane == WIDTH - 1) & (nrm == 1))
    for ref, (slot, held, _), first in zip(refs, BLOCKS, FIRST, strict=True):
        for c in range(held):
            q, s = first + c, slot + c
            at = slice(c * WIDTH, (c + 1) * WIDTH)
            shift = ref[SHIFT : SHIFT + 1, at]
            scale = 1.0 / (shift * shift + OMEGA * OMEGA)
            pa, pb = shift * scale, OMEGA * scale
            coef[q, 0:1] = shift
            coef[q, 1:2] = ref[DAMP : DAMP + 1, at]
            coef[q, 2:3] = pa
            coef[q, 3:4] = pb
            coef[q, 8:16] = ref[FLOW : FLOW + 8, at]
            for face in range(4):
                m = jnp.broadcast_to(ref[MASK[face] : MASK[face] + 1, at], (16, WIDTH))
                if face >= 2:
                    m = jnp.where(wall[face - 2], 0.0, m)
                masks[q, face] = m.astype(jnp.bfloat16)
            a = jnp.where(row < 5, ref[0:8, at], 0.0)
            b = jnp.where(row < 5, ref[8:16, at], 0.0)
            res[q, 0] = a
            res[q, 1] = b
            da, db = precond(pa, pb, a, b)
            dirs[s, 0] = da
            dirs[s, 1] = db
            high, low = split(jnp.concatenate([da, db], 0))
            parts[s, 0] = high
            parts[s, 1] = low
    for n, (b, c, r) in enumerate(LISTS):
        for t in range(2):
            start = c * WIDTH + t * LANES
            offset = refs[b][r : r + 1, start : start + LANES].astype(jnp.int32)
            index[n, t] = jnp.bitwise_and(lanes(8) + offset, LANES - 1)
    for n in FILLS_AT[0]:
        ghosts(dirs, dirs, parts, index, n)


def solve_kernel(
    coef, masks, res0, dirs0, parts0, index, halo, basis, sol_out, res_out,
    dirs, parts, res, sol, sdirs, sparts, sres, spre,
):
    nrm = lax.axis_index("nrm")
    lane = lanes(8)
    lane16 = lanes(16)
    group = jnp.bitwise_and(lane, HALO - 1)
    low_rows = lax.broadcasted_iota(jnp.int32, (8, LANES), 0) < 5
    steps = chebyshev()

    def dirs_at(step):
        return dirs0 if step == 0 else dirs.at[step % 2]

    def parts_at(step):
        return parts0 if step == 0 else parts.at[step % 2]

    def store_strip(par, b, values):
        for h in range(2):
            sdirs[par, b, h] = values[h]
        high, low = split(jnp.concatenate(values, 0))
        sparts[par, b, 0] = high
        sparts[par, b, 1] = low

    for b in range(5):
        at = slice(b * LANES, (b + 1) * LANES)
        shift = halo[SHIFT : SHIFT + 1, at]
        scale = 1.0 / (shift * shift + OMEGA * OMEGA)
        spre[b, 0:1] = shift * scale
        spre[b, 1:2] = OMEGA * scale
        x = [jnp.where(low_rows, halo[8 * h : 8 * h + 8, at], 0.0) for h in range(2)]
        for h in range(2):
            sres[b, h] = x[h]
        store_strip(0, b, list(precond(shift * scale, OMEGA * scale, *x)))

    def apply(d, far, y, shift, damp, flow):
        out = [shift * d[0] - OMEGA * d[1], shift * d[1] + OMEGA * d[0]]
        for h in range(2):
            out[h] = out[h] + damp * far[h]
        for m in range(5):
            f = flow(m)
            for h in range(2):
                out[h] = out[h] + f * y[16 * m + 8 * h : 16 * m + 8 * h + 8]
        return out

    def strips(step):
        par = step % 2
        source = dirs_at(step)
        for b in STRIPS[step]:
            slot, held, first = BLOCKS[b]
            at = slice(b * LANES, (b + 1) * LANES)
            before = halo[DON0 : DON0 + 1, at].astype(jnp.int32) + lane
            after = halo[DON1 : DON1 + 1, at].astype(jnp.int32) + lane
            rows, far, mid = [[], [], [], []], [], []
            for h in range(2):
                d = sdirs[par, b, h]
                edge = jnp.zeros((8, LANES), jnp.float32)
                for c in range(held):
                    col = first + c
                    tile = source[slot + c, h, :, pl.ds(pl.multiple_of((1 - nrm) * LANES, LANES), LANES)]
                    tile = pltpu.roll(tile, HALO * col + 1 + 14 * nrm, 1)
                    edge = jnp.where((lane >= HALO * col) & (lane < HALO * (col + 1)), tile, edge)
                west, west2 = pltpu.roll(d, HALO, 1), pltpu.roll(d, 2 * HALO, 1)
                east, east2 = pltpu.roll(d, LANES - HALO, 1), pltpu.roll(d, LANES - 2 * HALO, 1)
                if b > 0:
                    other = sdirs[par, b - 1, h]
                    near = jnp.take_along_axis(other, jnp.bitwise_and(before + 7 * HALO, LANES - 1), axis=1)
                    next2 = jnp.take_along_axis(other, jnp.bitwise_and(before + 6 * HALO, LANES - 1), axis=1)
                    west = jnp.where(lane < HALO, near, west)
                    west2 = jnp.where(lane < 2 * HALO, next2, west2)
                if b < 4:
                    other = sdirs[par, b + 1, h]
                    near = jnp.take_along_axis(other, jnp.bitwise_and(after + HALO, LANES - 1), axis=1)
                    next2 = jnp.take_along_axis(other, jnp.bitwise_and(after + 2 * HALO, LANES - 1), axis=1)
                    east = jnp.where(lane >= 7 * HALO, near, east)
                    east2 = jnp.where(lane >= 6 * HALO, next2, east2)
                south = jnp.where(group == 0, edge, pltpu.roll(d, 1, 1))
                north = jnp.where(group == HALO - 1, edge, pltpu.roll(d, LANES - 1, 1))
                for face, value in enumerate((west, east, south, north)):
                    rows[face].append(halo[MASK[face] : MASK[face] + 1, at] * value)
                far.append(west2 + east2)
                mid.append(d)
            high, low = split(jnp.concatenate(sum(rows, []), 0))
            y = jnp.dot(basis[...], jnp.concatenate([high, low, high], 0), preferred_element_type=jnp.float32)
            out = apply(
                mid, far, y, halo[SHIFT : SHIFT + 1, at], halo[DAMP : DAMP + 1, at],
                lambda m, at=at: halo[FLOW + m : FLOW + m + 1, at],
            )
            new = [sres[b, h] - out[h] for h in range(2)]
            for h in range(2):
                sres[b, h] = new[h]
            keep, gain = steps[step]
            turned = precond(spre[b, 0:1], spre[b, 1:2], *new)
            store_strip(1 - par, b, [keep * mid[h] + gain * turned[h] for h in range(2)])

    def column(step, b, c):
        slot, _, first = BLOCKS[b]
        s, q = slot + c, FIRST[b] + c
        par = step % 2
        p = parts_at(step)
        turn = 127 - 14 * nrm - HALO * (first + c)
        stack = [[], []]
        for k in range(2):
            tiles = [p[s, k, :, t * LANES : (t + 1) * LANES] for t in range(2)]
            edge = pltpu.roll(sparts[par, b, k], turn, 1)
            up = [pltpu.roll(x, 1, 1) for x in tiles]
            down = [pltpu.roll(x, LANES - 1, 1) for x in tiles]
            south = [jnp.where(lane16 == 0, edge, up[0]), jnp.where(lane16 == 0, up[0], up[1])]
            north = [jnp.where(lane16 == LANES - 1, down[1], down[0]), jnp.where(lane16 == LANES - 1, edge, down[1])]
            for face, value in enumerate(
                (p[s - 1, k], p[s + 1, k], jnp.concatenate(south, 1), jnp.concatenate(north, 1))
            ):
                stack[k].append(masks[q, face] * value)
        return jnp.concatenate(stack[0] + stack[1] + stack[0], 0)

    def finish(step, b, c, y):
        s, q = BLOCKS[b][0] + c, FIRST[b] + c
        d = dirs_at(step)
        mid = [d[s, h] for h in range(2)]
        far = [d[s - 2, h] + d[s + 2, h] for h in range(2)]
        out = apply(mid, far, y, coef[q, 0:1], coef[q, 1:2], lambda m: coef[q, 8 + m : 9 + m])
        old = res0 if step == 0 else res
        new = [old[q, h] - out[h] for h in range(2)]
        for h in range(2):
            res[q, h] = new[h]
            if b == OWN:
                sol[c, h] = mid[h] if step == 0 else sol[c, h] + mid[h]
        if step + 1 < ITERS:
            keep, gain = steps[step]
            turned = precond(coef[q, 2:3], coef[q, 3:4], *new)
            made = [keep * mid[h] + gain * turned[h] for h in range(2)]
            par = 1 - step % 2
            for h in range(2):
                dirs[par, s, h] = made[h]
            high, low = split(jnp.concatenate(made, 0))
            parts[par, s, 0] = high
            parts[par, s, 1] = low

    for step in range(ITERS):
        if step:
            par = step % 2
            for n in FILLS_AT[step]:
                ghosts(dirs.at[par], dirs.at[par], parts.at[par], index, n)
        strips(step)
        for b, start, pairs in RANGES[step]:

            def body(p, carry, step=step, b=b, start=start):
                for k in range(2):
                    c = start + 2 * p + k
                    y = jnp.dot(basis[...], column(step, b, c), preferred_element_type=jnp.float32)
                    finish(step, b, c, y)
                return carry

            lax.fori_loop(0, pairs, body, 0, unroll=UNROLL)

    for i in range(8):
        for h in range(2):
            sol_out[5 * h : 5 * h + 5, i, :] = sol[i, h, 0:5]
            res_out[5 * h : 5 * h + 5, i, :] = res[FIRST[OWN] + i, h, 0:5]


UNROLL = True


def shifted(cells, by):
    count = lax.axis_size("blk")
    return lax.ppermute(cells, "blk", [(i, i + by) for i in range(count) if 0 <= i + by < count])


def local(kernel, outs, scratch, *args, limit=16 << 20):
    vmem = pl.BlockSpec(memory_space=pltpu.VMEM)
    return pl.pallas_call(
        kernel,
        out_shape=outs,
        in_specs=[vmem] * len(args),
        out_specs=jax.tree.map(lambda _: vmem, outs),
        scratch_shapes=scratch,
        compiler_params=pltpu.CompilerParams(vmem_limit_bytes=limit),
    )(*args)


def inside(x):
    return pltpu.with_memory_space_constraint(x, pltpu.VMEM)


def step(right_side, mean_flow, jac_basis, pattern, shift_diag, dissipation, donors):
    rows, width = right_side.shape[1:]
    f32, bf16 = jnp.float32, jnp.bfloat16
    vmem = pltpu.VMEM
    half = rows * width // 2

    whole, lower, upper = local(
        pack_kernel,
        (vmem((FEATS, 2 * half), f32), vmem((FEATS, half), f32), vmem((FEATS, half), f32)),
        [],
        right_side, mean_flow, pattern, shift_diag, dissipation, donors,
        limit=None,
    )
    left1 = shifted(whole, 1)
    left2 = shifted(upper, 2)
    right1 = shifted(whole, -1)
    right2 = shifted(lower, -2)
    basis = local(
        basis_kernel, vmem((80, 192), bf16), [vmem((80, 64), f32)], jac_basis.transpose(1, 2, 0, 3)
    )

    cells = [inside(x) for x in (left2, left1, whole, right1, right2)]
    strip = local(strip_kernel, vmem((FEATS, 5 * LANES), f32), [], *cells)
    halo = lax.ppermute(strip, "nrm", [(0, 1), (1, 0)])
    ready = local(
        prep_kernel,
        (
            vmem((32, 16, WIDTH), f32),
            vmem((32, 4, 16, WIDTH), bf16),
            vmem((32, 2, 8, WIDTH), f32),
            vmem((SLOTS, 2, 8, WIDTH), f32),
            vmem((SLOTS, 2, 16, WIDTH), bf16),
            vmem((8, 2, 8, LANES), jnp.int32),
        ),
        [],
        *cells,
    )

    out = jax.ShapeDtypeStruct(right_side.shape, f32)
    scratch = [
        vmem((2, SLOTS, 2, 8, WIDTH), f32),
        vmem((2, SLOTS, 2, 16, WIDTH), bf16),
        vmem((32, 2, 8, WIDTH), f32),
        vmem((8, 2, 8, WIDTH), f32),
        vmem((2, 5, 2, 8, LANES), f32),
        vmem((2, 5, 2, 16, LANES), bf16),
        vmem((5, 2, 8, LANES), f32),
        vmem((5, 8, LANES), f32),
    ]
    return local(
        solve_kernel, (out, out), scratch, *[inside(x) for x in ready], inside(halo), inside(basis)
    )


def solution(mesh):
    return jax.shard_map(
        step,
        mesh=mesh,
        in_specs=(
            P(None, "blk", "nrm"),
            P(None, "blk", "nrm"),
            P(),
            P(None, "blk", "nrm"),
            P("blk", "nrm"),
            P("blk", "nrm"),
            P("blk", None, "nrm"),
        ),
        out_specs=(P(None, "blk", "nrm"), P(None, "blk", "nrm")),
        check_vma=False,
    )
```

time: 156 us -> 43.8 us (0.28)
  the two profiles are of different devices: /device:TPU:512 before, /device:TPU:254 now
where the time goes in v2:
time: 43.8 us; the launch traced here: 43.5 us
  starting transfers between devices  21.9 us (50%)
  waiting for transfers between devices  14.1 us (32%)
  Pallas kernels  6.84 us (16%)
  between operations  0.71 us (2%)
    ppermute x4, starting transfers between devices, shifted(): lax.ppermute(cells, 'blk', [(i, i + by) for i in range(count) if 0 <= i +...  19.6 us
    ppermute x4, waiting for transfers between devices, shifted(): lax.ppermute(cells, 'blk', [(i, i + by) for i in range(count) if 0 <= i +...  11 us
    pallas_call x5, Pallas kernels, local(): pl.pallas_call(kernel, out_shape=outs, in_specs=[vmem] * len(args), out_s...  6.84 us
    ppermute x1, waiting for transfers between devices, step(): halo = lax.ppermute(strip, 'nrm', [(0, 1), (1, 0)])  3.1 us
    ppermute x1, starting transfers between devices, step(): halo = lax.ppermute(strip, 'nrm', [(0, 1), (1, 0)])  2.36 us
  transfers between devices with their start and end apart: 5, of which 3 were waited for; matrix products, arithmetic and copies ran while one was open for 0% of the time, Pallas kernels for 1%

profile of v2, /device:TPU:254, one launch (start us, length us, event | category | flops | bytes accessed | tf_op | source)
XLA Modules:
  0.0 43.5 jit_solution(6460176197882688869)
XLA Ops:
  0.6 1.0 %shard_map.86 = (f32[24,2048]{1,0:T(8,128)S(1)}, f32[24,1024]{1,0:T(8,128)S(1)}, f32[24,1024]{1,0:T(8,128)S(1)}) custom-call(f32[10,8,256]{2,1,0:T(8,128)} %rhs.1, f32[5,8,256]{2,1,0:T(8,128)} %flow.1, s32[4,8,256]{2,1,0:T(8,128)} %mask.1, f32[8,256]{1,0:T(8,128)} %shift.1, f32[8,256]{1,0:T(8,128)} %damp.1, s32[1,2,256]{2,1,0:T(2,128)} %donors.1), custom_call_target="tpu_custom_call" | custom-call | tf_op jit(solution)/shard_map/pallas_call | solution.py:347
  1.7 1.9 %collective-permute-start.1 = (f32[24,2048]{1,0:T(8,128)S(1)}, f32[24,2048]{1,0:T(8,128)S(1)}, u32[]{:S(2)}, u32[]{:S(2)}) collective-permute-start(f32[24,2048]{1,0:T(8,128)S(1)} %get-tuple-element.12.own.refs_2_), channel_id=1, source_target_pairs={{0,2},{2,4},{4,6},{6,8},{8,10},{10,12},{12,14},{14,16},{16,18},{18... | collective-permute-start | bytes 589832 | tf_op jit(solution)/shard_map/ppermute | solution.py:342
  3.6 4.5 %collective-permute-start.2 = (f32[24,2048]{1,0:T(8,128)S(1)}, f32[24,2048]{1,0:T(8,128)S(1)}, u32[]{:S(2)}, u32[]{:S(2)}) collective-permute-start(f32[24,2048]{1,0:T(8,128)S(1)} %get-tuple-element.12.own.refs_2_), channel_id=1, source_target_pairs={{2,0},{4,2},{6,4},{8,6},{10,8},{12,10},{14,12},{16,14},{18,16},{20... | collective-permute-start | bytes 589832 | tf_op jit(solution)/shard_map/ppermute | solution.py:342
  8.2 11.1 %collective-permute-start = (f32[24,1024]{1,0:T(8,128)S(1)}, f32[24,1024]{1,0:T(8,128)S(1)}, u32[]{:S(2)}, u32[]{:S(2)}) collective-permute-start(f32[24,1024]{1,0:T(8,128)S(1)} %get-tuple-element.11), channel_id=1, source_target_pairs={{0,4},{2,6},{4,8},{6,10},{8,12},{10,14},{12,16},{14,18},{16,20},{1... | collective-permute-start | bytes 294920 | tf_op jit(solution)/shard_map/ppermute | solution.py:342
  19.2 0.0 copy-start
  19.2 2.1 %collective-permute-start.3 = (f32[24,1024]{1,0:T(8,128)S(1)}, f32[24,1024]{1,0:T(8,128)S(1)}, u32[]{:S(2)}, u32[]{:S(2)}) collective-permute-start(f32[24,1024]{1,0:T(8,128)S(1)} %get-tuple-element.13), channel_id=1, source_target_pairs={{4,0},{6,2},{8,4},{10,6},{12,8},{14,10},{16,12},{18,14},{20,16},{2... | collective-permute-start | bytes 294920 | tf_op jit(solution)/shard_map/ppermute | solution.py:342
  21.3 0.1 collective-permute-done.left2.refs_0_
  21.4 10.8 %collective-permute-done.3.right2.refs_4_ = f32[24,1024]{1,0:T(8,128)S(1)} collective-permute-done((f32[24,1024]{1,0:T(8,128)S(1)}, f32[24,1024]{1,0:T(8,128)S(1)}, u32[]{:S(2)}, u32[]{:S(2)}) %collective-permute-start.3) | collective-permute-done | bytes 98336 | tf_op jit(solution)/shard_map/ppermute | solution.py:342
  32.2 0.0 collective-permute-done.1.left1.refs_1_
  32.2 0.0 collective-permute-done.2.right1.refs_3_
  32.2 0.2 shard_map.88
  32.4 2.4 %collective-permute-start.4 = (f32[24,640]{1,0:T(8,128)S(1)}, f32[24,640]{1,0:T(8,128)S(1)}, u32[]{:S(2)}, u32[]{:S(2)}) collective-permute-start(f32[24,640]{1,0:T(8,128)S(1)} %shard_map.88), channel_id=1, source_target_pairs={{0,1},{1,0},{2,3},{3,2},{4,5},{5,4},{6,7},{7,6},{8,9},{9,8},{10,11... | collective-permute-start | bytes 184328 | tf_op jit(solution)/shard_map/ppermute | solution.py:384
  34.8 0.0 copy-done
  34.8 0.2 shard_map.89.basis
  35.0 0.4 shard_map.87
  35.4 3.1 %collective-permute-done.4.halo = f32[24,640]{1,0:T(8,128)S(1)} collective-permute-done((f32[24,640]{1,0:T(8,128)S(1)}, f32[24,640]{1,0:T(8,128)S(1)}, u32[]{:S(2)}, u32[]{:S(2)}) %collective-permute-start.4) | collective-permute-done | bytes 61472 | tf_op jit(solution)/shard_map/ppermute | solution.py:384
  38.5 5.0 %shard_map.90 = (f32[10,8,256]{2,1,0:T(8,128)}, f32[10,8,256]{2,1,0:T(8,128)}) custom-call(f32[32,16,256]{2,1,0:T(8,128)S(1)} %get-tuple-element.14.coef, bf16[32,4,16,256]{3,2,1,0:T(8,128)(2,1)S(1)} %get-tuple-element.15.masks, f32[32,2,8,256]{3,2,1,0:T(8,128)S(1)} %get-tuple-element.16.res0, f32[48,2,8,256]{3,2,1,0:T(8,128)S(1)} %get-tuple-element.17.dirs0, ...), custom_call_target="tpu_custom_call" | custom-call | tf_op jit(solution)/shard_map/pallas_call | solution.py:347
Async XLA Ops:
  1.7 30.6 %collective-permute-start.1 = (f32[24,2048]{1,0:T(8,128)S(1)}, f32[24,2048]{1,0:T(8,128)S(1)}, u32[]{:S(2)}, u32[]{:S(2)}) collective-permute-start(f32[24,2048]{1,0:T(8,128)S(1)} %get-tuple-element.12.own.refs_2_), channel_id=1, source_target_pairs={{0,2},{2,4},{4,6},{6,8},{8,10},{10,12},{12,14},{14,16},{16,18},{18... | collective-permute-start | bytes 589832 | tf_op jit(solution)/shard_map/ppermute | solution.py:342
  3.6 28.6 %collective-permute-start.2 = (f32[24,2048]{1,0:T(8,128)S(1)}, f32[24,2048]{1,0:T(8,128)S(1)}, u32[]{:S(2)}, u32[]{:S(2)}) collective-permute-start(f32[24,2048]{1,0:T(8,128)S(1)} %get-tuple-element.12.own.refs_2_), channel_id=1, source_target_pairs={{2,0},{4,2},{6,4},{8,6},{10,8},{12,10},{14,12},{16,14},{18,16},{20... | collective-permute-start | bytes 589832 | tf_op jit(solution)/shard_map/ppermute | solution.py:342
  8.2 13.3 %collective-permute-start = (f32[24,1024]{1,0:T(8,128)S(1)}, f32[24,1024]{1,0:T(8,128)S(1)}, u32[]{:S(2)}, u32[]{:S(2)}) collective-permute-start(f32[24,1024]{1,0:T(8,128)S(1)} %get-tuple-element.11), channel_id=1, source_target_pairs={{0,4},{2,6},{4,8},{6,10},{8,12},{10,14},{12,16},{14,18},{16,20},{1... | collective-permute-start | bytes 294920 | tf_op jit(solution)/shard_map/ppermute | solution.py:342
  19.2 15.6 %copy-start = (f32[4,5,10,10]{3,0,2,1:T(4,128)S(1)}, f32[4,5,10,10]{3,0,2,1:T(4,128)}, u32[]{:S(2)}) copy-start(f32[4,5,10,10]{3,0,2,1:T(4,128)} %param.9) | copy-start | bytes 24004
  19.2 13.0 %collective-permute-start.3 = (f32[24,1024]{1,0:T(8,128)S(1)}, f32[24,1024]{1,0:T(8,128)S(1)}, u32[]{:S(2)}, u32[]{:S(2)}) collective-permute-start(f32[24,1024]{1,0:T(8,128)S(1)} %get-tuple-element.13), channel_id=1, source_target_pairs={{4,0},{6,2},{8,4},{10,6},{12,8},{14,10},{16,12},{18,14},{20,16},{2... | collective-permute-start | bytes 294920 | tf_op jit(solution)/shard_map/ppermute | solution.py:342
  32.4 6.1 %collective-permute-start.4 = (f32[24,640]{1,0:T(8,128)S(1)}, f32[24,640]{1,0:T(8,128)S(1)}, u32[]{:S(2)}, u32[]{:S(2)}) collective-permute-start(f32[24,640]{1,0:T(8,128)S(1)} %shard_map.88), channel_id=1, source_target_pairs={{0,1},{1,0},{2,3},{3,2},{4,5},{5,4},{6,7},{7,6},{8,9},{9,8},{10,11... | collective-permute-start | bytes 184328 | tf_op jit(solution)/shard_map/ppermute | solution.py:384

commit v3 on v2

v3 whole, which is shorter than its diff:
```python
import functools

import jax
import jax.numpy as jnp
from jax import lax
from jax.experimental import pallas as pl
from jax.experimental.pallas import tpu as pltpu
from jax.sharding import PartitionSpec as P


ITERS = 6
OMEGA = 0.3
DELTA = 0.9

SHIFT, DAMP, DON0, DON1 = 5, 6, 7, 13
MASK = (14, 15, 21, 22)
FLOW = 16
FEATS = 24
HALO = 16
LANES = 128
WIDTH = 256

FAR1, OWN, NEAR = 1, 2, 3
BLOCKS = ((0, 4, 4, 4), (8, 8, 0, 8), (20, 8, 0, 8), (32, 6, 0, 8))
FIRST = (0, 4, 12, 20)
COLUMNS = 26
SLOTS = 38
MIDDLE = 3
RANGES = (
    ((0, 2, 1), (1, 0, 4), (2, 0, 4), (3, 0, 2)),
    ((1, 0, 4), (2, 0, 4), (3, 0, 1)),
    ((1, 2, 3), (2, 0, 4)),
    ((1, 4, 2), (2, 0, 4), (3, 0, 2)),
    ((1, 6, 1), (2, 0, 4), (3, 0, 1)),
    ((2, 0, 4),),
)
STRIPS = ((0, 1, 2, 3), (1, 2, 3), (1, 2), (1, 2, 3), (2,), ())
LISTS = ((0, 3, 1), (1, 0, 0), (1, 0, 1), (2, 0, 0), (2, 0, 1), (3, 0, 0))
FILLS = ((4, 8, 0), (6, 2, 1), (16, 20, 2), (18, 14, 3), (28, 32, 4), (30, 26, 5))
FILLS_AT = ((0, 1, 2, 3, 4, 5), (1, 2, 3, 4, 5), (2, 3, 4), (2, 3, 4, 5), (2, 3, 4, 5), (3, 4))
SENT_DIRS, SENT_RES = 6, 4


def chebyshev():
    sigma = 1.0 / DELTA
    rho = DELTA
    steps = []
    for _ in range(ITERS - 1):
        rho_new = 1.0 / (2.0 * sigma - rho)
        steps.append((rho_new * rho, 2.0 * rho_new / DELTA))
        rho = rho_new
    return steps


def split(full):
    high = full.astype(jnp.bfloat16)
    return high, (full - high.astype(jnp.float32)).astype(jnp.bfloat16)


def precond(pa, pb, a, b):
    return pa * a + pb * b, pa * b - pb * a


def lanes(rows):
    return lax.broadcasted_iota(jnp.int32, (rows, LANES), 1)


def mirrored():
    return lax.rem(lax.axis_index("blk"), 2)


def place(b, c, odd):
    _, _, _, sent = BLOCKS[b]
    return c + odd * (sent - 1 - 2 * c)


def pack_kernel(rhs, flow, mask, shift, damp, donors, whole, part):
    nrm = lax.axis_index("nrm")
    count, width = rhs.shape[1:]
    here = lax.broadcasted_iota(jnp.int32, (1, width), 1) + nrm * width
    offsets = (donors[0] - here).astype(jnp.float32)
    for i in range(count):
        at = slice(i * width, (i + 1) * width)
        whole[0:5, at] = rhs[0:5, i, :]
        whole[SHIFT : SHIFT + 1, at] = shift[i : i + 1, :]
        whole[DAMP : DAMP + 1, at] = damp[i : i + 1, :]
        whole[DON0 : DON0 + 1, at] = offsets[0:1]
        whole[8:13, at] = rhs[5:10, i, :]
        whole[DON1 : DON1 + 1, at] = offsets[1:2]
        whole[14:16, at] = mask[0:2, i, :].astype(jnp.float32)
        whole[16:21, at] = flow[:, i, :]
        whole[21:23, at] = mask[2:4, i, :].astype(jnp.float32)
        whole[23:24, at] = jnp.zeros((1, width), jnp.float32)
    half = count * width // 2
    part[...] = whole[:, pl.ds(pl.multiple_of((1 - mirrored()) * half, LANES), half)]


def basis_kernel(jac, basis, full):
    full[...] = jnp.zeros(full.shape, jnp.float32)
    for f in range(4):
        for m in range(5):
            for h in range(2):
                for g in range(2):
                    block = jac[m, 5 * h : 5 * h + 5, f, 5 * g : 5 * g + 5]
                    full[16 * m + 8 * h : 16 * m + 8 * h + 5, 16 * f + 8 * g : 16 * f + 8 * g + 5] = block
    j = full[...]
    lane = lanes(80)
    other = jnp.where(lane < 16, pltpu.roll(j, LANES - 16, 1), pltpu.roll(j, 16, 1))
    j = jnp.where((mirrored() == 1) & (lane < 32), other, j)[:, 0:64]
    high, low = split(j)
    basis[:, 0:64] = high
    basis[:, 64:128] = high
    basis[:, 128:192] = low


def strip_kernel(*refs):
    nrm, odd = lax.axis_index("nrm"), mirrored()
    strip = refs[-1]
    lane = lanes(FEATS)
    for b, ref in enumerate(refs[:-1]):
        first, sent = BLOCKS[b][2:]
        rows = jnp.zeros((FEATS, LANES), jnp.float32)
        for c in range(sent):
            start = place(b, c, odd) * WIDTH + (1 - nrm) * LANES
            col = first + c
            edge = ref[:, pl.ds(pl.multiple_of(start, LANES), LANES)]
            edge = pltpu.roll(edge, lax.rem(HALO * (col + 1 - nrm), LANES), 1)
            rows = jnp.where((lane >= HALO * col) & (lane < HALO * (col + 1)), edge, rows)
        strip[:, b * LANES : (b + 1) * LANES] = rows


def ghosts(src_d, dst_d, dst_h, index, n):
    dst, src, which = FILLS[n]
    lane = lanes(8)
    for c in range(2):
        for t in range(2):
            at = index[which, t]
            across = jnp.abs(at - lane) > LANES // 2
            picked = []
            for h in range(2):
                tiles = [src_d[src + c, h, :, u * LANES : (u + 1) * LANES] for u in (t, 1 - t)]
                here, there = (jnp.take_along_axis(x, at, axis=1) for x in tiles)
                picked.append(jnp.where(across, there, here))
                dst_d[dst + c, h, :, t * LANES : (t + 1) * LANES] = picked[h]
            high, low = split(jnp.concatenate(picked, 0))
            dst_h[dst + c, 0, :, t * LANES : (t + 1) * LANES] = high
            dst_h[dst + c, 1, :, t * LANES : (t + 1) * LANES] = low


def prep_kernel(far2, far1, own, near, coef, masks, res, dirs, parts, index):
    nrm, odd = lax.axis_index("nrm"), mirrored()
    refs = (far2, far1, own, near)
    row = lax.broadcasted_iota(jnp.int32, (8, WIDTH), 0)
    lane = lax.broadcasted_iota(jnp.int32, (16, WIDTH), 1)
    wall = ((lane == 0) & (nrm == 0), (lane == WIDTH - 1) & (nrm == 1))
    for b, ref in enumerate(refs):
        slot, held = BLOCKS[b][:2]
        for c in range(held):
            q, s = FIRST[b] + c, slot + c
            at = pl.ds(pl.multiple_of(place(b, c, odd) * WIDTH, WIDTH), WIDTH)
            shift = ref[SHIFT : SHIFT + 1, at]
            scale = 1.0 / (shift * shift + OMEGA * OMEGA)
            pa, pb = shift * scale, OMEGA * scale
            coef[q, 0:1] = shift
            coef[q, 1:2] = ref[DAMP : DAMP + 1, at]
            coef[q, 2:3] = pa
            coef[q, 3:4] = pb
            coef[q, 8:16] = ref[FLOW : FLOW + 8, at]
            m = [ref[MASK[face] : MASK[face] + 1, at] for face in range(4)]
            m[0], m[1] = jnp.where(odd == 1, m[1], m[0]), jnp.where(odd == 1, m[0], m[1])
            for face in range(4):
                wide = jnp.broadcast_to(m[face], (16, WIDTH))
                if face >= 2:
                    wide = jnp.where(wall[face - 2], 0.0, wide)
                masks[q, face] = wide.astype(jnp.bfloat16)
            x = jnp.where(row < 5, ref[0:8, at], 0.0)
            y = jnp.where(row < 5, ref[8:16, at], 0.0)
            res[q, 0] = x
            res[q, 1] = y
            dx, dy = precond(pa, pb, x, y)
            dirs[s, 0] = dx
            dirs[s, 1] = dy
            high, low = split(jnp.concatenate([dx, dy], 0))
            parts[s, 0] = high
            parts[s, 1] = low
    for n, (b, c, side) in enumerate(LISTS):
        for t in range(2):
            at = slice(c * WIDTH + t * LANES, c * WIDTH + (t + 1) * LANES)
            pair = [refs[b][r : r + 1, at] for r in (DON0, DON1)]
            offset = jnp.where(odd == 1, pair[1 - side], pair[side]).astype(jnp.int32)
            index[n, t] = jnp.bitwise_and(lanes(8) + offset, LANES - 1)
    for n in FILLS_AT[0]:
        ghosts(dirs, dirs, parts, index, n)


def near_message(message, dirs, res, sdirs, sres):
    for n in range(SENT_DIRS):
        for h in range(2):
            message[8 * (2 * n + h) : 8 * (2 * n + h) + 8, :] = dirs[BLOCKS[OWN][0] + 7 - n, h]
    for n in range(SENT_RES):
        for h in range(2):
            at = 16 * SENT_DIRS + 8 * (2 * n + h)
            message[at : at + 8, :] = res[FIRST[OWN] + 7 - n, h]
    at = 16 * (SENT_DIRS + SENT_RES)
    for h in range(2):
        message[at + 8 * h : at + 8 * h + 8, 0:LANES] = sdirs[OWN, h]
        message[at + 8 * h : at + 8 * h + 8, LANES:] = sres[OWN, h]


def solve_kernel(begin, *refs):
    if begin == 0:
        (coef, masks, res0, dirs0, parts0, index, halo, basis) = refs[:8]
        (dirs, res, sol, sdirs, sres, message, parts, sparts, spre, sdon) = refs[8:]
        end = MIDDLE
    else:
        (coef, masks, old_dirs, old_res, old_sol, old_sdirs, old_sres, message, index, halo, basis) = refs[:11]
        (sol_out, res_out, dirs, res, sol, sdirs, sres, parts, sparts, spre, sdon) = refs[11:]
        end = ITERS
    nrm, odd = lax.axis_index("nrm"), mirrored()
    lane = lanes(8)
    lane16 = lanes(16)
    group = jnp.bitwise_and(lane, HALO - 1)
    low_rows = lax.broadcasted_iota(jnp.int32, (8, LANES), 0) < 5
    steps = chebyshev()

    def dirs_at(step):
        return dirs0 if step == 0 else dirs.at[step % 2]

    def parts_at(step):
        return parts0 if step == 0 else parts.at[step % 2]

    def store(par, s, values):
        for h in range(2):
            dirs[par, s, h] = values[h]
        high, low = split(jnp.concatenate(values, 0))
        parts[par, s, 0] = high
        parts[par, s, 1] = low

    def store_strip(par, b, values):
        for h in range(2):
            sdirs[par, b, h] = values[h]
        high, low = split(jnp.concatenate(values, 0))
        sparts[par, b, 0] = high
        sparts[par, b, 1] = low

    for b in range(4):
        at = slice(b * LANES, (b + 1) * LANES)
        shift = halo[SHIFT : SHIFT + 1, at]
        scale = 1.0 / (shift * shift + OMEGA * OMEGA)
        spre[b, 0:1] = shift * scale
        spre[b, 1:2] = OMEGA * scale
        m = [halo[MASK[face] : MASK[face] + 1, at] for face in range(4)]
        spre[b, 2:3] = jnp.where(odd == 1, m[1], m[0])
        spre[b, 3:4] = jnp.where(odd == 1, m[0], m[1])
        spre[b, 4:5] = m[2]
        spre[b, 5:6] = m[3]
        pair = [halo[r : r + 1, at] for r in (DON0, DON1)]
        sdon[b, 0] = jnp.where(odd == 1, pair[1], pair[0]).astype(jnp.int32) + lane
        sdon[b, 1] = jnp.where(odd == 1, pair[0], pair[1]).astype(jnp.int32) + lane
        if begin == 0:
            x = [jnp.where(low_rows, halo[8 * h : 8 * h + 8, at], 0.0) for h in range(2)]
            for h in range(2):
                sres[b, h] = x[h]
            store_strip(0, b, list(precond(shift * scale, OMEGA * scale, *x)))

    if begin:
        par = begin % 2
        for b, kept in ((FAR1, range(2, 8)), (OWN, range(8))):
            for c in kept:
                s, q = BLOCKS[b][0] + c, FIRST[b] + c
                store(par, s, [old_dirs[par, s, h] for h in range(2)])
                for h in range(2):
                    res[q, h] = old_res[q, h]
            store_strip(par, b, [old_sdirs[par, b, h] for h in range(2)])
            for h in range(2):
                sres[b, h] = old_sres[b, h]
        for c in range(8):
            for h in range(2):
                sol[c, h] = old_sol[c, h]
        slot, first = BLOCKS[NEAR][0], FIRST[NEAR]
        for n in range(SENT_DIRS):
            at = 16 * n
            store(par, slot + n, [message[at + 8 * h : at + 8 * h + 8, :] for h in range(2)])
        for n in range(SENT_RES):
            for h in range(2):
                at = 16 * (SENT_DIRS + n) + 8 * h
                res[first + n, h] = message[at : at + 8, :]
        swap = 7 * HALO - (lane - group) + group
        at = 16 * (SENT_DIRS + SENT_RES)
        values = []
        for h in range(2):
            rows = slice(at + 8 * h, at + 8 * h + 8)
            values.append(jnp.take_along_axis(message[rows, 0:LANES], swap, axis=1))
            sres[NEAR, h] = jnp.take_along_axis(message[rows, LANES:], swap, axis=1)
        store_strip(par, NEAR, values)

    def apply(d, far, y, shift, damp, flow):
        out = [shift * d[0] - OMEGA * d[1], shift * d[1] + OMEGA * d[0]]
        for h in range(2):
            out[h] = out[h] + damp * far[h]
        for m in range(5):
            f = flow(m)
            for h in range(2):
                out[h] = out[h] + f * y[16 * m + 8 * h : 16 * m + 8 * h + 8]
        return out

    def strips(step):
        par = step % 2
        source = dirs_at(step)
        for b in STRIPS[step]:
            slot, held, first, _ = BLOCKS[b]
            at = slice(b * LANES, (b + 1) * LANES)
            before, after = sdon[b, 0], sdon[b, 1]
            rows, far, mid = [[], [], [], []], [], []
            for h in range(2):
                d = sdirs[par, b, h]
                edge = jnp.zeros((8, LANES), jnp.float32)
                for c in range(held):
                    col = first + c
                    tile = source[slot + c, h, :, pl.ds(pl.multiple_of((1 - nrm) * LANES, LANES), LANES)]
                    tile = pltpu.roll(tile, HALO * col + 1 + 14 * nrm, 1)
                    edge = jnp.where((lane >= HALO * col) & (lane < HALO * (col + 1)), tile, edge)
                west, west2 = pltpu.roll(d, HALO, 1), pltpu.roll(d, 2 * HALO, 1)
                east, east2 = pltpu.roll(d, LANES - HALO, 1), pltpu.roll(d, LANES - 2 * HALO, 1)
                if b > 0:
                    other = sdirs[par, b - 1, h]
                    close = jnp.take_along_axis(other, jnp.bitwise_and(before + 7 * HALO, LANES - 1), axis=1)
                    next2 = jnp.take_along_axis(other, jnp.bitwise_and(before + 6 * HALO, LANES - 1), axis=1)
                    west = jnp.where(lane < HALO, close, west)
                    west2 = jnp.where(lane < 2 * HALO, next2, west2)
                if b < 3:
                    other = sdirs[par, b + 1, h]
                    close = jnp.take_along_axis(other, jnp.bitwise_and(after + HALO, LANES - 1), axis=1)
                    next2 = jnp.take_along_axis(other, jnp.bitwise_and(after + 2 * HALO, LANES - 1), axis=1)
                    east = jnp.where(lane >= 7 * HALO, close, east)
                    east2 = jnp.where(lane >= 6 * HALO, next2, east2)
                south = jnp.where(group == 0, edge, pltpu.roll(d, 1, 1))
                north = jnp.where(group == HALO - 1, edge, pltpu.roll(d, LANES - 1, 1))
                for face, value in enumerate((west, east, south, north)):
                    rows[face].append(spre[b, 2 + face : 3 + face] * value)
                far.append(west2 + east2)
                mid.append(d)
            high, low = split(jnp.concatenate(sum(rows, []), 0))
            y = jnp.dot(basis[...], jnp.concatenate([high, low, high], 0), preferred_element_type=jnp.float32)
            out = apply(
                mid, far, y, halo[SHIFT : SHIFT + 1, at], halo[DAMP : DAMP + 1, at],
                lambda m, at=at: halo[FLOW + m : FLOW + m + 1, at],
            )
            new = [sres[b, h] - out[h] for h in range(2)]
            for h in range(2):
                sres[b, h] = new[h]
            keep, gain = steps[step]
            turned = precond(spre[b, 0:1], spre[b, 1:2], *new)
            store_strip(1 - par, b, [keep * mid[h] + gain * turned[h] for h in range(2)])

    def column(step, b, c):
        slot, _, first, _ = BLOCKS[b]
        s, q = slot + c, FIRST[b] + c
        par = step % 2
        p = parts_at(step)
        turn = 127 - 14 * nrm - HALO * (first + c)
        stack = [[], []]
        for k in range(2):
            tiles = [p[s, k, :, t * LANES : (t + 1) * LANES] for t in range(2)]
            edge = pltpu.roll(sparts[par, b, k], turn, 1)
            up = [pltpu.roll(x, 1, 1) for x in tiles]
            down = [pltpu.roll(x, LANES - 1, 1) for x in tiles]
            south = [jnp.where(lane16 == 0, edge, up[0]), jnp.where(lane16 == 0, up[0], up[1])]
            north = [jnp.where(lane16 == LANES - 1, down[1], down[0]), jnp.where(lane16 == LANES - 1, edge, down[1])]
            for face, value in enumerate(
                (p[s - 1, k], p[s + 1, k], jnp.concatenate(south, 1), jnp.concatenate(north, 1))
            ):
                stack[k].append(masks[q, face] * value)
        return jnp.concatenate(stack[0] + stack[1] + stack[0], 0)

    def finish(step, b, c, y):
        s, q = BLOCKS[b][0] + c, FIRST[b] + c
        d = dirs_at(step)
        mid = [d[s, h] for h in range(2)]
        far = [d[s - 2, h] + d[s + 2, h] for h in range(2)]
        out = apply(mid, far, y, coef[q, 0:1], coef[q, 1:2], lambda m: coef[q, 8 + m : 9 + m])
        old = res0 if step == 0 else res
        new = [old[q, h] - out[h] for h in range(2)]
        for h in range(2):
            res[q, h] = new[h]
            if b == OWN:
                sol[c, h] = mid[h] if step == 0 else sol[c, h] + mid[h]
        if step + 1 < ITERS:
            keep, gain = steps[step]
            turned = precond(coef[q, 2:3], coef[q, 3:4], *new)
            store(1 - step % 2, s, [keep * mid[h] + gain * turned[h] for h in range(2)])

    for step in range(begin, end):
        if step:
            par = step % 2
            for n in FILLS_AT[step]:
                ghosts(dirs.at[par], dirs.at[par], parts.at[par], index, n)
        strips(step)
        for b, start, pairs in RANGES[step]:
            for c in range(start, start + 2 * pairs):
                y = jnp.dot(basis[...], column(step, b, c), preferred_element_type=jnp.float32)
                finish(step, b, c, y)

    if begin == 0:
        par = end % 2
        near_message(message, dirs.at[par], res, sdirs.at[par], sres)
    else:
        for i in range(8):
            c = place(OWN, i, odd)
            for h in range(2):
                sol_out[5 * h : 5 * h + 5, i, :] = sol[c, h][0:5]
                res_out[5 * h : 5 * h + 5, i, :] = res[FIRST[OWN] + c, h][0:5]


def moved(cells, pairs):
    return lax.ppermute(cells, "blk", [p for p in pairs(lax.axis_size("blk"))])


def far_pairs(by):
    def pairs(count):
        for i in range(count):
            j = i - by if i % 2 == 0 else i + by
            if 0 <= j < count:
                yield j, i

    return pairs


def chip_pairs(count):
    return [(i, i + 1 - 2 * (i % 2)) for i in range(count)]


def local(kernel, outs, scratch, *args, limit=16 << 20):
    vmem = pl.BlockSpec(memory_space=pltpu.VMEM)
    return pl.pallas_call(
        kernel,
        out_shape=outs,
        in_specs=[vmem] * len(args),
        out_specs=jax.tree.map(lambda _: vmem, outs),
        scratch_shapes=scratch,
        compiler_params=pltpu.CompilerParams(vmem_limit_bytes=limit),
    )(*args)


def inside(x):
    return pltpu.with_memory_space_constraint(x, pltpu.VMEM)


def step(right_side, mean_flow, jac_basis, pattern, shift_diag, dissipation, donors):
    rows, width = right_side.shape[1:]
    f32, bf16 = jnp.float32, jnp.bfloat16
    vmem = pltpu.VMEM
    half = rows * width // 2

    whole, part = local(
        pack_kernel,
        (vmem((FEATS, 2 * half), f32), vmem((FEATS, half), f32)),
        [],
        right_side, mean_flow, pattern, shift_diag, dissipation, donors,
        limit=None,
    )
    far1 = moved(whole, far_pairs(1))
    far2 = moved(part, far_pairs(2))
    near = moved(whole, chip_pairs)
    basis = local(
        basis_kernel, vmem((80, 192), bf16), [vmem((80, LANES), f32)], jac_basis.transpose(1, 2, 0, 3)
    )

    cells = [inside(x) for x in (far2, far1, whole, near)]
    strip = local(strip_kernel, vmem((FEATS, 4 * LANES), f32), [], *cells)
    halo = lax.ppermute(strip, "nrm", [(0, 1), (1, 0)])
    coef, masks, res0, dirs0, parts0, index = local(
        prep_kernel,
        (
            vmem((COLUMNS, 16, WIDTH), f32),
            vmem((COLUMNS, 4, 16, WIDTH), bf16),
            vmem((COLUMNS, 2, 8, WIDTH), f32),
            vmem((SLOTS, 2, 8, WIDTH), f32),
            vmem((SLOTS, 2, 16, WIDTH), bf16),
            vmem((6, 2, 8, LANES), jnp.int32),
        ),
        [],
        *cells,
    )

    halo, basis = inside(halo), inside(basis)
    state = (
        vmem((2, SLOTS, 2, 8, WIDTH), f32),
        vmem((COLUMNS, 2, 8, WIDTH), f32),
        vmem((8, 2, 8, WIDTH), f32),
        vmem((2, 4, 2, 8, LANES), f32),
        vmem((4, 2, 8, LANES), f32),
    )
    scratch = (
        vmem((2, SLOTS, 2, 16, WIDTH), bf16),
        vmem((2, 4, 2, 16, LANES), bf16),
        vmem((4, 8, LANES), f32),
        vmem((4, 2, 8, LANES), jnp.int32),
    )
    *kept, message = local(
        functools.partial(solve_kernel, 0),
        (*state, vmem((16 * (SENT_DIRS + SENT_RES + 1), WIDTH), f32)),
        scratch,
        *[inside(x) for x in (coef, masks, res0, dirs0, parts0, index)], halo, basis,
    )
    message = moved(message, chip_pairs)
    out = jax.ShapeDtypeStruct(right_side.shape, f32)
    return local(
        functools.partial(solve_kernel, MIDDLE), (out, out), (*state, *scratch),
        *[inside(x) for x in (coef, masks, *kept, message, index)], halo, basis,
    )


def solution(mesh):
    return jax.shard_map(
        step,
        mesh=mesh,
        in_specs=(
            P(None, "blk", "nrm"),
            P(None, "blk", "nrm"),
            P(),
            P(None, "blk", "nrm"),
            P("blk", "nrm"),
            P("blk", "nrm"),
            P("blk", None, "nrm"),
        ),
        out_specs=(P(None, "blk", "nrm"), P(None, "blk", "nrm")),
        check_vma=False,
    )
```

time: 43.8 us -> 41 us (0.936)
  the two profiles are of different devices: /device:TPU:254 before, /device:TPU:512 now
where the time goes in v3:
time: 41 us; the launch traced here: 40.4 us
  starting transfers between devices  18 us (44%)
  waiting for transfers between devices  14.4 us (35%)
  Pallas kernels  6.45 us (16%)
  local copies, waits for them, and re-layouts  0.89 us (2%)
  between operations  0.7 us (2%)
    ppermute x4, starting transfers between devices, moved(): return lax.ppermute(cells, 'blk', [p for p in pairs(lax.axis_size('blk'))])  15.4 us
    ppermute x4, waiting for transfers between devices, moved(): return lax.ppermute(cells, 'blk', [p for p in pairs(lax.axis_size('blk'))])  12.6 us
    pallas_call x6, Pallas kernels, local(): pl.pallas_call(kernel, out_shape=outs, in_specs=[vmem] * len(args), out_s...  6.45 us
    ppermute x1, starting transfers between devices, step(): halo = lax.ppermute(strip, 'nrm', [(0, 1), (1, 0)])  2.58 us
    ppermute x1, waiting for transfers between devices, step(): halo = lax.ppermute(strip, 'nrm', [(0, 1), (1, 0)])  1.79 us
    unnamed x2, local copies, waits for them, and re-layouts  0.89 us
  transfers between devices with their start and end apart: 5, of which 3 were waited for; matrix products, arithmetic and copies ran while one was open for 0% of the time, Pallas kernels for 2%

profile of v3, /device:TPU:512, one launch (start us, length us, event | category | flops | bytes accessed | tf_op | source)
XLA Modules:
  0.0 40.4 jit_solution(2652354164211845822)
XLA Ops:
  0.6 1.0 %shard_map.86 = (f32[24,2048]{1,0:T(8,128)S(1)}, f32[24,1024]{1,0:T(8,128)S(1)}) custom-call(f32[10,8,256]{2,1,0:T(8,128)} %rhs.1, f32[5,8,256]{2,1,0:T(8,128)} %flow.1, s32[4,8,256]{2,1,0:T(8,128)} %mask.1, f32[8,256]{1,0:T(8,128)} %shift.1, f32[8,256]{1,0:T(8,128)} %damp.1, s32[1,2,256]{2,1,0:T(2,128)} %donors.1), custom_call_target="tpu_custom_call" | custom-call | tf_op jit(solution)/shard_map/pallas_call | solution.py:435
  1.7 1.9 %collective-permute-start.2 = (f32[24,2048]{1,0:T(8,128)S(1)}, f32[24,2048]{1,0:T(8,128)S(1)}, u32[]{:S(2)}, u32[]{:S(2)}) collective-permute-start(f32[24,2048]{1,0:T(8,128)S(1)} %get-tuple-element.17.own.refs_2_), channel_id=1, source_target_pairs={{0,2},{2,0},{4,6},{6,4},{8,10},{10,8},{12,14},{14,12},{16,18},{18,... | collective-permute-start | bytes 589832 | tf_op jit(solution)/shard_map/ppermute | solution.py:416
  3.6 9.7 %collective-permute-start.1 = (f32[24,2048]{1,0:T(8,128)S(1)}, f32[24,2048]{1,0:T(8,128)S(1)}, u32[]{:S(2)}, u32[]{:S(2)}) collective-permute-start(f32[24,2048]{1,0:T(8,128)S(1)} %get-tuple-element.17.own.refs_2_), channel_id=1, source_target_pairs={{4,2},{2,4},{8,6},{6,8},{12,10},{10,12},{16,14},{14,16},{20,18},{1... | collective-permute-start | bytes 589832 | tf_op jit(solution)/shard_map/ppermute | solution.py:416
  13.3 1.9 %collective-permute-start = (f32[24,1024]{1,0:T(8,128)S(1)}, f32[24,1024]{1,0:T(8,128)S(1)}, u32[]{:S(2)}, u32[]{:S(2)}) collective-permute-start(f32[24,1024]{1,0:T(8,128)S(1)} %get-tuple-element.16), channel_id=1, source_target_pairs={{6,2},{0,4},{10,6},{4,8},{14,10},{8,12},{18,14},{12,16},{22,18},{1... | collective-permute-start | bytes 294920 | tf_op jit(solution)/shard_map/ppermute | solution.py:416
  15.2 11.2 %collective-permute-done.far2.refs_0_ = f32[24,1024]{1,0:T(8,128)S(1)} collective-permute-done((f32[24,1024]{1,0:T(8,128)S(1)}, f32[24,1024]{1,0:T(8,128)S(1)}, u32[]{:S(2)}, u32[]{:S(2)}) %collective-permute-start) | collective-permute-done | bytes 98336 | tf_op jit(solution)/shard_map/ppermute | solution.py:416
  26.4 0.0 collective-permute-done.2.near.refs_3_
  26.4 0.0 collective-permute-done.1.far1.refs_1_
  26.4 0.2 shard_map.88
  26.5 2.6 %collective-permute-start.3 = (f32[24,512]{1,0:T(8,128)S(1)}, f32[24,512]{1,0:T(8,128)S(1)}, u32[]{:S(2)}, u32[]{:S(2)}) collective-permute-start(f32[24,512]{1,0:T(8,128)S(1)} %shard_map.88), channel_id=1, source_target_pairs={{0,1},{1,0},{2,3},{3,2},{4,5},{5,4},{6,7},{7,6},{8,9},{9,8},{10,11... | collective-permute-start | bytes 147464 | tf_op jit(solution)/shard_map/ppermute | solution.py:471
  29.1 0.0 copy-start
  29.1 0.9 %copy-done = f32[4,5,10,10]{3,0,2,1:T(4,128)S(1)} copy-done((f32[4,5,10,10]{3,0,2,1:T(4,128)S(1)}, f32[4,5,10,10]{3,0,2,1:T(4,128)}, u32[]{:S(2)}) %copy-start) | copy-done | bytes 8024
  30.0 0.3 shard_map.89.refs_7_.refs_10_
  30.3 0.4 shard_map.87
  30.7 1.8 %collective-permute-done.3.refs_6_.refs_9_ = f32[24,512]{1,0:T(8,128)S(1)} collective-permute-done((f32[24,512]{1,0:T(8,128)S(1)}, f32[24,512]{1,0:T(8,128)S(1)}, u32[]{:S(2)}, u32[]{:S(2)}) %collective-permute-start.3) | collective-permute-done | bytes 49184 | tf_op jit(solution)/shard_map/ppermute | solution.py:471
  32.5 2.3 %shard_map.90 = (f32[2,38,2,8,256]{4,3,2,1,0:T(8,128)S(1)}, f32[26,2,8,256]{3,2,1,0:T(8,128)S(1)}, f32[8,2,8,256]{3,2,1,0:T(8,128)S(1)}, f32[2,4,2,8,128]{4,3,2,...) custom-call(f32[26,16,256]{2,1,0:T(8,128)S(1)} %get-tuple-element.18.refs_0_, ...), custom_call_target="tpu_custom_call" | custom-call | tf_op jit(solution)/shard_map/pallas_call | solution.py:435
  34.9 1.9 %collective-permute-start.4 = (f32[176,256]{1,0:T(8,128)S(1)}, f32[176,256]{1,0:T(8,128)S(1)}, u32[]{:S(2)}, u32[]{:S(2)}) collective-permute-start(f32[176,256]{1,0:T(8,128)S(1)} %get-tuple-element.29), channel_id=1, source_target_pairs={{0,2},{2,0},{4,6},{6,4},{8,10},{10,8},{12,14},{14,12},{16,18},{18,... | collective-permute-start | bytes 540680 | tf_op jit(solution)/shard_map/ppermute | solution.py:416
  36.8 1.4 %collective-permute-done.4.refs_7_ = f32[176,256]{1,0:T(8,128)S(1)} collective-permute-done((f32[176,256]{1,0:T(8,128)S(1)}, f32[176,256]{1,0:T(8,128)S(1)}, u32[]{:S(2)}, u32[]{:S(2)}) %collective-permute-start.4) | collective-permute-done | bytes 180256 | tf_op jit(solution)/shard_map/ppermute | solution.py:416
  38.2 2.2 %shard_map.91 = (f32[10,8,256]{2,1,0:T(8,128)}, f32[10,8,256]{2,1,0:T(8,128)}) custom-call(f32[26,16,256]{2,1,0:T(8,128)S(1)} %get-tuple-element.18.refs_0_, bf16[26,4,16,256]{3,2,1,0:T(8,128)(2,1)S(1)} %get-tuple-element.19.refs_1_, f32[2,38,2,8,256]{4,3,2,1,0:T(8,128)S(1)} %get-tuple-element.24.refs_2_, f32[26,2,8,256]{3,2,1,0:T(8,128)S(1)} %get-tuple-element.25.refs_3_, ...), custom_call_target="tpu_custom_call" | custom-call | tf_op jit(solution)/shard_map/pallas_call | solution.py:435
Async XLA Ops:
  1.7 24.7 %collective-permute-start.2 = (f32[24,2048]{1,0:T(8,128)S(1)}, f32[24,2048]{1,0:T(8,128)S(1)}, u32[]{:S(2)}, u32[]{:S(2)}) collective-permute-start(f32[24,2048]{1,0:T(8,128)S(1)} %get-tuple-element.17.own.refs_2_), channel_id=1, source_target_pairs={{0,2},{2,0},{4,6},{6,4},{8,10},{10,8},{12,14},{14,12},{16,18},{18,... | collective-permute-start | bytes 589832 | tf_op jit(solution)/shard_map/ppermute | solution.py:416
  3.6 22.8 %collective-permute-start.1 = (f32[24,2048]{1,0:T(8,128)S(1)}, f32[24,2048]{1,0:T(8,128)S(1)}, u32[]{:S(2)}, u32[]{:S(2)}) collective-permute-start(f32[24,2048]{1,0:T(8,128)S(1)} %get-tuple-element.17.own.refs_2_), channel_id=1, source_target_pairs={{4,2},{2,4},{8,6},{6,8},{12,10},{10,12},{16,14},{14,16},{20,18},{1... | collective-permute-start | bytes 589832 | tf_op jit(solution)/shard_map/ppermute | solution.py:416
  13.3 13.1 %collective-permute-start = (f32[24,1024]{1,0:T(8,128)S(1)}, f32[24,1024]{1,0:T(8,128)S(1)}, u32[]{:S(2)}, u32[]{:S(2)}) collective-permute-start(f32[24,1024]{1,0:T(8,128)S(1)} %get-tuple-element.16), channel_id=1, source_target_pairs={{6,2},{0,4},{10,6},{4,8},{14,10},{8,12},{18,14},{12,16},{22,18},{1... | collective-permute-start | bytes 294920 | tf_op jit(solution)/shard_map/ppermute | solution.py:416
  26.5 6.0 %collective-permute-start.3 = (f32[24,512]{1,0:T(8,128)S(1)}, f32[24,512]{1,0:T(8,128)S(1)}, u32[]{:S(2)}, u32[]{:S(2)}) collective-permute-start(f32[24,512]{1,0:T(8,128)S(1)} %shard_map.88), channel_id=1, source_target_pairs={{0,1},{1,0},{2,3},{3,2},{4,5},{5,4},{6,7},{7,6},{8,9},{9,8},{10,11... | collective-permute-start | bytes 147464 | tf_op jit(solution)/shard_map/ppermute | solution.py:471
  29.1 0.9 %copy-start = (f32[4,5,10,10]{3,0,2,1:T(4,128)S(1)}, f32[4,5,10,10]{3,0,2,1:T(4,128)}, u32[]{:S(2)}) copy-start(f32[4,5,10,10]{3,0,2,1:T(4,128)} %param.9) | copy-start | bytes 24004
  34.9 3.3 %collective-permute-start.4 = (f32[176,256]{1,0:T(8,128)S(1)}, f32[176,256]{1,0:T(8,128)S(1)}, u32[]{:S(2)}, u32[]{:S(2)}) collective-permute-start(f32[176,256]{1,0:T(8,128)S(1)} %get-tuple-element.29), channel_id=1, source_target_pairs={{0,2},{2,0},{4,6},{6,4},{8,10},{10,8},{12,14},{14,12},{16,18},{18,... | collective-permute-start | bytes 540680 | tf_op jit(solution)/shard_map/ppermute | solution.py:416

commit v4 on v3

v4 whole, which is shorter than its diff:
```python
import functools

import jax
import jax.numpy as jnp
from jax import lax
from jax.experimental import pallas as pl
from jax.experimental.pallas import tpu as pltpu
from jax.sharding import PartitionSpec as P


ITERS = 6
OMEGA = 0.3
DELTA = 0.9

SHIFT, DAMP, DON0, DON1 = 5, 6, 21, 22
MASK = (7, 13, 14, 15)
FLOW = 16
WHOLE_B, WHOLE_FLOW, WHOLE_DON, WHOLE_ROWS = 128, 256, 336, 344
PART_B, PART_FLOW, PART_DON, PART_ROWS = 64, 128, 148, 152
FEATS = 24
HALO = 16
LANES = 128
WIDTH = 256

FAR2, FAR1, OWN, NEAR = 0, 1, 2, 3
BLOCKS = ((0, 4, 4, 4), (8, 8, 0, 8), (20, 8, 0, 8), (32, 6, 0, 8))
FIRST = (0, 4, 12, 20)
COLUMNS = 26
SLOTS = 38
MIDDLE = 3
FIRST_HALF, EARLY, LATE = 0, 1, 2
PLANS = (
    {
        0: (((0, 2, 1), (1, 0, 4), (2, 0, 4), (3, 0, 2)), (), ()),
        1: (((1, 0, 4), (2, 0, 4), (3, 0, 1)), (1, 2, 3, 4, 5), ()),
        2: (((1, 2, 3), (2, 0, 4)), (2, 3, 4), ()),
    },
    {
        3: (((1, 4, 2), (2, 0, 3)), (2, 3), (1, 2)),
        4: (((1, 6, 1), (2, 0, 2)), (2, 3), (2,)),
        5: (((2, 0, 1),), (3,), ()),
    },
    {
        3: (((2, 6, 1), (3, 0, 2)), (4, 5), (2, 3)),
        4: (((2, 4, 2), (3, 0, 1)), (4, 5), (2,)),
        5: (((2, 2, 3),), (4,), ()),
    },
)
EARLY_LANES = 6 * HALO
TILES = ((0, 1), (1, 0), (1, 1), (2, 0), (2, 1), (3, 0), (3, 1))
TILES_AT = (range(0, 6), range(1, 6), range(1, 5))
FIX = 1 + 3 * (MIDDLE - 1)
LISTS = ((0, 1), (1, 0), (1, 1), (2, 0), (2, 1), (3, 0))
FILLS = ((4, 8, 0), (6, 2, 1), (16, 20, 2), (18, 14, 3), (28, 32, 4), (30, 26, 5))
SENT_DIRS, SENT_RES = 6, 4


def chebyshev():
    sigma = 1.0 / DELTA
    rho = DELTA
    steps = []
    for _ in range(ITERS - 1):
        rho_new = 1.0 / (2.0 * sigma - rho)
        steps.append((rho_new * rho, 2.0 * rho_new / DELTA))
        rho = rho_new
    return steps


def split(full):
    high = full.astype(jnp.bfloat16)
    return high, (full - high.astype(jnp.float32)).astype(jnp.bfloat16)


def precond(pa, pb, a, b):
    return pa * a + pb * b, pa * b - pb * a


def lanes(rows):
    return lax.broadcasted_iota(jnp.int32, (rows, LANES), 1)


def mirrored():
    return lax.rem(lax.axis_index("blk"), 2)


def place(b, c, odd):
    return c if b == FAR2 else c + odd * (7 - 2 * c)


def flow_row(b, c, m, t, odd):
    if b == FAR2:
        return PART_FLOW + 10 * (c - 2) + 2 * m + t if c >= 2 else None
    return WHOLE_FLOW + 8 * (2 * m + t) + place(b, c, odd)


def donor_row(b, side, t, odd):
    if b == FAR2:
        return PART_DON + t
    return WHOLE_DON + 2 * (side + odd * (1 - 2 * side)) + t


def pack_kernel(rhs, flow, mask, shift, damp, donors, whole, part):
    nrm, odd = lax.axis_index("nrm"), mirrored()
    count, width = rhs.shape[1:]
    here = lax.broadcasted_iota(jnp.int32, (1, width), 1) + nrm * width
    offsets = (donors[0] - here).astype(jnp.float32)
    for t in range(2):
        half = slice(t * LANES, (t + 1) * LANES)
        for i in range(count):
            at = 8 * (2 * i + t)
            whole[at : at + 5] = rhs[0:5, i, half]
            whole[at + SHIFT : at + SHIFT + 1] = shift[i : i + 1, half]
            whole[at + DAMP : at + DAMP + 1] = damp[i : i + 1, half]
            whole[at + 7 : at + 8] = mask[0:1, i, half].astype(jnp.float32)
            at = at + WHOLE_B
            whole[at : at + 5] = rhs[5:10, i, half]
            whole[at + 5 : at + 8] = mask[1:4, i, half].astype(jnp.float32)
        for m in range(5):
            at = WHOLE_FLOW + 8 * (2 * m + t)
            whole[at : at + 8] = flow[m, :, half]
        for side in range(2):
            at = WHOLE_DON + 2 * side + t
            whole[at : at + 1] = offsets[side : side + 1, half]
    whole[WHOLE_DON + 4 : WHOLE_ROWS] = jnp.zeros((4, LANES), jnp.float32)
    for c in range(4):
        p = place(OWN, 4 + c, odd)
        for t in range(2):
            for to, base in ((0, 0), (PART_B, WHOLE_B)):
                at = pl.multiple_of(base + 8 * (2 * p + t), 8)
                part[to + 8 * (2 * c + t) : to + 8 * (2 * c + t) + 8] = whole[pl.ds(at, 8)]
            for m in range(5):
                to = flow_row(FAR2, c, m, t, odd)
                if to is not None:
                    part[to : to + 1] = whole[pl.ds(flow_row(OWN, 4 + c, m, t, odd), 1)]
    for t in range(2):
        part[PART_DON + t : PART_DON + t + 1] = whole[pl.ds(donor_row(OWN, 1, t, odd), 1)]
    part[PART_DON + 2 : PART_ROWS] = jnp.zeros((2, LANES), jnp.float32)


def basis_kernel(jac, basis, full):
    full[...] = jnp.zeros(full.shape, jnp.float32)
    for f in range(4):
        for m in range(5):
            for h in range(2):
                for g in range(2):
                    block = jac[m, 5 * h : 5 * h + 5, f, 5 * g : 5 * g + 5]
                    full[16 * m + 8 * h : 16 * m + 8 * h + 5, 16 * f + 8 * g : 16 * f + 8 * g + 5] = block
    j = full[...]
    lane = lanes(80)
    other = jnp.where(lane < 16, pltpu.roll(j, LANES - 16, 1), pltpu.roll(j, 16, 1))
    j = jnp.where((mirrored() == 1) & (lane < 32), other, j)[:, 0:64]
    high, low = split(j)
    basis[:, 0:64] = high
    basis[:, 64:128] = high
    basis[:, 128:192] = low


def strip_kernel(*refs):
    nrm, odd = lax.axis_index("nrm"), mirrored()
    strip = refs[-1]
    lane = lanes(FEATS)
    t = 1 - nrm
    for b, ref in enumerate(refs[:-1]):
        first, sent = BLOCKS[b][2:]
        second = PART_B if b == FAR2 else WHOLE_B
        rows = jnp.zeros((FEATS, LANES), jnp.float32)
        lists = [ref[pl.ds(donor_row(b, side, t, 0), 1)] for side in range(2)]
        for c in range(sent):
            at = 8 * (2 * place(b, c, odd) + t)
            col = first + c
            edge = [ref[pl.ds(pl.multiple_of(base + at, 8), 8)] for base in (0, second)]
            if flow_row(b, c, 0, 0, 0) is None:
                edge.append(jnp.zeros((8, LANES), jnp.float32))
            else:
                flows = [ref[pl.ds(flow_row(b, c, m, t, odd), 1)] for m in range(5)]
                edge.append(jnp.concatenate(flows + lists + [jnp.zeros((1, LANES), jnp.float32)], 0))
            edge = pltpu.roll(jnp.concatenate(edge, 0), lax.rem(HALO * (col + 1 - nrm), LANES), 1)
            rows = jnp.where((lane >= HALO * col) & (lane < HALO * (col + 1)), edge, rows)
        strip[:, b * LANES : (b + 1) * LANES] = rows


def ghosts(src_d, dst_d, dst_h, index, n):
    dst, src, which = FILLS[n]
    lane = lanes(8)
    for c in range(2):
        for t in range(2):
            at = index[which, t]
            across = jnp.abs(at - lane) > LANES // 2
            picked = []
            for h in range(2):
                tiles = [src_d[src + c, h, :, u * LANES : (u + 1) * LANES] for u in (t, 1 - t)]
                here, there = (jnp.take_along_axis(x, at, axis=1) for x in tiles)
                picked.append(jnp.where(across, there, here))
                dst_d[dst + c, h, :, t * LANES : (t + 1) * LANES] = picked[h]
            high, low = split(jnp.concatenate(picked, 0))
            dst_h[dst + c, 0, :, t * LANES : (t + 1) * LANES] = high
            dst_h[dst + c, 1, :, t * LANES : (t + 1) * LANES] = low


def prep_kernel(far2, far1, own, near, coef, masks, res, dirs, parts, index):
    nrm, odd = lax.axis_index("nrm"), mirrored()
    refs = (far2, far1, own, near)
    row = lax.broadcasted_iota(jnp.int32, (8, WIDTH), 0)
    lane = lax.broadcasted_iota(jnp.int32, (16, WIDTH), 1)
    wall = ((lane == 0) & (nrm == 0), (lane == WIDTH - 1) & (nrm == 1))
    for b, ref in enumerate(refs):
        slot, held = BLOCKS[b][:2]
        second = PART_B if b == FAR2 else WHOLE_B
        for c in range(held):
            q, s = FIRST[b] + c, slot + c
            at = 16 * place(b, c, odd)

            def both(row, count, ref=ref, at=at, second=second):
                base = at + (row if row < 8 else second + row - 8)
                if count == 8:
                    base = pl.multiple_of(base, 8)
                return jnp.concatenate([ref[pl.ds(base, count)], ref[pl.ds(base + 8, count)]], 1)

            shift = both(SHIFT, 1)
            scale = 1.0 / (shift * shift + OMEGA * OMEGA)
            pa, pb = shift * scale, OMEGA * scale
            coef[q, 0:1] = shift
            coef[q, 1:2] = both(DAMP, 1)
            coef[q, 2:3] = pa
            coef[q, 3:4] = pb
            for m in range(5):
                for t in range(2):
                    r = flow_row(b, c, m, t, odd)
                    if r is not None:
                        coef[q, 8 + m : 9 + m, t * LANES : (t + 1) * LANES] = ref[pl.ds(r, 1)]
            m = [both(MASK[face], 1) for face in range(4)]
            m[0], m[1] = jnp.where(odd == 1, m[1], m[0]), jnp.where(odd == 1, m[0], m[1])
            for face in range(4):
                wide = jnp.broadcast_to(m[face], (16, WIDTH))
                if face >= 2:
                    wide = jnp.where(wall[face - 2], 0.0, wide)
                masks[q, face] = wide.astype(jnp.bfloat16)
            x = jnp.where(row < 5, both(0, 8), 0.0)
            y = jnp.where(row < 5, both(8, 8), 0.0)
            res[q, 0] = x
            res[q, 1] = y
            dx, dy = precond(pa, pb, x, y)
            dirs[s, 0] = dx
            dirs[s, 1] = dy
            high, low = split(jnp.concatenate([dx, dy], 0))
            parts[s, 0] = high
            parts[s, 1] = low
    for n, (b, side) in enumerate(LISTS):
        for t in range(2):
            offset = refs[b][pl.ds(donor_row(b, side, t, odd), 1)].astype(jnp.int32)
            index[n, t] = jnp.bitwise_and(lanes(8) + offset, LANES - 1)
    for n in range(len(FILLS)):
        ghosts(dirs, dirs, parts, index, n)


def patched(main, tile, c, nrm):
    lane = lax.broadcasted_iota(jnp.int32, (8, WIDTH), 1)
    tile = pltpu.roll(tile, 7 * HALO - 2 * HALO * (c % 4), 1)
    return jnp.where(
        jnp.where(nrm == 0, WIDTH - 1 - lane, lane) < FIX, jnp.concatenate([tile, tile], 1), main
    )


def apply(basis, rows, d, far, shift, damp, flow):
    y = jnp.dot(basis[...], rows, preferred_element_type=jnp.float32)
    out = [shift * d[0] - OMEGA * d[1], shift * d[1] + OMEGA * d[0]]
    for h in range(2):
        out[h] = out[h] + damp * far[h]
    for m in range(5):
        f = flow(m)
        for h in range(2):
            out[h] = out[h] + f * y[16 * m + 8 * h : 16 * m + 8 * h + 8]
    return out


def edge_kernel(
    strip, halo, basis, dirs, res, ed, er, es, sdirs, sres, message, feat, pre, don, cur, rem,
):
    nrm, odd = lax.axis_index("nrm"), mirrored()
    lane = lanes(8)
    wide = lanes(FEATS)
    low_rows = lax.broadcasted_iota(jnp.int32, (8, LANES), 0) < 5
    steps = chebyshev()
    for e, (b, t) in enumerate(TILES):
        at = slice(b * LANES, (b + 1) * LANES)
        mine, theirs = strip[:, at], halo[:, at]
        pair = (jnp.where(nrm == 0, mine, theirs), jnp.where(nrm == 0, theirs, mine))
        from_lane = HALO * (4 * t + jnp.right_shift(lane, 5)) + jnp.bitwise_and(lane, HALO - 1)
        for k in range(3):
            picked = [jnp.take_along_axis(x[8 * k : 8 * k + 8], from_lane, axis=1) for x in pair]
            feat[e, 8 * k : 8 * k + 8] = jnp.where(jnp.bitwise_and(lane, HALO) == 0, *picked)
        shift = feat[e, SHIFT : SHIFT + 1]
        scale = 1.0 / (shift * shift + OMEGA * OMEGA)
        pre[e, 0:1] = shift * scale
        pre[e, 1:2] = OMEGA * scale
        m = [feat[e, MASK[face] : MASK[face] + 1] for face in range(4)]
        pre[e, 2:3] = jnp.where(odd == 1, m[1], m[0])
        pre[e, 3:4] = jnp.where(odd == 1, m[0], m[1])
        pre[e, 4:5] = m[2]
        pre[e, 5:6] = m[3]
        pair = [feat[e, r : r + 1] for r in (DON0, DON1)]
        don[e, 0] = jnp.where(odd == 1, pair[1], pair[0]).astype(jnp.int32) + lane
        don[e, 1] = jnp.where(odd == 1, pair[0], pair[1]).astype(jnp.int32) + lane
        x = [jnp.where(low_rows, feat[e, 8 * h : 8 * h + 8], 0.0) for h in range(2)]
        made = precond(shift * scale, OMEGA * scale, *x)
        for h in range(2):
            rem[e, h] = x[h]
            cur[0, e, h] = made[h]

    span = 2 * HALO
    for step in range(MIDDLE):
        par = step % 2
        for e in TILES_AT[step]:
            b, t = TILES[e]
            rows, far, mid = [[], [], [], []], [], []
            for h in range(2):
                d = cur[par, e, h]
                west, west2 = pltpu.roll(d, span, 1), pltpu.roll(d, 2 * span, 1)
                east, east2 = pltpu.roll(d, LANES - span, 1), pltpu.roll(d, LANES - 2 * span, 1)
                if e > 0:
                    other = cur[par, e - 1, h]
                    if t == 0:
                        close = jnp.take_along_axis(other, jnp.bitwise_and(don[e, 0] + 3 * span, LANES - 1), axis=1)
                        next2 = jnp.take_along_axis(other, jnp.bitwise_and(don[e, 0] + 2 * span, LANES - 1), axis=1)
                    else:
                        close, next2 = pltpu.roll(other, span, 1), pltpu.roll(other, 2 * span, 1)
                    west = jnp.where(lane < span, close, west)
                    west2 = jnp.where(lane < 2 * span, next2, west2)
                if e + 1 < len(TILES):
                    other = cur[par, e + 1, h]
                    if t == 1:
                        close = jnp.take_along_axis(other, jnp.bitwise_and(don[e, 1] + span, LANES - 1), axis=1)
                        next2 = jnp.take_along_axis(other, jnp.bitwise_and(don[e, 1] + 2 * span, LANES - 1), axis=1)
                    else:
                        close, next2 = pltpu.roll(other, LANES - span, 1), pltpu.roll(other, LANES - 2 * span, 1)
                    east = jnp.where(lane >= 3 * span, close, east)
                    east2 = jnp.where(lane >= 2 * span, next2, east2)
                for face, value in enumerate((west, east, pltpu.roll(d, 1, 1), pltpu.roll(d, LANES - 1, 1))):
                    rows[face].append(pre[e, 2 + face : 3 + face] * value)
                far.append(west2 + east2)
                mid.append(d)
            high, low = split(jnp.concatenate(sum(rows, []), 0))
            out = apply(
                basis, jnp.concatenate([high, low, high], 0), mid, far,
                feat[e, SHIFT : SHIFT + 1], feat[e, DAMP : DAMP + 1], lambda m, e=e: feat[e, FLOW + m : FLOW + m + 1],
            )
            new = [rem[e, h] - out[h] for h in range(2)]
            keep, gain = steps[step]
            turned = precond(pre[e, 0:1], pre[e, 1:2], *new)
            for h in range(2):
                rem[e, h] = new[h]
                cur[1 - par, e, h] = keep * mid[h] + gain * turned[h]
                if b == OWN:
                    es[t, h] = mid[h] if step == 0 else es[t, h] + mid[h]

    par = MIDDLE % 2
    from_lane = span * jnp.bitwise_and(jnp.right_shift(lane, 4), 3) + HALO * (1 - nrm) + jnp.bitwise_and(lane, HALO - 1)
    for e in range(1, 5):
        for h in range(2):
            ed[e - 1, h] = cur[par, e, h]
            er[e - 1, h] = rem[e, h]
    for b in (FAR1, OWN):
        for h in range(2):
            for out, tiles in ((sdirs, cur.at[par]), (sres, rem)):
                halves = [jnp.take_along_axis(tiles[2 * b - 1 + t, h], from_lane, axis=1) for t in range(2)]
                out[b - 1, h] = jnp.where(lane < LANES // 2, *halves)

    for n in range(SENT_DIRS):
        c = 7 - n
        for h in range(2):
            at = 8 * (2 * n + h)
            message[at : at + 8, :] = patched(dirs[par, BLOCKS[OWN][0] + c, h], ed[2 + c // 4, h], c, nrm)
    for n in range(SENT_RES):
        c = 7 - n
        for h in range(2):
            at = 16 * SENT_DIRS + 8 * (2 * n + h)
            message[at : at + 8, :] = patched(res[FIRST[OWN] + c, h], er[2 + c // 4, h], c, nrm)
    at = 16 * (SENT_DIRS + SENT_RES)
    for h in range(2):
        message[at + 8 * h : at + 8 * h + 8, 0:LANES] = sdirs[OWN - 1, h]
        message[at + 8 * h : at + 8 * h + 8, LANES:] = sres[OWN - 1, h]


def solve_kernel(phase, *refs):
    if phase == FIRST_HALF:
        (coef, masks, res0, dirs0, parts0, index, basis) = refs[:7]
        (dirs, res, sol, parts) = refs[7:]
    elif phase == EARLY:
        (coef, masks, old_dirs, old_res, old_sol, ed, er, es, old_sdirs, old_sres, index, halo, basis) = refs[:13]
        (dirs, res, sol, parts, kept_dirs, kept_res, sdirs, sres, sparts, spre, sdon) = refs[13:]
    else:
        (coef, masks, _, _, _, _, kept_dirs, kept_res, old_sdirs, old_sres, message, index, halo, basis) = refs[:14]
        (sol_out, res_out, dirs, res, sol, parts, sdirs, sres, sparts, spre, sdon) = refs[14:]
    nrm, odd = lax.axis_index("nrm"), mirrored()
    lane = lanes(8)
    lane16 = lanes(16)
    group = jnp.bitwise_and(lane, HALO - 1)
    low_rows = lax.broadcasted_iota(jnp.int32, (8, LANES), 0) < 5
    steps = chebyshev()

    def dirs_at(step):
        return dirs0 if step == 0 else dirs.at[step % 2]

    def parts_at(step):
        return parts0 if step == 0 else parts.at[step % 2]

    def store(par, s, values):
        for h in range(2):
            dirs[par, s, h] = values[h]
        high, low = split(jnp.concatenate(values, 0))
        parts[par, s, 0] = high
        parts[par, s, 1] = low

    def store_strip(par, b, values):
        for h in range(2):
            sdirs[par, b, h] = values[h]
        high, low = split(jnp.concatenate(values, 0))
        sparts[par, b, 0] = high
        sparts[par, b, 1] = low

    if phase != FIRST_HALF:
        for b in (FAR1, OWN) if phase == EARLY else (OWN, NEAR):
            at = slice(b * LANES, (b + 1) * LANES)
            shift = halo[SHIFT : SHIFT + 1, at]
            scale = 1.0 / (shift * shift + OMEGA * OMEGA)
            spre[b, 0:1] = shift * scale
            spre[b, 1:2] = OMEGA * scale
            m = [halo[MASK[face] : MASK[face] + 1, at] for face in range(4)]
            spre[b, 2:3] = jnp.where(odd == 1, m[1], m[0])
            spre[b, 3:4] = jnp.where(odd == 1, m[0], m[1])
            spre[b, 4:5] = m[2]
            spre[b, 5:6] = m[3]
            pair = [halo[r : r + 1, at] for r in (DON0, DON1)]
            sdon[b, 0] = jnp.where(odd == 1, pair[1], pair[0]).astype(jnp.int32) + lane
            sdon[b, 1] = jnp.where(odd == 1, pair[0], pair[1]).astype(jnp.int32) + lane
        par = MIDDLE % 2
        for b in (FAR1, OWN):
            store_strip(par, b, [old_sdirs[b - 1, h] for h in range(2)])
            for h in range(2):
                sres[b, h] = old_sres[b - 1, h]
    if phase == EARLY:
        blank = [jnp.zeros((8, LANES), jnp.float32)] * 2
        store_strip(0, NEAR, blank)
        store_strip(1, NEAR, blank)
        for b, kept in ((FAR1, range(2, 8)), (OWN, range(8))):
            for c in kept:
                s, q, e = BLOCKS[b][0] + c, FIRST[b] + c, 2 * (b - 1) + c // 4
                store(par, s, [patched(old_dirs[par, s, h], ed[e, h], c, nrm) for h in range(2)])
                for h in range(2):
                    res[q, h] = patched(old_res[q, h], er[e, h], c, nrm)
        for c in range(8):
            for h in range(2):
                sol[c, h] = patched(old_sol[c, h], es[c // 4, h], c, nrm)
    if phase == LATE:
        store_strip(1 - par, FAR1, [kept_dirs[0, h] for h in range(2)])
        slot, first = BLOCKS[NEAR][0], FIRST[NEAR]
        for n in range(SENT_DIRS):
            at = 16 * n
            store(par, slot + n, [message[at + 8 * h : at + 8 * h + 8, :] for h in range(2)])
        for n in range(SENT_RES):
            for h in range(2):
                at = 16 * (SENT_DIRS + n) + 8 * h
                res[first + n, h] = message[at : at + 8, :]
        swap = 7 * HALO - (lane - group) + group
        at = 16 * (SENT_DIRS + SENT_RES)
        values = []
        for h in range(2):
            rows = slice(at + 8 * h, at + 8 * h + 8)
            values.append(jnp.take_along_axis(message[rows, 0:LANES], swap, axis=1))
            sres[NEAR, h] = jnp.take_along_axis(message[rows, LANES:], swap, axis=1)
        store_strip(par, NEAR, values)

    def strips(step):
        par = step % 2
        source = dirs_at(step)
        for b in PLANS[phase][step][2]:
            slot, held, first, _ = BLOCKS[b]
            at = slice(b * LANES, (b + 1) * LANES)
            before, after = sdon[b, 0], sdon[b, 1]
            rows, far, mid = [[], [], [], []], [], []
            for h in range(2):
                d = sdirs[par, b, h]
                edge = jnp.zeros((8, LANES), jnp.float32)
                for c in range(held):
                    col = first + c
                    tile = source[slot + c, h, :, pl.ds(pl.multiple_of((1 - nrm) * LANES, LANES), LANES)]
                    tile = pltpu.roll(tile, HALO * col + 1 + 14 * nrm, 1)
                    edge = jnp.where((lane >= HALO * col) & (lane < HALO * (col + 1)), tile, edge)
                west, west2 = pltpu.roll(d, HALO, 1), pltpu.roll(d, 2 * HALO, 1)
                east, east2 = pltpu.roll(d, LANES - HALO, 1), pltpu.roll(d, LANES - 2 * HALO, 1)
                if b > 1:
                    other = sdirs[par, b - 1, h]
                    close = jnp.take_along_axis(other, jnp.bitwise_and(before + 7 * HALO, LANES - 1), axis=1)
                    next2 = jnp.take_along_axis(other, jnp.bitwise_and(before + 6 * HALO, LANES - 1), axis=1)
                    west = jnp.where(lane < HALO, close, west)
                    west2 = jnp.where(lane < 2 * HALO, next2, west2)
                if b < 3:
                    other = sdirs[par, b + 1, h]
                    close = jnp.take_along_axis(other, jnp.bitwise_and(after + HALO, LANES - 1), axis=1)
                    next2 = jnp.take_along_axis(other, jnp.bitwise_and(after + 2 * HALO, LANES - 1), axis=1)
                    east = jnp.where(lane >= 7 * HALO, close, east)
                    east2 = jnp.where(lane >= 6 * HALO, next2, east2)
                south = jnp.where(group == 0, edge, pltpu.roll(d, 1, 1))
                north = jnp.where(group == HALO - 1, edge, pltpu.roll(d, LANES - 1, 1))
                for face, value in enumerate((west, east, south, north)):
                    rows[face].append(spre[b, 2 + face : 3 + face] * value)
                far.append(west2 + east2)
                mid.append(d)
            high, low = split(jnp.concatenate(sum(rows, []), 0))
            out = apply(
                basis, jnp.concatenate([high, low, high], 0), mid, far, halo[SHIFT : SHIFT + 1, at], halo[DAMP : DAMP + 1, at],
                lambda m, at=at: halo[FLOW + m : FLOW + m + 1, at],
            )
            new = [sres[b, h] - out[h] for h in range(2)]
            keep, gain = steps[step]
            turned = precond(spre[b, 0:1], spre[b, 1:2], *new)
            made = [keep * mid[h] + gain * turned[h] for h in range(2)]
            if phase == LATE and b == OWN and step == MIDDLE:
                done = lane < EARLY_LANES
                new = [jnp.where(done, kept_res[h], new[h]) for h in range(2)]
                made = [jnp.where(done, kept_dirs[1, h], made[h]) for h in range(2)]
            for h in range(2):
                sres[b, h] = new[h]
                if phase == EARLY and step == MIDDLE:
                    kept_dirs[b - 1, h] = made[h]
                    if b == OWN:
                        kept_res[h] = new[h]
            store_strip(1 - par, b, made)

    def column(step, b, c):
        slot, _, first, _ = BLOCKS[b]
        s, q = slot + c, FIRST[b] + c
        par = step % 2
        p = parts_at(step)
        turn = 127 - 14 * nrm - HALO * (first + c)
        stack = [[], []]
        for k in range(2):
            tiles = [p[s, k, :, t * LANES : (t + 1) * LANES] for t in range(2)]
            up = [pltpu.roll(x, 1, 1) for x in tiles]
            down = [pltpu.roll(x, LANES - 1, 1) for x in tiles]
            south = [up[0], jnp.where(lane16 == 0, up[0], up[1])]
            north = [jnp.where(lane16 == LANES - 1, down[1], down[0]), down[1]]
            if phase != FIRST_HALF:
                edge = pltpu.roll(sparts[par, b, k], turn, 1)
                south[0] = jnp.where(lane16 == 0, edge, south[0])
                north[1] = jnp.where(lane16 == LANES - 1, edge, north[1])
            for face, value in enumerate(
                (p[s - 1, k], p[s + 1, k], jnp.concatenate(south, 1), jnp.concatenate(north, 1))
            ):
                stack[k].append(masks[q, face] * value)
        return jnp.concatenate(stack[0] + stack[1] + stack[0], 0)

    def finish(step, b, c, rows):
        s, q = BLOCKS[b][0] + c, FIRST[b] + c
        d = dirs_at(step)
        mid = [d[s, h] for h in range(2)]
        far = [d[s - 2, h] + d[s + 2, h] for h in range(2)]
        out = apply(basis, rows, mid, far, coef[q, 0:1], coef[q, 1:2], lambda m: coef[q, 8 + m : 9 + m])
        old = res0 if step == 0 else res
        new = [old[q, h] - out[h] for h in range(2)]
        for h in range(2):
            res[q, h] = new[h]
            if b == OWN:
                sol[c, h] = mid[h] if step == 0 else sol[c, h] + mid[h]
        if step + 1 < ITERS:
            keep, gain = steps[step]
            turned = precond(coef[q, 2:3], coef[q, 3:4], *new)
            store(1 - step % 2, s, [keep * mid[h] + gain * turned[h] for h in range(2)])

    for step, (columns, fills, _) in PLANS[phase].items():
        par = step % 2
        for n in fills:
            ghosts(dirs.at[par], dirs.at[par], parts.at[par], index, n)
        strips(step)
        for b, start, pairs in columns:
            for c in range(start, start + 2 * pairs):
                finish(step, b, c, column(step, b, c))

    if phase == LATE:
        for i in range(8):
            c = place(OWN, i, odd)
            for h in range(2):
                sol_out[5 * h : 5 * h + 5, i, :] = sol[c, h][0:5]
                res_out[5 * h : 5 * h + 5, i, :] = res[FIRST[OWN] + c, h][0:5]


def moved(cells, pairs):
    return lax.ppermute(cells, "blk", [p for p in pairs(lax.axis_size("blk"))])


def far_pairs(by):
    def pairs(count):
        for i in range(count):
            j = i - by if i % 2 == 0 else i + by
            if 0 <= j < count:
                yield j, i

    return pairs


def chip_pairs(count):
    return [(i, i + 1 - 2 * (i % 2)) for i in range(count)]


def local(kernel, outs, scratch, *args, limit=16 << 20, aliases=None):
    vmem = pl.BlockSpec(memory_space=pltpu.VMEM)
    return pl.pallas_call(
        kernel,
        out_shape=outs,
        in_specs=[vmem] * len(args),
        out_specs=jax.tree.map(lambda _: vmem, outs),
        scratch_shapes=scratch,
        input_output_aliases=aliases or {},
        compiler_params=pltpu.CompilerParams(vmem_limit_bytes=limit),
    )(*args)


def inside(x):
    return pltpu.with_memory_space_constraint(x, pltpu.VMEM)


def step(right_side, mean_flow, jac_basis, pattern, shift_diag, dissipation, donors):
    f32, bf16 = jnp.float32, jnp.bfloat16
    vmem = pltpu.VMEM

    whole, part = local(
        pack_kernel,
        (vmem((WHOLE_ROWS, LANES), f32), vmem((PART_ROWS, LANES), f32)),
        [],
        right_side, mean_flow, pattern, shift_diag, dissipation, donors,
        limit=None,
    )
    far1 = moved(whole, far_pairs(1))
    far2 = moved(part, far_pairs(2))
    near = moved(whole, chip_pairs)
    basis = local(
        basis_kernel, vmem((80, 192), bf16), [vmem((80, LANES), f32)], jac_basis.transpose(1, 2, 0, 3)
    )

    cells = [inside(x) for x in (far2, far1, whole, near)]
    strip = local(strip_kernel, vmem((FEATS, 4 * LANES), f32), [], *cells)
    halo = lax.ppermute(strip, "nrm", [(0, 1), (1, 0)])
    coef, masks, res0, dirs0, parts0, index = local(
        prep_kernel,
        (
            vmem((COLUMNS, 16, WIDTH), f32),
            vmem((COLUMNS, 4, 16, WIDTH), bf16),
            vmem((COLUMNS, 2, 8, WIDTH), f32),
            vmem((SLOTS, 2, 8, WIDTH), f32),
            vmem((SLOTS, 2, 16, WIDTH), bf16),
            vmem((6, 2, 8, LANES), jnp.int32),
        ),
        [],
        *cells,
    )

    basis = inside(basis)
    fixed = [inside(x) for x in (coef, masks)]
    index = inside(index)
    state = (
        vmem((2, SLOTS, 2, 8, WIDTH), f32),
        vmem((COLUMNS, 2, 8, WIDTH), f32),
        vmem((8, 2, 8, WIDTH), f32),
    )
    parts = vmem((2, SLOTS, 2, 16, WIDTH), bf16)
    dirs, res, sol = local(
        functools.partial(solve_kernel, FIRST_HALF), state, (parts,),
        *fixed, *[inside(x) for x in (res0, dirs0, parts0)], index, basis,
    )
    dirs, res, halo = inside(dirs), inside(res), inside(halo)
    *edges, message = local(
        edge_kernel,
        (
            vmem((4, 2, 8, LANES), f32),
            vmem((4, 2, 8, LANES), f32),
            vmem((2, 2, 8, LANES), f32),
            vmem((2, 2, 8, LANES), f32),
            vmem((2, 2, 8, LANES), f32),
            vmem((16 * (SENT_DIRS + SENT_RES + 1), WIDTH), f32),
        ),
        (
            vmem((7, FEATS, LANES), f32),
            vmem((7, 8, LANES), f32),
            vmem((7, 2, 8, LANES), jnp.int32),
            vmem((2, 7, 2, 8, LANES), f32),
            vmem((7, 2, 8, LANES), f32),
        ),
        inside(strip), halo, basis, dirs, res,
    )
    message = moved(message, chip_pairs)
    scratch = (
        vmem((2, 4, 2, 8, LANES), f32),
        vmem((4, 2, 8, LANES), f32),
        vmem((2, 4, 2, 16, LANES), bf16),
        vmem((4, 8, LANES), f32),
        vmem((4, 2, 8, LANES), jnp.int32),
    )
    edges = [inside(x) for x in edges]
    kept = local(
        functools.partial(solve_kernel, EARLY),
        (*state, parts, vmem((2, 2, 8, LANES), f32), vmem((2, 8, LANES), f32)),
        scratch,
        *fixed, dirs, res, inside(sol), *edges, index, halo, basis,
    )
    out = jax.ShapeDtypeStruct(right_side.shape, f32)
    return local(
        functools.partial(solve_kernel, LATE), (out, out, *state, parts), scratch,
        *fixed, *[inside(x) for x in kept], *edges[3:], inside(message), index, halo, basis,
        aliases={2: 2, 3: 3, 4: 4, 5: 5},
    )[:2]


def solution(mesh):
    return jax.shard_map(
        step,
        mesh=mesh,
        in_specs=(
            P(None, "blk", "nrm"),
            P(None, "blk", "nrm"),
            P(),
            P(None, "blk", "nrm"),
            P("blk", "nrm"),
            P("blk", "nrm"),
            P("blk", None, "nrm"),
        ),
        out_specs=(P(None, "blk", "nrm"), P(None, "blk", "nrm")),
        check_vma=False,
    )
```

time: 41 us -> 39.2 us (0.956)
  the two profiles are of different devices: /device:TPU:512 before, /device:TPU:513 now
where the time goes in v4:
time: 39.2 us; the launch traced here: 38.9 us
  starting transfers between devices  27.7 us (71%)
  Pallas kernels  7.73 us (20%)
  waiting for transfers between devices  1.9 us (5%)
  local copies, waits for them, and re-layouts  0.89 us (2%)
  between operations  0.74 us (2%)
    ppermute x4, starting transfers between devices, moved(): return lax.ppermute(cells, 'blk', [p for p in pairs(lax.axis_size('blk'))])  24.9 us
    pallas_call x8, Pallas kernels, local(): pl.pallas_call(kernel, out_shape=outs, in_specs=[vmem] * len(args), out_s...  7.73 us
    ppermute x1, starting transfers between devices, step(): halo = lax.ppermute(strip, 'nrm', [(0, 1), (1, 0)])  2.74 us
    ppermute x4, waiting for transfers between devices, moved(): return lax.ppermute(cells, 'blk', [p for p in pairs(lax.axis_size('blk'))])  1.89 us
    unnamed x2, local copies, waits for them, and re-layouts  0.89 us
  transfers between devices with their start and end apart: 5, of which 1 were waited for; matrix products, arithmetic and copies ran while one was open for 0% of the time, Pallas kernels for 9%

profile of v4, /device:TPU:513, one launch (start us, length us, event | category | flops | bytes accessed | tf_op | source)
XLA Modules:
  0.0 38.9 jit_solution(14874067351546390319)
XLA Ops:
  0.6 1.0 %shard_map.86 = (f32[344,128]{1,0:T(8,128)S(1)}, f32[152,128]{1,0:T(8,128)S(1)}) custom-call(f32[10,8,256]{2,1,0:T(8,128)} %rhs.1, f32[5,8,256]{2,1,0:T(8,128)} %flow.1, s32[4,8,256]{2,1,0:T(8,128)} %mask.1, f32[8,256]{1,0:T(8,128)} %shift.1, f32[8,256]{1,0:T(8,128)} %damp.1, s32[1,2,256]{2,1,0:T(2,128)} %donors.1), custom_call_target="tpu_custom_call" | custom-call | tf_op jit(solution)/shard_map/pallas_call | solution.py:607
  1.7 2.6 %collective-permute-start.2 = (f32[344,128]{1,0:T(8,128)S(1)}, f32[344,128]{1,0:T(8,128)S(1)}, u32[]{:S(2)}, u32[]{:S(2)}) collective-permute-start(f32[344,128]{1,0:T(8,128)S(1)} %get-tuple-element.28.own.refs_2_), channel_id=1, source_target_pairs={{0,2},{2,0},{4,6},{6,4},{8,10},{10,8},{12,14},{14,12},{16,18},{18,... | collective-permute-start | bytes 528392 | tf_op jit(solution)/shard_map/ppermute | solution.py:588
  4.2 4.1 %collective-permute-start.1 = (f32[344,128]{1,0:T(8,128)S(1)}, f32[344,128]{1,0:T(8,128)S(1)}, u32[]{:S(2)}, u32[]{:S(2)}) collective-permute-start(f32[344,128]{1,0:T(8,128)S(1)} %get-tuple-element.28.own.refs_2_), channel_id=1, source_target_pairs={{4,2},{2,4},{8,6},{6,8},{12,10},{10,12},{16,14},{14,16},{20,18},{1... | collective-permute-start | bytes 528392 | tf_op jit(solution)/shard_map/ppermute | solution.py:588
  8.4 7.4 %collective-permute-start = (f32[152,128]{1,0:T(8,128)S(1)}, f32[152,128]{1,0:T(8,128)S(1)}, u32[]{:S(2)}, u32[]{:S(2)}) collective-permute-start(f32[152,128]{1,0:T(8,128)S(1)} %get-tuple-element.27), channel_id=1, source_target_pairs={{6,2},{0,4},{10,6},{4,8},{14,10},{8,12},{18,14},{12,16},{22,18},{1... | collective-permute-start | bytes 233480 | tf_op jit(solution)/shard_map/ppermute | solution.py:588
  15.8 1.9 %collective-permute-done.far2.refs_0_ = f32[152,128]{1,0:T(8,128)S(1)} collective-permute-done((f32[152,128]{1,0:T(8,128)S(1)}, f32[152,128]{1,0:T(8,128)S(1)}, u32[]{:S(2)}, u32[]{:S(2)}) %collective-permute-start) | collective-permute-done | bytes 77856 | tf_op jit(solution)/shard_map/ppermute | solution.py:588
  17.7 0.0 collective-permute-done.2.near.refs_3_
  17.7 0.0 collective-permute-done.1.far1.refs_1_
  17.7 0.2 shard_map.90.strip
  17.9 2.7 %collective-permute-start.3 = (f32[24,512]{1,0:T(8,128)S(1)}, f32[24,512]{1,0:T(8,128)S(1)}, u32[]{:S(2)}, u32[]{:S(2)}) collective-permute-start(f32[24,512]{1,0:T(8,128)S(1)} %shard_map.90.strip), channel_id=1, source_target_pairs={{0,1},{1,0},{2,3},{3,2},{4,5},{5,4},{6,7},{7,6},{8,9},{9,8},{10,11... | collective-permute-start | bytes 147464 | tf_op jit(solution)/shard_map/ppermute | solution.py:642
  20.6 0.0 copy-start
  20.6 0.9 %copy-done = f32[4,5,10,10]{3,0,2,1:T(4,128)S(1)} copy-done((f32[4,5,10,10]{3,0,2,1:T(4,128)S(1)}, f32[4,5,10,10]{3,0,2,1:T(4,128)}, u32[]{:S(2)}) %copy-start) | copy-done | bytes 8024
  21.5 0.3 shard_map.88.refs_6_.basis.refs_12_.refs_13_
  21.8 0.4 %shard_map.87 = (f32[26,16,256]{2,1,0:T(8,128)S(1)}, bf16[26,4,16,256]{3,2,1,0:T(8,128)(2,1)S(1)}, f32[26,2,8,256]{3,2,1,0:T(8,128)S(1)}, f32[38,2,8,256]{3,2,1,...) custom-call(f32[152,128]{1,0:T(8,128)S(1)} %collective-permute-done.far2.refs_0_, ...), custom_call_target="tpu_custom_call" | custom-call | tf_op jit(solution)/shard_map/pallas_call | solution.py:607
  22.3 1.6 %shard_map.89 = (f32[2,38,2,8,256]{4,3,2,1,0:T(8,128)S(1)}, f32[26,2,8,256]{3,2,1,0:T(8,128)S(1)}, f32[8,2,8,256]{3,2,1,0:T(8,128)S(1)}) custom-call(f32[26,16,256]{2,1,0:T(8,128)S(1)} %get-tuple-element.29.refs_0_, bf16[26,4,16,256]{3,2,1,0:T(8,128)(2,1)S(1)} %get-tuple-element.30.refs_1_, f32[26,2,8,256]{3,2,1,0:T(8,128)S(1)} %get-tuple-element.31.refs_2_, ...), custom_call_target="tpu_custom_call" | custom-call | tf_op jit(solution)/shard_map/pallas_call | solution.py:607
  23.9 0.0 collective-permute-done.3.halo.refs_11_.refs_12_
  23.9 1.1 %shard_map.91 = (f32[4,2,8,128]{3,2,1,0:T(8,128)S(1)}, f32[4,2,8,128]{3,2,1,0:T(8,128)S(1)}, f32[2,2,8,128]{3,2,1,0:T(8,128)S(1)}, f32[2,2,8,128]{3,2,1,0:T(8,12...) custom-call(f32[24,512]{1,0:T(8,128)S(1)} %shard_map.90.strip, ...), custom_call_target="tpu_custom_call" | custom-call | tf_op jit(solution)/shard_map/pallas_call | solution.py:607
  25.0 10.8 %collective-permute-start.4 = (f32[176,256]{1,0:T(8,128)S(1)}, f32[176,256]{1,0:T(8,128)S(1)}, u32[]{:S(2)}, u32[]{:S(2)}) collective-permute-start(f32[176,256]{1,0:T(8,128)S(1)} %get-tuple-element.49), channel_id=1, source_target_pairs={{0,2},{2,0},{4,6},{6,4},{8,10},{10,8},{12,14},{14,12},{16,18},{18,... | collective-permute-start | bytes 540680 | tf_op jit(solution)/shard_map/ppermute | solution.py:588
  35.8 1.3 %shard_map.92 = (f32[2,38,2,8,256]{4,3,2,1,0:T(8,128)S(1)}, f32[26,2,8,256]{3,2,1,0:T(8,128)S(1)}, f32[8,2,8,256]{3,2,1,0:T(8,128)S(1)}, bf16[2,38,2,16,256]{4,3...) custom-call(f32[26,16,256]{2,1,0:T(8,128)S(1)} %get-tuple-element.29.refs_0_, ...), custom_call_target="tpu_custom_call" | custom-call | tf_op jit(solution)/shard_map/pallas_call | solution.py:607
  37.1 0.0 collective-permute-done.4.refs_10_
  37.1 1.8 %shard_map.93 = (f32[10,8,256]{2,1,0:T(8,128)}, f32[10,8,256]{2,1,0:T(8,128)}, f32[2,38,2,8,256]{4,3,2,1,0:T(8,128)S(1)}, f32[26,2,8,256]{3,2,1,0:T(8,128)S(1)},...) custom-call(f32[26,16,256]{2,1,0:T(8,128)S(1)} %get-tuple-element.29, ...), custom_call_target="tpu_custom_call", output_to_operand_aliasing={{2}: (2, {}), {3}: (3, {}), {4}: (4, {}), {5}: (5, {})} | custom-call | tf_op jit(solution)/shard_map/pallas_call | solution.py:607
Async XLA Ops:
  1.7 16.0 %collective-permute-start.2 = (f32[344,128]{1,0:T(8,128)S(1)}, f32[344,128]{1,0:T(8,128)S(1)}, u32[]{:S(2)}, u32[]{:S(2)}) collective-permute-start(f32[344,128]{1,0:T(8,128)S(1)} %get-tuple-element.28.own.refs_2_), channel_id=1, source_target_pairs={{0,2},{2,0},{4,6},{6,4},{8,10},{10,8},{12,14},{14,12},{16,18},{18,... | collective-permute-start | bytes 528392 | tf_op jit(solution)/shard_map/ppermute | solution.py:588
  4.2 13.4 %collective-permute-start.1 = (f32[344,128]{1,0:T(8,128)S(1)}, f32[344,128]{1,0:T(8,128)S(1)}, u32[]{:S(2)}, u32[]{:S(2)}) collective-permute-start(f32[344,128]{1,0:T(8,128)S(1)} %get-tuple-element.28.own.refs_2_), channel_id=1, source_target_pairs={{4,2},{2,4},{8,6},{6,8},{12,10},{10,12},{16,14},{14,16},{20,18},{1... | collective-permute-start | bytes 528392 | tf_op jit(solution)/shard_map/ppermute | solution.py:588
  8.4 9.3 %collective-permute-start = (f32[152,128]{1,0:T(8,128)S(1)}, f32[152,128]{1,0:T(8,128)S(1)}, u32[]{:S(2)}, u32[]{:S(2)}) collective-permute-start(f32[152,128]{1,0:T(8,128)S(1)} %get-tuple-element.27), channel_id=1, source_target_pairs={{6,2},{0,4},{10,6},{4,8},{14,10},{8,12},{18,14},{12,16},{22,18},{1... | collective-permute-start | bytes 233480 | tf_op jit(solution)/shard_map/ppermute | solution.py:588
  17.9 6.0 %collective-permute-start.3 = (f32[24,512]{1,0:T(8,128)S(1)}, f32[24,512]{1,0:T(8,128)S(1)}, u32[]{:S(2)}, u32[]{:S(2)}) collective-permute-start(f32[24,512]{1,0:T(8,128)S(1)} %shard_map.90.strip), channel_id=1, source_target_pairs={{0,1},{1,0},{2,3},{3,2},{4,5},{5,4},{6,7},{7,6},{8,9},{9,8},{10,11... | collective-permute-start | bytes 147464 | tf_op jit(solution)/shard_map/ppermute | solution.py:642
  20.6 0.9 %copy-start = (f32[4,5,10,10]{3,0,2,1:T(4,128)S(1)}, f32[4,5,10,10]{3,0,2,1:T(4,128)}, u32[]{:S(2)}) copy-start(f32[4,5,10,10]{3,0,2,1:T(4,128)} %param.9) | copy-start | bytes 24004
  25.0 12.1 %collective-permute-start.4 = (f32[176,256]{1,0:T(8,128)S(1)}, f32[176,256]{1,0:T(8,128)S(1)}, u32[]{:S(2)}, u32[]{:S(2)}) collective-permute-start(f32[176,256]{1,0:T(8,128)S(1)} %get-tuple-element.49), channel_id=1, source_target_pairs={{0,2},{2,0},{4,6},{6,4},{8,10},{10,8},{12,14},{14,12},{16,18},{18,... | collective-permute-start | bytes 540680 | tf_op jit(solution)/shard_map/ppermute | solution.py:588

commit v5 on v4

--- a/solution.py
+++ b/solution.py
@@ -155,12 +155,14 @@
     basis[:, 128:192] = low
 
 
-def strip_kernel(*refs):
+def strip_kernel(blocks, *refs):
     nrm, odd = lax.axis_index("nrm"), mirrored()
     strip = refs[-1]
     lane = lanes(FEATS)
     t = 1 - nrm
-    for b, ref in enumerate(refs[:-1]):
+    if len(blocks) == 1:
+        strip[...] = refs[0][...]
+    for b, ref in zip(blocks, refs[-1 - len(blocks) : -1], strict=True):
         first, sent = BLOCKS[b][2:]
         second = PART_B if b == FAR2 else WHOLE_B
         rows = jnp.zeros((FEATS, LANES), jnp.float32)
@@ -550,6 +552,12 @@
                 stack[k].append(masks[q, face] * value)
         return jnp.concatenate(stack[0] + stack[1] + stack[0], 0)
 
+    def write(c, total, left):
+        i = place(OWN, c, odd)
+        for h in range(2):
+            sol_out[5 * h : 5 * h + 5, i, :] = total[h][0:5]
+            res_out[5 * h : 5 * h + 5, i, :] = left[h][0:5]
+
     def finish(step, b, c, rows):
         s, q = BLOCKS[b][0] + c, FIRST[b] + c
         d = dirs_at(step)
@@ -562,11 +570,16 @@
             res[q, h] = new[h]
             if b == OWN:
                 sol[c, h] = mid[h] if step == 0 else sol[c, h] + mid[h]
+        if phase == LATE and step + 1 == ITERS:
+            write(c, [sol[c, h] for h in range(2)], new)
         if step + 1 < ITERS:
             keep, gain = steps[step]
             turned = precond(coef[q, 2:3], coef[q, 3:4], *new)
             store(1 - step % 2, s, [keep * mid[h] + gain * turned[h] for h in range(2)])
 
+    if phase == LATE:
+        for c in range(2):
+            write(c, [sol[c, h] for h in range(2)], [res[FIRST[OWN] + c, h] for h in range(2)])
     for step, (columns, fills, _) in PLANS[phase].items():
         par = step % 2
         for n in fills:
@@ -575,13 +588,6 @@
         for b, start, pairs in columns:
             for c in range(start, start + 2 * pairs):
                 finish(step, b, c, column(step, b, c))
-
-    if phase == LATE:
-        for i in range(8):
-            c = place(OWN, i, odd)
-            for h in range(2):
-                sol_out[5 * h : 5 * h + 5, i, :] = sol[c, h][0:5]
-                res_out[5 * h : 5 * h + 5, i, :] = res[FIRST[OWN] + c, h][0:5]
 
 
 def moved(cells, pairs):
@@ -638,7 +644,13 @@
     )
 
     cells = [inside(x) for x in (far2, far1, whole, near)]
-    strip = local(strip_kernel, vmem((FEATS, 4 * LANES), f32), [], *cells)
+    strip = local(
+        functools.partial(strip_kernel, (FAR2, OWN, NEAR)), vmem((FEATS, 4 * LANES), f32), [],
+        *(cells[b] for b in (FAR2, OWN, NEAR)),
+    )
+    strip = local(
+        functools.partial(strip_kernel, (FAR1,)), vmem((FEATS, 4 * LANES), f32), [], inside(strip), cells[FAR1]
+    )
     halo = lax.ppermute(strip, "nrm", [(0, 1), (1, 0)])
     coef, masks, res0, dirs0, parts0, index = local(
         prep_kernel,

time: 39.2 us -> 39.3 us (level)
    pallas_call x8 -> x9, Pallas kernels: 7.73 us -> 7.78 us  [local(): pl.pallas_call(kernel, out_shape=outs, in_specs=[vmem] * len(args), out_s...]
  transfers between devices with their start and end apart: 5 -> 5, of which waited for: 1 -> 1; matrix products, arithmetic and copies ran while one was open for 0% -> 0% of each run, Pallas kernels for 9% -> 10%
where the time goes in v5:
time: 39.3 us; the launch traced here: 39 us
  starting transfers between devices  27.7 us (70%)
  Pallas kernels  7.78 us (20%)
  waiting for transfers between devices  1.9 us (5%)
  local copies, waits for them, and re-layouts  0.89 us (2%)
  between operations  0.74 us (2%)
    ppermute x4, starting transfers between devices, moved(): return lax.ppermute(cells, 'blk', [p for p in pairs(lax.axis_size('blk'))])  24.9 us
    pallas_call x9, Pallas kernels, local(): pl.pallas_call(kernel, out_shape=outs, in_specs=[vmem] * len(args), out_s...  7.78 us
    ppermute x1, starting transfers between devices, step(): halo = lax.ppermute(strip, 'nrm', [(0, 1), (1, 0)])  2.74 us
    ppermute x4, waiting for transfers between devices, moved(): return lax.ppermute(cells, 'blk', [p for p in pairs(lax.axis_size('blk'))])  1.89 us
    unnamed x2, local copies, waits for them, and re-layouts  0.89 us
  transfers between devices with their start and end apart: 5, of which 1 were waited for; matrix products, arithmetic and copies ran while one was open for 0% of the time, Pallas kernels for 10%

profile of v5, /device:TPU:513, one launch (start us, length us, event | category | flops | bytes accessed | tf_op | source)
XLA Modules:
  0.0 39.0 jit_solution(17343787854223117591)
XLA Ops:
  0.6 1.0 %shard_map.86 = (f32[344,128]{1,0:T(8,128)S(1)}, f32[152,128]{1,0:T(8,128)S(1)}) custom-call(f32[10,8,256]{2,1,0:T(8,128)} %rhs.1, f32[5,8,256]{2,1,0:T(8,128)} %flow.1, s32[4,8,256]{2,1,0:T(8,128)} %mask.1, f32[8,256]{1,0:T(8,128)} %shift.1, f32[8,256]{1,0:T(8,128)} %damp.1, s32[1,2,256]{2,1,0:T(2,128)} %donors.1), custom_call_target="tpu_custom_call" | custom-call | tf_op jit(solution)/shard_map/pallas_call | solution.py:613
  1.7 2.6 %collective-permute-start.2 = (f32[344,128]{1,0:T(8,128)S(1)}, f32[344,128]{1,0:T(8,128)S(1)}, u32[]{:S(2)}, u32[]{:S(2)}) collective-permute-start(f32[344,128]{1,0:T(8,128)S(1)} %get-tuple-element.28.own.refs_1_), channel_id=1, source_target_pairs={{0,2},{2,0},{4,6},{6,4},{8,10},{10,8},{12,14},{14,12},{16,18},{18,... | collective-permute-start | bytes 528392 | tf_op jit(solution)/shard_map/ppermute | solution.py:594
  4.2 4.1 %collective-permute-start.1 = (f32[344,128]{1,0:T(8,128)S(1)}, f32[344,128]{1,0:T(8,128)S(1)}, u32[]{:S(2)}, u32[]{:S(2)}) collective-permute-start(f32[344,128]{1,0:T(8,128)S(1)} %get-tuple-element.28.own.refs_1_), channel_id=1, source_target_pairs={{4,2},{2,4},{8,6},{6,8},{12,10},{10,12},{16,14},{14,16},{20,18},{1... | collective-permute-start | bytes 528392 | tf_op jit(solution)/shard_map/ppermute | solution.py:594
  8.4 7.4 %collective-permute-start = (f32[152,128]{1,0:T(8,128)S(1)}, f32[152,128]{1,0:T(8,128)S(1)}, u32[]{:S(2)}, u32[]{:S(2)}) collective-permute-start(f32[152,128]{1,0:T(8,128)S(1)} %get-tuple-element.27), channel_id=1, source_target_pairs={{6,2},{0,4},{10,6},{4,8},{14,10},{8,12},{18,14},{12,16},{22,18},{1... | collective-permute-start | bytes 233480 | tf_op jit(solution)/shard_map/ppermute | solution.py:594
  15.8 1.9 %collective-permute-done.far2.refs_0_ = f32[152,128]{1,0:T(8,128)S(1)} collective-permute-done((f32[152,128]{1,0:T(8,128)S(1)}, f32[152,128]{1,0:T(8,128)S(1)}, u32[]{:S(2)}, u32[]{:S(2)}) %collective-permute-start) | collective-permute-done | bytes 77856 | tf_op jit(solution)/shard_map/ppermute | solution.py:594
  17.7 0.0 collective-permute-done.2.near.refs_2_
  17.7 0.2 shard_map.90.refs_0_
  17.8 0.0 collective-permute-done.1.far1.refs_1_
  17.8 0.1 shard_map.91.strip
  18.0 2.7 %collective-permute-start.3 = (f32[24,512]{1,0:T(8,128)S(1)}, f32[24,512]{1,0:T(8,128)S(1)}, u32[]{:S(2)}, u32[]{:S(2)}) collective-permute-start(f32[24,512]{1,0:T(8,128)S(1)} %shard_map.91.strip), channel_id=1, source_target_pairs={{0,1},{1,0},{2,3},{3,2},{4,5},{5,4},{6,7},{7,6},{8,9},{9,8},{10,11... | collective-permute-start | bytes 147464 | tf_op jit(solution)/shard_map/ppermute | solution.py:654
  20.7 0.0 copy-start
  20.7 0.9 %copy-done = f32[4,5,10,10]{3,0,2,1:T(4,128)S(1)} copy-done((f32[4,5,10,10]{3,0,2,1:T(4,128)S(1)}, f32[4,5,10,10]{3,0,2,1:T(4,128)}, u32[]{:S(2)}) %copy-start) | copy-done | bytes 8024
  21.6 0.3 shard_map.88.refs_6_.basis.refs_12_.refs_13_
  21.9 0.4 %shard_map.87 = (f32[26,16,256]{2,1,0:T(8,128)S(1)}, bf16[26,4,16,256]{3,2,1,0:T(8,128)(2,1)S(1)}, f32[26,2,8,256]{3,2,1,0:T(8,128)S(1)}, f32[38,2,8,256]{3,2,1,...) custom-call(f32[152,128]{1,0:T(8,128)S(1)} %collective-permute-done.far2.refs_0_, ...), custom_call_target="tpu_custom_call" | custom-call | tf_op jit(solution)/shard_map/pallas_call | solution.py:613
  22.4 1.6 %shard_map.89 = (f32[2,38,2,8,256]{4,3,2,1,0:T(8,128)S(1)}, f32[26,2,8,256]{3,2,1,0:T(8,128)S(1)}, f32[8,2,8,256]{3,2,1,0:T(8,128)S(1)}) custom-call(f32[26,16,256]{2,1,0:T(8,128)S(1)} %get-tuple-element.29.refs_0_, bf16[26,4,16,256]{3,2,1,0:T(8,128)(2,1)S(1)} %get-tuple-element.30.refs_1_, f32[26,2,8,256]{3,2,1,0:T(8,128)S(1)} %get-tuple-element.31.refs_2_, ...), custom_call_target="tpu_custom_call" | custom-call | tf_op jit(solution)/shard_map/pallas_call | solution.py:613
  23.9 0.0 collective-permute-done.3.halo.refs_11_.refs_12_
  23.9 1.1 %shard_map.92 = (f32[4,2,8,128]{3,2,1,0:T(8,128)S(1)}, f32[4,2,8,128]{3,2,1,0:T(8,128)S(1)}, f32[2,2,8,128]{3,2,1,0:T(8,128)S(1)}, f32[2,2,8,128]{3,2,1,0:T(8,12...) custom-call(f32[24,512]{1,0:T(8,128)S(1)} %shard_map.91.strip, ...), custom_call_target="tpu_custom_call" | custom-call | tf_op jit(solution)/shard_map/pallas_call | solution.py:613
  25.0 10.8 %collective-permute-start.4 = (f32[176,256]{1,0:T(8,128)S(1)}, f32[176,256]{1,0:T(8,128)S(1)}, u32[]{:S(2)}, u32[]{:S(2)}) collective-permute-start(f32[176,256]{1,0:T(8,128)S(1)} %get-tuple-element.49), channel_id=1, source_target_pairs={{0,2},{2,0},{4,6},{6,4},{8,10},{10,8},{12,14},{14,12},{16,18},{18,... | collective-permute-start | bytes 540680 | tf_op jit(solution)/shard_map/ppermute | solution.py:594
  35.9 1.3 %shard_map.93 = (f32[2,38,2,8,256]{4,3,2,1,0:T(8,128)S(1)}, f32[26,2,8,256]{3,2,1,0:T(8,128)S(1)}, f32[8,2,8,256]{3,2,1,0:T(8,128)S(1)}, bf16[2,38,2,16,256]{4,3...) custom-call(f32[26,16,256]{2,1,0:T(8,128)S(1)} %get-tuple-element.29.refs_0_, ...), custom_call_target="tpu_custom_call" | custom-call | tf_op jit(solution)/shard_map/pallas_call | solution.py:613
  37.2 0.0 collective-permute-done.4.refs_10_
  37.2 1.8 %shard_map.94 = (f32[10,8,256]{2,1,0:T(8,128)}, f32[10,8,256]{2,1,0:T(8,128)}, f32[2,38,2,8,256]{4,3,2,1,0:T(8,128)S(1)}, f32[26,2,8,256]{3,2,1,0:T(8,128)S(1)},...) custom-call(f32[26,16,256]{2,1,0:T(8,128)S(1)} %get-tuple-element.29, ...), custom_call_target="tpu_custom_call", output_to_operand_aliasing={{2}: (2, {}), {3}: (3, {}), {4}: (4, {}), {5}: (5, {})} | custom-call | tf_op jit(solution)/shard_map/pallas_call | solution.py:613
Async XLA Ops:
  1.7 16.0 %collective-permute-start.2 = (f32[344,128]{1,0:T(8,128)S(1)}, f32[344,128]{1,0:T(8,128)S(1)}, u32[]{:S(2)}, u32[]{:S(2)}) collective-permute-start(f32[344,128]{1,0:T(8,128)S(1)} %get-tuple-element.28.own.refs_1_), channel_id=1, source_target_pairs={{0,2},{2,0},{4,6},{6,4},{8,10},{10,8},{12,14},{14,12},{16,18},{18,... | collective-permute-start | bytes 528392 | tf_op jit(solution)/shard_map/ppermute | solution.py:594
  4.2 13.6 %collective-permute-start.1 = (f32[344,128]{1,0:T(8,128)S(1)}, f32[344,128]{1,0:T(8,128)S(1)}, u32[]{:S(2)}, u32[]{:S(2)}) collective-permute-start(f32[344,128]{1,0:T(8,128)S(1)} %get-tuple-element.28.own.refs_1_), channel_id=1, source_target_pairs={{4,2},{2,4},{8,6},{6,8},{12,10},{10,12},{16,14},{14,16},{20,18},{1... | collective-permute-start | bytes 528392 | tf_op jit(solution)/shard_map/ppermute | solution.py:594
  8.4 9.3 %collective-permute-start = (f32[152,128]{1,0:T(8,128)S(1)}, f32[152,128]{1,0:T(8,128)S(1)}, u32[]{:S(2)}, u32[]{:S(2)}) collective-permute-start(f32[152,128]{1,0:T(8,128)S(1)} %get-tuple-element.27), channel_id=1, source_target_pairs={{6,2},{0,4},{10,6},{4,8},{14,10},{8,12},{18,14},{12,16},{22,18},{1... | collective-permute-start | bytes 233480 | tf_op jit(solution)/shard_map/ppermute | solution.py:594
  18.0 6.0 %collective-permute-start.3 = (f32[24,512]{1,0:T(8,128)S(1)}, f32[24,512]{1,0:T(8,128)S(1)}, u32[]{:S(2)}, u32[]{:S(2)}) collective-permute-start(f32[24,512]{1,0:T(8,128)S(1)} %shard_map.91.strip), channel_id=1, source_target_pairs={{0,1},{1,0},{2,3},{3,2},{4,5},{5,4},{6,7},{7,6},{8,9},{9,8},{10,11... | collective-permute-start | bytes 147464 | tf_op jit(solution)/shard_map/ppermute | solution.py:654
  20.7 0.9 %copy-start = (f32[4,5,10,10]{3,0,2,1:T(4,128)S(1)}, f32[4,5,10,10]{3,0,2,1:T(4,128)}, u32[]{:S(2)}) copy-start(f32[4,5,10,10]{3,0,2,1:T(4,128)} %param.9) | copy-start | bytes 24004
  25.0 12.1 %collective-permute-start.4 = (f32[176,256]{1,0:T(8,128)S(1)}, f32[176,256]{1,0:T(8,128)S(1)}, u32[]{:S(2)}, u32[]{:S(2)}) collective-permute-start(f32[176,256]{1,0:T(8,128)S(1)} %get-tuple-element.49), channel_id=1, source_target_pairs={{0,2},{2,0},{4,6},{6,4},{8,10},{10,8},{12,14},{14,12},{16,18},{18,... | collective-permute-start | bytes 540680 | tf_op jit(solution)/shard_map/ppermute | solution.py:594

commit v6 on v5

--- a/solution.py
+++ b/solution.py
@@ -388,8 +388,8 @@
         (coef, masks, res0, dirs0, parts0, index, basis) = refs[:7]
         (dirs, res, sol, parts) = refs[7:]
     elif phase == EARLY:
-        (coef, masks, old_dirs, old_res, old_sol, ed, er, es, old_sdirs, old_sres, index, halo, basis) = refs[:13]
-        (dirs, res, sol, parts, kept_dirs, kept_res, sdirs, sres, sparts, spre, sdon) = refs[13:]
+        (coef, masks, _, _, _, _, ed, er, es, old_sdirs, old_sres, index, halo, basis) = refs[:14]
+        (dirs, res, sol, parts, kept_dirs, kept_res, sdirs, sres, sparts, spre, sdon) = refs[14:]
     else:
         (coef, masks, _, _, _, _, kept_dirs, kept_res, old_sdirs, old_sres, message, index, halo, basis) = refs[:14]
         (sol_out, res_out, dirs, res, sol, parts, sdirs, sres, sparts, spre, sdon) = refs[14:]
@@ -444,15 +444,24 @@
         blank = [jnp.zeros((8, LANES), jnp.float32)] * 2
         store_strip(0, NEAR, blank)
         store_strip(1, NEAR, blank)
+        at = pl.ds(pl.multiple_of((1 - nrm) * LANES, LANES), LANES)
+        close = jnp.where(nrm == 0, LANES - 1 - lane, lane) < FIX
+
+        def mend(ref, tile, c):
+            value = jnp.where(close, pltpu.roll(tile, 7 * HALO - 2 * HALO * (c % 4), 1), ref[:, at])
+            ref[:, at] = value
+            return value
+
         for b, kept in ((FAR1, range(2, 8)), (OWN, range(8))):
             for c in kept:
                 s, q, e = BLOCKS[b][0] + c, FIRST[b] + c, 2 * (b - 1) + c // 4
-                store(par, s, [patched(old_dirs[par, s, h], ed[e, h], c, nrm) for h in range(2)])
+                high, low = split(jnp.concatenate([mend(dirs.at[par, s, h], ed[e, h], c) for h in range(2)], 0))
+                parts[par, s, 0, :, at] = high
+                parts[par, s, 1, :, at] = low
                 for h in range(2):
-                    res[q, h] = patched(old_res[q, h], er[e, h], c, nrm)
-        for c in range(8):
-            for h in range(2):
-                sol[c, h] = patched(old_sol[c, h], es[c // 4, h], c, nrm)
+                    mend(res.at[q, h], er[e, h], c)
+                    if b == OWN:
+                        mend(sol.at[c, h], es[c // 4, h], c)
     if phase == LATE:
         store_strip(1 - par, FAR1, [kept_dirs[0, h] for h in range(2)])
         slot, first = BLOCKS[NEAR][0], FIRST[NEAR]
@@ -675,8 +684,8 @@
         vmem((8, 2, 8, WIDTH), f32),
     )
     parts = vmem((2, SLOTS, 2, 16, WIDTH), bf16)
-    dirs, res, sol = local(
-        functools.partial(solve_kernel, FIRST_HALF), state, (parts,),
+    dirs, res, sol, pieces = local(
+        functools.partial(solve_kernel, FIRST_HALF), (*state, parts), (),
         *fixed, *[inside(x) for x in (res0, dirs0, parts0)], index, basis,
     )
     dirs, res, halo = inside(dirs), inside(res), inside(halo)
@@ -712,7 +721,8 @@
         functools.partial(solve_kernel, EARLY),
         (*state, parts, vmem((2, 2, 8, LANES), f32), vmem((2, 8, LANES), f32)),
         scratch,
-        *fixed, dirs, res, inside(sol), *edges, index, halo, basis,
+        *fixed, dirs, res, inside(sol), inside(pieces), *edges, index, halo, basis,
+        aliases={2: 0, 3: 1, 4: 2, 5: 3},
     )
     out = jax.ShapeDtypeStruct(right_side.shape, f32)
     return local(

time: 39.3 us -> 39.3 us (level)
  no operation moved by 1% of the time
where the time goes in v6:
time: 39.3 us; the launch traced here: 39 us
  starting transfers between devices  27.5 us (70%)
  Pallas kernels  7.97 us (20%)
  waiting for transfers between devices  1.9 us (5%)
  local copies, waits for them, and re-layouts  0.89 us (2%)
  between operations  0.74 us (2%)
    ppermute x4, starting transfers between devices, moved(): return lax.ppermute(cells, 'blk', [p for p in pairs(lax.axis_size('blk'))])  24.8 us
    pallas_call x9, Pallas kernels, local(): pl.pallas_call(kernel, out_shape=outs, in_specs=[vmem] * len(args), out_s...  7.97 us
    ppermute x1, starting transfers between devices, step(): halo = lax.ppermute(strip, 'nrm', [(0, 1), (1, 0)])  2.74 us
    ppermute x4, waiting for transfers between devices, moved(): return lax.ppermute(cells, 'blk', [p for p in pairs(lax.axis_size('blk'))])  1.89 us
    unnamed x2, local copies, waits for them, and re-layouts  0.89 us
  transfers between devices with their start and end apart: 5, of which 1 were waited for; matrix products, arithmetic and copies ran while one was open for 0% of the time, Pallas kernels for 10%

profile of v6, /device:TPU:513, one launch (start us, length us, event | category | flops | bytes accessed | tf_op | source)
XLA Modules:
  0.0 39.0 jit_solution(10646763732605036782)
XLA Ops:
  0.6 1.0 %shard_map.86 = (f32[344,128]{1,0:T(8,128)S(1)}, f32[152,128]{1,0:T(8,128)S(1)}) custom-call(f32[10,8,256]{2,1,0:T(8,128)} %rhs.1, f32[5,8,256]{2,1,0:T(8,128)} %flow.1, s32[4,8,256]{2,1,0:T(8,128)} %mask.1, f32[8,256]{1,0:T(8,128)} %shift.1, f32[8,256]{1,0:T(8,128)} %damp.1, s32[1,2,256]{2,1,0:T(2,128)} %donors.1), custom_call_target="tpu_custom_call" | custom-call | tf_op jit(solution)/shard_map/pallas_call | solution.py:622
  1.7 2.6 %collective-permute-start.2 = (f32[344,128]{1,0:T(8,128)S(1)}, f32[344,128]{1,0:T(8,128)S(1)}, u32[]{:S(2)}, u32[]{:S(2)}) collective-permute-start(f32[344,128]{1,0:T(8,128)S(1)} %get-tuple-element.29.own.refs_1_), channel_id=1, source_target_pairs={{0,2},{2,0},{4,6},{6,4},{8,10},{10,8},{12,14},{14,12},{16,18},{18,... | collective-permute-start | bytes 528392 | tf_op jit(solution)/shard_map/ppermute | solution.py:603
  4.2 4.1 %collective-permute-start.1 = (f32[344,128]{1,0:T(8,128)S(1)}, f32[344,128]{1,0:T(8,128)S(1)}, u32[]{:S(2)}, u32[]{:S(2)}) collective-permute-start(f32[344,128]{1,0:T(8,128)S(1)} %get-tuple-element.29.own.refs_1_), channel_id=1, source_target_pairs={{4,2},{2,4},{8,6},{6,8},{12,10},{10,12},{16,14},{14,16},{20,18},{1... | collective-permute-start | bytes 528392 | tf_op jit(solution)/shard_map/ppermute | solution.py:603
  8.4 7.4 %collective-permute-start = (f32[152,128]{1,0:T(8,128)S(1)}, f32[152,128]{1,0:T(8,128)S(1)}, u32[]{:S(2)}, u32[]{:S(2)}) collective-permute-start(f32[152,128]{1,0:T(8,128)S(1)} %get-tuple-element.28), channel_id=1, source_target_pairs={{6,2},{0,4},{10,6},{4,8},{14,10},{8,12},{18,14},{12,16},{22,18},{1... | collective-permute-start | bytes 233480 | tf_op jit(solution)/shard_map/ppermute | solution.py:603
  15.8 1.9 %collective-permute-done.far2.refs_0_ = f32[152,128]{1,0:T(8,128)S(1)} collective-permute-done((f32[152,128]{1,0:T(8,128)S(1)}, f32[152,128]{1,0:T(8,128)S(1)}, u32[]{:S(2)}, u32[]{:S(2)}) %collective-permute-start) | collective-permute-done | bytes 77856 | tf_op jit(solution)/shard_map/ppermute | solution.py:603
  17.7 0.0 collective-permute-done.2.near.refs_2_
  17.7 0.2 shard_map.90.refs_0_
  17.8 0.0 collective-permute-done.1.far1.refs_1_
  17.8 0.1 shard_map.91.strip
  18.0 2.7 %collective-permute-start.3 = (f32[24,512]{1,0:T(8,128)S(1)}, f32[24,512]{1,0:T(8,128)S(1)}, u32[]{:S(2)}, u32[]{:S(2)}) collective-permute-start(f32[24,512]{1,0:T(8,128)S(1)} %shard_map.91.strip), channel_id=1, source_target_pairs={{0,1},{1,0},{2,3},{3,2},{4,5},{5,4},{6,7},{7,6},{8,9},{9,8},{10,11... | collective-permute-start | bytes 147464 | tf_op jit(solution)/shard_map/ppermute | solution.py:663
  20.7 0.0 copy-start
  20.7 0.9 %copy-done = f32[4,5,10,10]{3,0,2,1:T(4,128)S(1)} copy-done((f32[4,5,10,10]{3,0,2,1:T(4,128)S(1)}, f32[4,5,10,10]{3,0,2,1:T(4,128)}, u32[]{:S(2)}) %copy-start) | copy-done | bytes 8024
  21.6 0.3 shard_map.88.refs_6_.basis.refs_13_
  21.9 0.4 %shard_map.87 = (f32[26,16,256]{2,1,0:T(8,128)S(1)}, bf16[26,4,16,256]{3,2,1,0:T(8,128)(2,1)S(1)}, f32[26,2,8,256]{3,2,1,0:T(8,128)S(1)}, f32[38,2,8,256]{3,2,1,...) custom-call(f32[152,128]{1,0:T(8,128)S(1)} %collective-permute-done.far2.refs_0_, ...), custom_call_target="tpu_custom_call" | custom-call | tf_op jit(solution)/shard_map/pallas_call | solution.py:622
  22.4 1.8 %shard_map.89 = (f32[2,38,2,8,256]{4,3,2,1,0:T(8,128)S(1)}, f32[26,2,8,256]{3,2,1,0:T(8,128)S(1)}, f32[8,2,8,256]{3,2,1,0:T(8,128)S(1)}, bf16[2,38,2,16,256]{4,3,2,1,0:T(8,128)(2,1)S(1)}) custom-call(f32[26,16,256]{2,1,0:T(8,128)S(1)} %get-tuple-element.30.refs_0_, bf16[26,4,16,256]{3,2,1,0:T(8,128)(2,1)S(1)} %get-tuple-element.31.refs_1_, ...), custom_call_target="tpu_custom_call" | custom-call | tf_op jit(solution)/shard_map/pallas_call | solution.py:622
  24.1 0.0 collective-permute-done.3.halo.refs_12_
  24.2 1.1 %shard_map.92 = (f32[4,2,8,128]{3,2,1,0:T(8,128)S(1)}, f32[4,2,8,128]{3,2,1,0:T(8,128)S(1)}, f32[2,2,8,128]{3,2,1,0:T(8,128)S(1)}, f32[2,2,8,128]{3,2,1,0:T(8,12...) custom-call(f32[24,512]{1,0:T(8,128)S(1)} %shard_map.91.strip, ...), custom_call_target="tpu_custom_call" | custom-call | tf_op jit(solution)/shard_map/pallas_call | solution.py:622
  25.2 10.7 %collective-permute-start.4 = (f32[176,256]{1,0:T(8,128)S(1)}, f32[176,256]{1,0:T(8,128)S(1)}, u32[]{:S(2)}, u32[]{:S(2)}) collective-permute-start(f32[176,256]{1,0:T(8,128)S(1)} %get-tuple-element.51), channel_id=1, source_target_pairs={{0,2},{2,0},{4,6},{6,4},{8,10},{10,8},{12,14},{14,12},{16,18},{18,... | collective-permute-start | bytes 540680 | tf_op jit(solution)/shard_map/ppermute | solution.py:603
  35.9 1.3 %shard_map.93 = (f32[2,38,2,8,256]{4,3,2,1,0:T(8,128)S(1)}, f32[26,2,8,256]{3,2,1,0:T(8,128)S(1)}, f32[8,2,8,256]{3,2,1,0:T(8,128)S(1)}, bf16[2,38,2,16,256]{4,3...) custom-call(f32[26,16,256]{2,1,0:T(8,128)S(1)} %get-tuple-element.30, ...), custom_call_target="tpu_custom_call", output_to_operand_aliasing={{0}: (2, {}), {1}: (3, {}), {2}: (4, {}), {3}: (5, {})} | custom-call | tf_op jit(solution)/shard_map/pallas_call | solution.py:622
  37.2 0.0 collective-permute-done.4.refs_10_
  37.2 1.8 %shard_map.94 = (f32[10,8,256]{2,1,0:T(8,128)}, f32[10,8,256]{2,1,0:T(8,128)}, f32[2,38,2,8,256]{4,3,2,1,0:T(8,128)S(1)}, f32[26,2,8,256]{3,2,1,0:T(8,128)S(1)},...) custom-call(f32[26,16,256]{2,1,0:T(8,128)S(1)} %get-tuple-element.30, ...), custom_call_target="tpu_custom_call", output_to_operand_aliasing={{2}: (2, {}), {3}: (3, {}), {4}: (4, {}), {5}: (5, {})} | custom-call | tf_op jit(solution)/shard_map/pallas_call | solution.py:622
Async XLA Ops:
  1.7 16.0 %collective-permute-start.2 = (f32[344,128]{1,0:T(8,128)S(1)}, f32[344,128]{1,0:T(8,128)S(1)}, u32[]{:S(2)}, u32[]{:S(2)}) collective-permute-start(f32[344,128]{1,0:T(8,128)S(1)} %get-tuple-element.29.own.refs_1_), channel_id=1, source_target_pairs={{0,2},{2,0},{4,6},{6,4},{8,10},{10,8},{12,14},{14,12},{16,18},{18,... | collective-permute-start | bytes 528392 | tf_op jit(solution)/shard_map/ppermute | solution.py:603
  4.2 13.6 %collective-permute-start.1 = (f32[344,128]{1,0:T(8,128)S(1)}, f32[344,128]{1,0:T(8,128)S(1)}, u32[]{:S(2)}, u32[]{:S(2)}) collective-permute-start(f32[344,128]{1,0:T(8,128)S(1)} %get-tuple-element.29.own.refs_1_), channel_id=1, source_target_pairs={{4,2},{2,4},{8,6},{6,8},{12,10},{10,12},{16,14},{14,16},{20,18},{1... | collective-permute-start | bytes 528392 | tf_op jit(solution)/shard_map/ppermute | solution.py:603
  8.4 9.3 %collective-permute-start = (f32[152,128]{1,0:T(8,128)S(1)}, f32[152,128]{1,0:T(8,128)S(1)}, u32[]{:S(2)}, u32[]{:S(2)}) collective-permute-start(f32[152,128]{1,0:T(8,128)S(1)} %get-tuple-element.28), channel_id=1, source_target_pairs={{6,2},{0,4},{10,6},{4,8},{14,10},{8,12},{18,14},{12,16},{22,18},{1... | collective-permute-start | bytes 233480 | tf_op jit(solution)/shard_map/ppermute | solution.py:603
  18.0 6.2 %collective-permute-start.3 = (f32[24,512]{1,0:T(8,128)S(1)}, f32[24,512]{1,0:T(8,128)S(1)}, u32[]{:S(2)}, u32[]{:S(2)}) collective-permute-start(f32[24,512]{1,0:T(8,128)S(1)} %shard_map.91.strip), channel_id=1, source_target_pairs={{0,1},{1,0},{2,3},{3,2},{4,5},{5,4},{6,7},{7,6},{8,9},{9,8},{10,11... | collective-permute-start | bytes 147464 | tf_op jit(solution)/shard_map/ppermute | solution.py:663
  20.7 0.9 %copy-start = (f32[4,5,10,10]{3,0,2,1:T(4,128)S(1)}, f32[4,5,10,10]{3,0,2,1:T(4,128)}, u32[]{:S(2)}) copy-start(f32[4,5,10,10]{3,0,2,1:T(4,128)} %param.9) | copy-start | bytes 24004
  25.2 12.0 %collective-permute-start.4 = (f32[176,256]{1,0:T(8,128)S(1)}, f32[176,256]{1,0:T(8,128)S(1)}, u32[]{:S(2)}, u32[]{:S(2)}) collective-permute-start(f32[176,256]{1,0:T(8,128)S(1)} %get-tuple-element.51), channel_id=1, source_target_pairs={{0,2},{2,0},{4,6},{6,4},{8,10},{10,8},{12,14},{14,12},{16,18},{18,... | collective-permute-start | bytes 540680 | tf_op jit(solution)/shard_map/ppermute | solution.py:603
